TPU v7x, 128 devices: a whole 4x4x4 slice. The times are simulated.
128 devices in a mesh: depth: 8 (over x, y_lo), chan: 16 (over z, y_hi, core).
Axes of the slice: x: 4, y: 4 (y_hi: 2, y_lo: 2; y = y_hi * 2 + y_lo), z: 4, core: 2. Of those that a mesh axis runs over, the one named last changes fastest.
Arguments:
- volume: float32 [512, 32, 1024], P('chan', 'depth'), may hold values from -6 to 6
- conv_weight: float32 [1, 3, 16, 32, 864], P(None, None, 'chan'), may hold values from -0.21875 to 0.21875
- norm_gain: float32 [1, 512], replicated, may hold values from 0.1 to 1.9
- mlp_in: float32 [1, 1024, 512], replicated, may hold values from -0.25 to 0.25
- mlp_out: float32 [1, 512, 1024], replicated, may hold values from -0.1875 to 0.1875
Outputs:
- features: float32 [512, 32, 1024], P('chan', 'depth')
All inputs are finite; a program needn't handle non-finite values.
Results may differ from a plain program's by a relative error of at most 0.0001.
Values sent between devices are 32-bit elements; how exact they have to be, the bound alone decides.
No kernel may reach another device: no remote copies, remote signals or barrier semaphores. Data moves between devices by JAX's collectives and lax.ppermute only.
A program may use at most 64 MiB of HBM per device.

v0:
```python
import functools

import jax
import jax.numpy as jnp
from jax import lax
from jax.experimental import pallas as pl
from jax.experimental.pallas import tpu as pltpu
from jax.sharding import PartitionSpec as P

W = 32
F32 = jnp.float32
BF16 = jnp.bfloat16
VMEM = pl.BlockSpec(memory_space=pltpu.VMEM)


def call(body, outs, flops, moved, n_in, scratch=(), limit=None):
    return pl.pallas_call(
        body,
        out_shape=outs,
        in_specs=[VMEM] * n_in,
        out_specs=jax.tree.map(lambda _: VMEM, outs),
        scratch_shapes=scratch,
        cost_estimate=pl.CostEstimate(flops=flops, bytes_accessed=moved, transcendentals=0),
        compiler_params=pltpu.CompilerParams(vmem_limit_bytes=limit or (32 << 20)),
    )


def halves(x):
    hi = x.astype(BF16)
    return hi, (x - hi.astype(F32)).astype(BF16)


def gelu(v):
    return 0.5 * v * (1.0 + jnp.tanh(0.7978845608028654 * (v + 0.044715 * (v * v * v))))


def planes_kernel(x_ref, lo_ref, mid_ref, hi_ref):
    lo_ref[...] = x_ref[:, 0, :]
    for p in range(mid_ref.shape[0]):
        mid_ref[p] = x_ref[:, p + 1, :]
    hi_ref[...] = x_ref[:, x_ref.shape[1] - 1, :]


def taps_kernel(k_ref, w_ref, pad_ref):
    layers, width, taps = k_ref.shape
    lane = lax.broadcasted_iota(jnp.int32, (width, 128), 1)
    pad_ref[...] = jnp.zeros_like(pad_ref)
    for layer in range(layers):
        pad_ref[:, :taps] = k_ref[layer]
        for tap in range(9):
            start = tap * 3 * width
            base, shift = start // 128 * 128, start % 128
            pair = pad_ref[:, base : base + 256]
            if shift:
                pair = pltpu.roll(pair, 256 - shift, 1)
            hi, lo = halves(jnp.where(lane < 3 * width, pair[:, :128], 0.0))
            rows = pl.ds(tap * width, width)
            w_ref[layer, rows, 0:128] = hi
            w_ref[layer, rows, 128:256] = hi
            w_ref[layer, rows, 256:384] = lo


def mlp_weights_kernel(gain_ref, a_ref, b_ref, ah_ref, al_ref, bh_ref, bl_ref):
    gain = gain_ref[...]
    rows = 128
    for r in range(0, a_ref.shape[0], rows):
        hi, lo = halves(a_ref[r : r + rows, :] * gain)
        ah_ref[r : r + rows, :] = hi
        al_ref[r : r + rows, :] = lo
    for r in range(0, b_ref.shape[0], rows):
        hi, lo = halves(b_ref[r : r + rows, :])
        bh_ref[r : r + rows, :] = hi
        bl_ref[r : r + rows, :] = lo


def conv_plane(weight, three, acc_ref):
    zero = jnp.zeros_like(three[0][0])
    his = [t[0] for t in three] + [zero]
    los = [t[1] for t in three] + [zero]
    acc_ref[...] = jnp.dot(weight, jnp.concatenate(his + los + his, axis=0), preferred_element_type=F32)
    width = zero.shape[0]
    cells = zero.shape[1]

    def tap(b, c):
        return acc_ref[(b * 3 + c) * width : (b * 3 + c + 1) * width, :]

    column = lax.broadcasted_iota(jnp.int32, (width, 128), 1) % W
    sums = [
        tap(1, c) + pltpu.roll(tap(0, c), W, 1) + pltpu.roll(tap(2, c), cells - W, 1) for c in range(3)
    ]
    parts = []
    for v in range(0, cells, 128):
        left, here, right = (s[:, v : v + 128] for s in sums)
        left = jnp.where(column == 0, pltpu.roll(left, 128 - W + 1, 1), pltpu.roll(left, 1, 1))
        right = jnp.where(column == W - 1, pltpu.roll(right, W - 1, 1), pltpu.roll(right, 127, 1))
        parts.append(left + here + right)
    return jnp.concatenate(parts, axis=1)


def inner_kernel(layer, last, w_ref, lo_ref, mid_ref, hi_ref, *rest):
    if last:
        base_ref, out_ref, acc_ref = rest
    else:
        out_ref, acc_ref = rest
    planes = [halves(lo_ref[...])] + [halves(mid_ref[p]) for p in range(mid_ref.shape[0])] + [halves(hi_ref[...])]
    weight = w_ref[layer]
    for p in range(mid_ref.shape[0]):
        total = conv_plane(weight, planes[p : p + 3], acc_ref.at[p])
        if last:
            store_cells(out_ref, p, base_ref[p] + total)
        else:
            out_ref[p] = gelu(total)


def store_cells(out_ref, plane, value):
    size = out_ref.shape[2]
    runs = value.shape[1] // size
    for q in range(runs):
        out_ref[plane * runs + q] = value[:, q * size : (q + 1) * size]


def outer_kernel(layer, last, w_ref, before_ref, lo_ref, mid_ref, hi_ref, after_ref, *rest):
    inner = mid_ref.shape[0]
    if last:
        base_lo_ref, base_hi_ref, done_ref, out_ref, acc_ref = rest
    else:
        out_lo_ref, out_hi_ref, acc_ref = rest
    weight = w_ref[layer]
    low = [halves(before_ref[...]), halves(lo_ref[...]), halves(mid_ref[0])]
    high = [halves(mid_ref[inner - 1]), halves(hi_ref[...]), halves(after_ref[...])]
    low = conv_plane(weight, low, acc_ref.at[0])
    if last:
        store_cells(out_ref, 0, base_lo_ref[...] + low)
    else:
        out_lo_ref[...] = gelu(low)
    high = conv_plane(weight, high, acc_ref.at[1])
    if last:
        store_cells(out_ref, inner + 1, base_hi_ref[...] + high)
        runs = done_ref.shape[0] // inner
        out_ref[runs : runs * (inner + 1)] = done_ref[...]
    else:
        out_hi_ref[...] = gelu(high)


def mlp_kernel(y_ref, ah_ref, al_ref, bh_ref, bl_ref, out_ref, hh_ref, hl_ref):
    y = y_ref[...]
    scale = lax.rsqrt(jnp.mean(y * y, axis=0, keepdims=True) + 1e-06)
    hi, lo = halves(y * scale)
    seen = jnp.concatenate([hi, lo, hi], axis=0)
    rows = 256
    for r in range(0, ah_ref.shape[0], rows):
        part = jnp.concatenate([ah_ref[r : r + rows, :], ah_ref[r : r + rows, :], al_ref[r : r + rows, :]], axis=1)
        hid = gelu(jnp.dot(part, seen, preferred_element_type=F32))
        hh, hl = halves(hid)
        hh_ref[r : r + rows, :] = hh
        hl_ref[r : r + rows, :] = hl
    seen = jnp.concatenate([hh_ref[...], hl_ref[...], hh_ref[...]], axis=0)
    for r in range(0, bh_ref.shape[0], rows):
        part = jnp.concatenate([bh_ref[r : r + rows, :], bh_ref[r : r + rows, :], bl_ref[r : r + rows, :]], axis=1)
        out_ref[r : r + rows, :] = y_ref[r : r + rows, :] + jnp.dot(part, seen, preferred_element_type=F32)


def place_kernel(in_ref, out_ref):
    size = in_ref.shape[2]
    runs = out_ref.shape[2] // size
    for p in range(out_ref.shape[1]):
        for q in range(runs):
            out_ref[:, p, q * size : (q + 1) * size] = in_ref[p * runs + q]


def per_device(volume, conv_weight, norm_gain, mlp_in, mlp_out):
    width, planes, cells = volume.shape
    inner = planes - 2
    count = lax.axis_size("depth")
    members = lax.axis_size("chan")
    kernels = conv_weight[0, :, 0]
    layers = kernels.shape[0]
    channels, hidden = mlp_out.shape[1], mlp_out.shape[2]
    size = planes * cells // members
    flops = 2 * 288 * 384 * cells
    plane = jax.ShapeDtypeStruct((width, cells), F32)
    middle = jax.ShapeDtypeStruct((inner, width, cells), F32)
    acc = [pltpu.VMEM((2, 9 * width, cells), F32)]
    up = [(i, (i + 1) % count) for i in range(count)]
    down = [((i + 1) % count, i) for i in range(count)]

    lo, mid, hi = call(planes_kernel, (plane, middle, plane), 0, volume.size * 8, 1)(volume)
    first = (lo, mid, hi)
    before = lax.ppermute(hi, "depth", up)
    after = lax.ppermute(lo, "depth", down)
    weight = call(
        taps_kernel,
        jax.ShapeDtypeStruct((layers, 9 * width, 384), BF16),
        0,
        kernels.size * 8,
        1,
        [pltpu.VMEM((width, 1024), F32)],
    )(kernels)
    w_in = jax.ShapeDtypeStruct((hidden, channels), BF16)
    w_out = jax.ShapeDtypeStruct((channels, hidden), BF16)
    pieces = call(
        mlp_weights_kernel, (w_in, w_in, w_out, w_out), 0, mlp_in.size * 16, 3
    )(norm_gain, mlp_in[0], mlp_out[0])
    for layer in range(layers):
        last = layer == layers - 1
        if last:
            done = call(
                functools.partial(inner_kernel, layer, True),
                jax.ShapeDtypeStruct((inner * cells // size, width, size), F32),
                inner * flops,
                volume.size * 8,
                5,
                acc,
            )(weight, lo, mid, hi, first[1])
            mixed = call(
                functools.partial(outer_kernel, layer, True),
                jax.ShapeDtypeStruct((members, width, size), F32),
                2 * flops,
                volume.size * 8,
                9,
                acc,
            )(weight, before, lo, mid, hi, after, first[0], first[2], done)
        else:
            new_mid = call(
                functools.partial(inner_kernel, layer, False), middle, inner * flops, volume.size * 8, 4, acc
            )(weight, lo, mid, hi)
            new_lo, new_hi = call(
                functools.partial(outer_kernel, layer, False), (plane, plane), 2 * flops, volume.size * 8, 6, acc
            )(weight, before, lo, mid, hi, after)
            lo, mid, hi = new_lo, new_mid, new_hi
            before = lax.ppermute(hi, "depth", up)
            after = lax.ppermute(lo, "depth", down)
    here = lax.all_to_all(mixed, "chan", split_axis=0, concat_axis=0, tiled=True)
    out = call(
        mlp_kernel,
        jax.ShapeDtypeStruct((channels, size), F32),
        12 * hidden * channels * size,
        mlp_in.size * 8,
        5,
        [pltpu.VMEM((hidden, size), BF16)] * 2,
    )(here.reshape(channels, size), *pieces)
    back = lax.all_to_all(out.reshape(members, width, size), "chan", split_axis=0, concat_axis=0, tiled=True)
    return call(place_kernel, jax.ShapeDtypeStruct(volume.shape, F32), 0, volume.size * 8, 1)(back)


def solution(mesh):
    in_specs = (P("chan", "depth", None), P(None, None, "chan", None, None), P(), P(), P())
    out_specs = P("chan", "depth", None)
    return jax.shard_map(
        per_device, mesh=mesh, in_specs=in_specs, out_specs=out_specs, check_vma=False
    )
```

profile of v0, /device:TPU:1, one launch (start us, length us, event | category | flops | bytes accessed | tf_op | source)
XLA Modules:
  0.0 76.5 jit_solution(17009929503704917087)
XLA Ops:
  0.0 0.0 copy-start.2
  0.0 1.0 %copy-done.2 = f32[32,4,1024]{2,1,0:T(4,128)S(1)} copy-done((f32[32,4,1024]{2,1,0:T(4,128)S(1)}, f32[32,4,1024]{2,1,0:T(4,128)}, u32[]{:S(2)}) %copy-start.2) | copy-done | bytes 524312
  1.0 0.1 shard_map.56
  1.1 2.2 %collective-permute-start = (f32[32,1024]{1,0:T(8,128)S(1)}, f32[32,1024]{1,0:T(8,128)S(1)}, u32[]{:S(2)}, u32[]{:S(2)}) collective-permute-start(f32[32,1024]{1,0:T(8,128)S(1)} %get-tuple-element.16.hi_ref.rest_1_), channel_id=1, source_target_pairs={{0,16},{16,32},{32,48},{48,64},{64,80},{80,96},{96,112},{112,0},{1... | collective-permute-start | bytes 393224 | tf_op jit(solution)/shard_map/ppermute | solution.py:189
  3.3 2.3 %collective-permute-start.1 = (f32[32,1024]{1,0:T(8,128)S(1)}, f32[32,1024]{1,0:T(8,128)S(1)}, u32[]{:S(2)}, u32[]{:S(2)}) collective-permute-start(f32[32,1024]{1,0:T(8,128)S(1)} %get-tuple-element.17.lo_ref.rest_0_), channel_id=1, source_target_pairs={{16,0},{32,16},{48,32},{64,48},{80,64},{96,80},{112,96},{0,112},{1... | collective-permute-start | bytes 393224 | tf_op jit(solution)/shard_map/ppermute | solution.py:190
  5.6 0.0 copy-start.3
  5.6 1.0 %copy-done.3 = f32[1,3,1,32,864]{4,3,2,1,0:T(8,128)S(1)} copy-done((f32[1,3,1,32,864]{4,3,2,1,0:T(8,128)S(1)}, f32[1,3,1,32,864]{4,3,2,1,0:T(8,128)}, u32[]{:S(2)}) %copy-start.3) | copy-done | bytes 331800
  6.6 0.2 shard_map.55.w_ref
  6.8 1.6 %collective-permute-done.before_ref = f32[32,1024]{1,0:T(8,128)S(1)} collective-permute-done((f32[32,1024]{1,0:T(8,128)S(1)}, f32[32,1024]{1,0:T(8,128)S(1)}, u32[]{:S(2)}, u32[]{:S(2)}) %collective-permute-start) | collective-permute-done | bytes 131104 | tf_op jit(solution)/shard_map/ppermute | solution.py:189
  8.4 2.3 %collective-permute-done.1.after_ref = f32[32,1024]{1,0:T(8,128)S(1)} collective-permute-done((f32[32,1024]{1,0:T(8,128)S(1)}, f32[32,1024]{1,0:T(8,128)S(1)}, u32[]{:S(2)}, u32[]{:S(2)}) %collective-permute-start.1) | collective-permute-done | bytes 131104 | tf_op jit(solution)/shard_map/ppermute | solution.py:190
  10.8 1.1 %shard_map.57 = (f32[32,1024]{1,0:T(8,128)S(1)}, f32[32,1024]{1,0:T(8,128)S(1)}) custom-call(bf16[3,288,384]{2,1,0:T(8,128)(2,1)S(1)} %shard_map.55.w_ref, f32[32,1024]{1,0:T(8,128)S(1)} %collective-permute-done.before_ref, f32[32,1024]{1,0:T(8,128)S(1)} %get-tuple-element.17.lo_ref.rest_0_, f32[2,32,1024]{2,1,0:T(8,128)S(1)} %get-tuple-element.18.mid_ref.rest_0_, ...), custom_call_target="tpu_custom_call" | custom-call | flops 452984832 | bytes 1048576 | tf_op jit(solution)/shard_map/pallas_call | solution.py:227
  11.9 0.1 collective-permute-start.2
  12.0 3.6 %collective-permute-start.3 = (f32[32,1024]{1,0:T(8,128)S(1)}, f32[32,1024]{1,0:T(8,128)S(1)}, u32[]{:S(2)}, u32[]{:S(2)}) collective-permute-start(f32[32,1024]{1,0:T(8,128)S(1)} %get-tuple-element.20.lo_ref), channel_id=1, source_target_pairs={{16,0},{32,16},{48,32},{64,48},{80,64},{96,80},{112,96},{0,112},{1... | collective-permute-start | bytes 393224 | tf_op jit(solution)/shard_map/ppermute | solution.py:232
  15.6 1.1 %shard_map.58.mid_ref = f32[2,32,1024]{2,1,0:T(8,128)S(1)} custom-call(bf16[3,288,384]{2,1,0:T(8,128)(2,1)S(1)} %shard_map.55.w_ref, f32[32,1024]{1,0:T(8,128)S(1)} %get-tuple-element.17.lo_ref.rest_0_, f32[2,32,1024]{2,1,0:T(8,128)S(1)} %get-tuple-element.18.mid_ref.rest_0_, f32[32,1024]{1,0:T(8,128)S(1)} %get-tuple-element.16.hi_ref.rest_1_), custom_call_target="tpu_custom_call" | custom-call | flops 452984832 | bytes 1048576 | tf_op jit(solution)/shard_map/pallas_call | solution.py:224
  16.7 1.4 %collective-permute-done.2.before_ref = f32[32,1024]{1,0:T(8,128)S(1)} collective-permute-done((f32[32,1024]{1,0:T(8,128)S(1)}, f32[32,1024]{1,0:T(8,128)S(1)}, u32[]{:S(2)}, u32[]{:S(2)}) %collective-permute-start.2) | collective-permute-done | bytes 131104 | tf_op jit(solution)/shard_map/ppermute | solution.py:231
  18.0 2.7 %collective-permute-done.3.after_ref = f32[32,1024]{1,0:T(8,128)S(1)} collective-permute-done((f32[32,1024]{1,0:T(8,128)S(1)}, f32[32,1024]{1,0:T(8,128)S(1)}, u32[]{:S(2)}, u32[]{:S(2)}) %collective-permute-start.3) | collective-permute-done | bytes 131104 | tf_op jit(solution)/shard_map/ppermute | solution.py:232
  20.8 1.1 %shard_map.59 = (f32[32,1024]{1,0:T(8,128)S(1)}, f32[32,1024]{1,0:T(8,128)S(1)}) custom-call(bf16[3,288,384]{2,1,0:T(8,128)(2,1)S(1)} %shard_map.55.w_ref, f32[32,1024]{1,0:T(8,128)S(1)} %collective-permute-done.2.before_ref, f32[32,1024]{1,0:T(8,128)S(1)} %get-tuple-element.20.lo_ref, f32[2,32,1024]{2,1,0:T(8,128)S(1)} %shard_map.58.mid_ref, ...), custom_call_target="tpu_custom_call" | custom-call | flops 452984832 | bytes 1048576 | tf_op jit(solution)/shard_map/pallas_call | solution.py:227
  21.9 0.1 collective-permute-start.4
  22.0 3.6 %collective-permute-start.5 = (f32[32,1024]{1,0:T(8,128)S(1)}, f32[32,1024]{1,0:T(8,128)S(1)}, u32[]{:S(2)}, u32[]{:S(2)}) collective-permute-start(f32[32,1024]{1,0:T(8,128)S(1)} %get-tuple-element.22.lo_ref), channel_id=1, source_target_pairs={{16,0},{32,16},{48,32},{64,48},{80,64},{96,80},{112,96},{0,112},{1... | collective-permute-start | bytes 393224 | tf_op jit(solution)/shard_map/ppermute | solution.py:232
  25.6 1.1 %shard_map.60.mid_ref = f32[2,32,1024]{2,1,0:T(8,128)S(1)} custom-call(bf16[3,288,384]{2,1,0:T(8,128)(2,1)S(1)} %shard_map.55.w_ref, f32[32,1024]{1,0:T(8,128)S(1)} %get-tuple-element.20.lo_ref, f32[2,32,1024]{2,1,0:T(8,128)S(1)} %shard_map.58.mid_ref, f32[32,1024]{1,0:T(8,128)S(1)} %get-tuple-element.19.hi_ref), custom_call_target="tpu_custom_call" | custom-call | flops 452984832 | bytes 1048576 | tf_op jit(solution)/shard_map/pallas_call | solution.py:224
  26.7 1.1 %shard_map.61.rest_2_ = f32[8,32,256]{2,1,0:T(8,128)S(1)} custom-call(bf16[3,288,384]{2,1,0:T(8,128)(2,1)S(1)} %shard_map.55.w_ref, f32[32,1024]{1,0:T(8,128)S(1)} %get-tuple-element.22.lo_ref, f32[2,32,1024]{2,1,0:T(8,128)S(1)} %shard_map.60.mid_ref, f32[32,1024]{1,0:T(8,128)S(1)} %get-tuple-element.21.hi_ref, ...), custom_call_target="tpu_custom_call" | custom-call | flops 452984832 | bytes 1048576 | tf_op jit(solution)/shard_map/pallas_call | solution.py:207
  27.8 0.0 copy-start
  27.8 0.0 copy-start.4
  27.8 0.2 collective-permute-done.4.before_ref
  28.0 3.4 %collective-permute-done.5.after_ref = f32[32,1024]{1,0:T(8,128)S(1)} collective-permute-done((f32[32,1024]{1,0:T(8,128)S(1)}, f32[32,1024]{1,0:T(8,128)S(1)}, u32[]{:S(2)}, u32[]{:S(2)}) %collective-permute-start.5) | collective-permute-done | bytes 131104 | tf_op jit(solution)/shard_map/ppermute | solution.py:232
  31.5 1.9 %shard_map.62 = f32[16,32,256]{2,1,0:T(8,128)} custom-call(bf16[3,288,384]{2,1,0:T(8,128)(2,1)S(1)} %shard_map.55.w_ref, f32[32,1024]{1,0:T(8,128)S(1)} %collective-permute-done.4.before_ref, f32[32,1024]{1,0:T(8,128)S(1)} %get-tuple-element.22.lo_ref, f32[2,32,1024]{2,1,0:T(8,128)S(1)} %shard_map.60.mid_ref, f32[32,1024]{1,0:T(8,128)S(1)} %get-tuple-element.21.hi_ref, ...), custom_call_target="tpu_custom_call" | custom-call | flops 452984832 | bytes 1048576 | tf_op jit(solution)/shard_map/pallas_call | solution.py:215
  33.4 8.9 %all-to-all-start = ((f32[16,32,256]{2,1,0:T(8,128)}), f32[16,32,256]{2,1,0:T(8,128)S(1)}, u32[]{:S(2)}, u32[]{:S(2)}) async-start(f32[16,32,256]{2,1,0:T(8,128)} %shard_map.62), calls=%async_computation | async-start | bytes 1048576 | tf_op jit(solution)/shard_map/all_to_all | solution.py:233
  42.2 0.0 copy-done
  42.2 0.0 copy-done.4
  42.3 0.0 copy-start.1
  42.3 1.6 %copy-done.1 = f32[1,512,1024]{2,1,0:T(8,128)S(1)} copy-done((f32[1,512,1024]{2,1,0:T(8,128)S(1)}, f32[1,512,1024]{2,1,0:T(8,128)}, u32[]{:S(2)}) %copy-start.1) | copy-done | bytes 2097176
  43.8 0.7 shard_map.63
  44.6 0.0 copy-start.5
  44.6 1.0 %copy-done.5 = bf16[1024,512]{1,0:T(8,128)(2,1)} copy-done((bf16[1024,512]{1,0:T(8,128)(2,1)}, bf16[1024,512]{1,0:T(8,128)(2,1)S(1)}, u32[]{:S(2)}) %copy-start.5) | copy-done | bytes 1048600
  45.6 0.0 copy-start.7
  45.6 1.0 %copy-done.7 = bf16[1024,512]{1,0:T(8,128)(2,1)} copy-done((bf16[1024,512]{1,0:T(8,128)(2,1)}, bf16[1024,512]{1,0:T(8,128)(2,1)S(1)}, u32[]{:S(2)}) %copy-start.7) | copy-done | bytes 1048600
  46.5 0.0 copy-start.9
  46.5 1.0 %copy-done.9 = bf16[512,1024]{1,0:T(8,128)(2,1)} copy-done((bf16[512,1024]{1,0:T(8,128)(2,1)}, bf16[512,1024]{1,0:T(8,128)(2,1)S(1)}, u32[]{:S(2)}) %copy-start.9) | copy-done | bytes 1048600
  47.5 1.0 %copy-done.11 = bf16[512,1024]{1,0:T(8,128)(2,1)} copy-done((bf16[512,1024]{1,0:T(8,128)(2,1)}, bf16[512,1024]{1,0:T(8,128)(2,1)S(1)}, u32[]{:S(2)}) %copy-start.11) | copy-done | bytes 1048600
  48.5 5.0 %all-to-all-done = f32[16,32,256]{2,1,0:T(8,128)S(1)} async-done(((f32[16,32,256]{2,1,0:T(8,128)}), f32[16,32,256]{2,1,0:T(8,128)S(1)}, u32[]{:S(2)}, u32[]{:S(2)}) %all-to-all-start) | async-done | bytes 524320 | tf_op jit(solution)/shard_map/all_to_all | solution.py:233
  53.5 0.0 copy-start.6
  53.5 1.2 %copy-done.6 = bf16[1024,512]{1,0:T(8,128)(2,1)S(1)} copy-done((bf16[1024,512]{1,0:T(8,128)(2,1)S(1)}, bf16[1024,512]{1,0:T(8,128)(2,1)}, u32[]{:S(2)}) %copy-start.6) | copy-done | bytes 1048600
  54.8 1.2 %copy-done.8 = bf16[1024,512]{1,0:T(8,128)(2,1)S(1)} copy-done((bf16[1024,512]{1,0:T(8,128)(2,1)S(1)}, bf16[1024,512]{1,0:T(8,128)(2,1)}, u32[]{:S(2)}) %copy-start.8) | copy-done | bytes 1048600
  56.0 1.2 %copy-done.10 = bf16[512,1024]{1,0:T(8,128)(2,1)S(1)} copy-done((bf16[512,1024]{1,0:T(8,128)(2,1)S(1)}, bf16[512,1024]{1,0:T(8,128)(2,1)}, u32[]{:S(2)}) %copy-start.10) | copy-done | bytes 1048600
  57.2 1.2 %copy-done.12 = bf16[512,1024]{1,0:T(8,128)(2,1)S(1)} copy-done((bf16[512,1024]{1,0:T(8,128)(2,1)S(1)}, bf16[512,1024]{1,0:T(8,128)(2,1)}, u32[]{:S(2)}) %copy-start.12) | copy-done | bytes 1048600
  58.4 2.0 %shard_map.64 = f32[512,256]{1,0:T(8,128)S(1)} custom-call(f32[512,256]{1,0:T(8,128)S(1)} %bitcast.7, bf16[1024,512]{1,0:T(8,128)(2,1)S(1)} %copy-done.6, bf16[1024,512]{1,0:T(8,128)(2,1)S(1)} %copy-done.8, bf16[512,1024]{1,0:T(8,128)(2,1)S(1)} %copy-done.10, bf16[512,1024]{1,0:T(8,128)(2,1)S(1)} %copy-done.12), custom_call_target="tpu_custom_call" | custom-call | flops 1610612736 | bytes 4194304 | tf_op jit(solution)/shard_map/pallas_call | solution.py:234
  60.4 15.0 %all_to_all.10.in_ref = f32[16,32,256]{2,1,0:T(8,128)S(1)} all-to-all(f32[16,32,256]{2,1,0:T(8,128)S(1)} %bitcast.8), channel_id=1, replica_groups=mesh['depth'=8,'chan'=16] {'chan'}, dimensions={0} | all-to-all | bytes 1048576 | tf_op jit(solution)/shard_map/all_to_all | solution.py:242
  75.4 1.0 %shard_map.65 = f32[32,4,1024]{2,1,0:T(4,128)} custom-call(f32[16,32,256]{2,1,0:T(8,128)S(1)} %all_to_all.10.in_ref), custom_call_target="tpu_custom_call" | custom-call | bytes 1048576 | tf_op jit(solution)/shard_map/pallas_call | solution.py:243
  (4 shorter events, 0.0 us)
Async XLA Ops:
  0.0 1.0 %copy-start.2 = (f32[32,4,1024]{2,1,0:T(4,128)S(1)}, f32[32,4,1024]{2,1,0:T(4,128)}, u32[]{:S(2)}) copy-start(f32[32,4,1024]{2,1,0:T(4,128)} %x_ref.1) | copy-start | bytes 1572868
  1.1 7.3 %collective-permute-start = (f32[32,1024]{1,0:T(8,128)S(1)}, f32[32,1024]{1,0:T(8,128)S(1)}, u32[]{:S(2)}, u32[]{:S(2)}) collective-permute-start(f32[32,1024]{1,0:T(8,128)S(1)} %get-tuple-element.16.hi_ref.rest_1_), channel_id=1, source_target_pairs={{0,16},{16,32},{32,48},{48,64},{64,80},{80,96},{96,112},{112,0},{1... | collective-permute-start | bytes 393224 | tf_op jit(solution)/shard_map/ppermute | solution.py:189
  3.3 7.4 %collective-permute-start.1 = (f32[32,1024]{1,0:T(8,128)S(1)}, f32[32,1024]{1,0:T(8,128)S(1)}, u32[]{:S(2)}, u32[]{:S(2)}) collective-permute-start(f32[32,1024]{1,0:T(8,128)S(1)} %get-tuple-element.17.lo_ref.rest_0_), channel_id=1, source_target_pairs={{16,0},{32,16},{48,32},{64,48},{80,64},{96,80},{112,96},{0,112},{1... | collective-permute-start | bytes 393224 | tf_op jit(solution)/shard_map/ppermute | solution.py:190
  5.6 1.0 %copy-start.3 = (f32[1,3,1,32,864]{4,3,2,1,0:T(8,128)S(1)}, f32[1,3,1,32,864]{4,3,2,1,0:T(8,128)}, u32[]{:S(2)}) copy-start(f32[1,3,1,32,864]{4,3,2,1,0:T(8,128)} %param.6) | copy-start | bytes 995332
  11.9 6.1 %collective-permute-start.2 = (f32[32,1024]{1,0:T(8,128)S(1)}, f32[32,1024]{1,0:T(8,128)S(1)}, u32[]{:S(2)}, u32[]{:S(2)}) collective-permute-start(f32[32,1024]{1,0:T(8,128)S(1)} %get-tuple-element.19.hi_ref), channel_id=1, source_target_pairs={{0,16},{16,32},{32,48},{48,64},{64,80},{80,96},{96,112},{112,0},{1... | collective-permute-start | bytes 393224 | tf_op jit(solution)/shard_map/ppermute | solution.py:231
  12.0 8.8 %collective-permute-start.3 = (f32[32,1024]{1,0:T(8,128)S(1)}, f32[32,1024]{1,0:T(8,128)S(1)}, u32[]{:S(2)}, u32[]{:S(2)}) collective-permute-start(f32[32,1024]{1,0:T(8,128)S(1)} %get-tuple-element.20.lo_ref), channel_id=1, source_target_pairs={{16,0},{32,16},{48,32},{64,48},{80,64},{96,80},{112,96},{0,112},{1... | collective-permute-start | bytes 393224 | tf_op jit(solution)/shard_map/ppermute | solution.py:232
  21.9 6.1 %collective-permute-start.4 = (f32[32,1024]{1,0:T(8,128)S(1)}, f32[32,1024]{1,0:T(8,128)S(1)}, u32[]{:S(2)}, u32[]{:S(2)}) collective-permute-start(f32[32,1024]{1,0:T(8,128)S(1)} %get-tuple-element.21.hi_ref), channel_id=1, source_target_pairs={{0,16},{16,32},{32,48},{48,64},{64,80},{80,96},{96,112},{112,0},{1... | collective-permute-start | bytes 393224 | tf_op jit(solution)/shard_map/ppermute | solution.py:231
  22.0 9.5 %collective-permute-start.5 = (f32[32,1024]{1,0:T(8,128)S(1)}, f32[32,1024]{1,0:T(8,128)S(1)}, u32[]{:S(2)}, u32[]{:S(2)}) collective-permute-start(f32[32,1024]{1,0:T(8,128)S(1)} %get-tuple-element.22.lo_ref), channel_id=1, source_target_pairs={{16,0},{32,16},{48,32},{64,48},{80,64},{96,80},{112,96},{0,112},{1... | collective-permute-start | bytes 393224 | tf_op jit(solution)/shard_map/ppermute | solution.py:232
  27.8 14.5 %copy-start = (f32[1,1024,512]{2,1,0:T(8,128)S(1)}, f32[1,1024,512]{2,1,0:T(8,128)}, u32[]{:S(2)}) copy-start(f32[1,1024,512]{2,1,0:T(8,128)} %param.8) | copy-start | bytes 6291460
  27.8 14.5 %copy-start.4 = (f32[1,512]{1,0:T(1,128)S(1)}, f32[1,512]{1,0:T(1,128)}, u32[]{:S(2)}) copy-start(f32[1,512]{1,0:T(1,128)} %gain_ref.1) | copy-start | bytes 6148
  33.4 20.2 %all-to-all-start = ((f32[16,32,256]{2,1,0:T(8,128)}), f32[16,32,256]{2,1,0:T(8,128)S(1)}, u32[]{:S(2)}, u32[]{:S(2)}) async-start(f32[16,32,256]{2,1,0:T(8,128)} %shard_map.62), calls=%async_computation | async-start | bytes 1048576 | tf_op jit(solution)/shard_map/all_to_all | solution.py:233
  42.3 1.6 %copy-start.1 = (f32[1,512,1024]{2,1,0:T(8,128)S(1)}, f32[1,512,1024]{2,1,0:T(8,128)}, u32[]{:S(2)}) copy-start(f32[1,512,1024]{2,1,0:T(8,128)} %param.9) | copy-start | bytes 6291460
  44.6 1.0 %copy-start.5 = (bf16[1024,512]{1,0:T(8,128)(2,1)}, bf16[1024,512]{1,0:T(8,128)(2,1)S(1)}, u32[]{:S(2)}) copy-start(bf16[1024,512]{1,0:T(8,128)(2,1)S(1)} %get-tuple-element.23.ah_ref) | copy-start | bytes 3145732
  45.6 1.0 %copy-start.7 = (bf16[1024,512]{1,0:T(8,128)(2,1)}, bf16[1024,512]{1,0:T(8,128)(2,1)S(1)}, u32[]{:S(2)}) copy-start(bf16[1024,512]{1,0:T(8,128)(2,1)S(1)} %get-tuple-element.24.al_ref) | copy-start | bytes 3145732
  46.5 1.0 %copy-start.9 = (bf16[512,1024]{1,0:T(8,128)(2,1)}, bf16[512,1024]{1,0:T(8,128)(2,1)S(1)}, u32[]{:S(2)}) copy-start(bf16[512,1024]{1,0:T(8,128)(2,1)S(1)} %get-tuple-element.25.bh_ref) | copy-start | bytes 3145732
  47.5 1.0 %copy-start.11 = (bf16[512,1024]{1,0:T(8,128)(2,1)}, bf16[512,1024]{1,0:T(8,128)(2,1)S(1)}, u32[]{:S(2)}) copy-start(bf16[512,1024]{1,0:T(8,128)(2,1)S(1)} %get-tuple-element.26.bl_ref) | copy-start | bytes 3145732
  53.5 1.2 %copy-start.6 = (bf16[1024,512]{1,0:T(8,128)(2,1)S(1)}, bf16[1024,512]{1,0:T(8,128)(2,1)}, u32[]{:S(2)}) copy-start(bf16[1024,512]{1,0:T(8,128)(2,1)} %copy-done.5) | copy-start | bytes 3145732
  54.8 1.2 %copy-start.8 = (bf16[1024,512]{1,0:T(8,128)(2,1)S(1)}, bf16[1024,512]{1,0:T(8,128)(2,1)}, u32[]{:S(2)}) copy-start(bf16[1024,512]{1,0:T(8,128)(2,1)} %copy-done.7) | copy-start | bytes 3145732
  56.0 1.2 %copy-start.10 = (bf16[512,1024]{1,0:T(8,128)(2,1)S(1)}, bf16[512,1024]{1,0:T(8,128)(2,1)}, u32[]{:S(2)}) copy-start(bf16[512,1024]{1,0:T(8,128)(2,1)} %copy-done.9) | copy-start | bytes 3145732
  57.2 1.2 %copy-start.12 = (bf16[512,1024]{1,0:T(8,128)(2,1)S(1)}, bf16[512,1024]{1,0:T(8,128)(2,1)}, u32[]{:S(2)}) copy-start(bf16[512,1024]{1,0:T(8,128)(2,1)} %copy-done.11) | copy-start | bytes 3145732
where the time goes:
time: 77 us; the launch traced here: 76.5 us
  starting transfers between devices  20.6 us (27%)
  waiting for transfers between devices  16.8 us (22%)
  blocking collectives  15 us (19%)
  local copies, waits for them, and re-layouts  12.4 us (16%)
  Pallas kernels  11.6 us (15%)
    all_to_all x1, blocking collectives, per_device(): lax.all_to_all(out.reshape(members, width, size), 'chan', split_axis=0, c...  15 us
    unnamed x26, local copies, waits for them, and re-layouts  12.4 us
    ppermute x3, starting transfers between devices, per_device(): after = lax.ppermute(lo, 'depth', down)  9.4 us
    all_to_all x1, starting transfers between devices, per_device(): lax.all_to_all(mixed, 'chan', split_axis=0, concat_axis=0, tiled=True)  8.86 us
    ppermute x3, waiting for transfers between devices, per_device(): after = lax.ppermute(lo, 'depth', down)  8.53 us
    all_to_all x1, waiting for transfers between devices, per_device(): lax.all_to_all(mixed, 'chan', split_axis=0, concat_axis=0, tiled=True)  5.04 us
    ppermute x3, waiting for transfers between devices, per_device(): before = lax.ppermute(hi, 'depth', up)  3.19 us
    ppermute x3, starting transfers between devices, per_device(): before = lax.ppermute(hi, 'depth', up)  2.34 us
  transfers between devices with their start and end apart: 7, of which 7 were waited for; matrix products, arithmetic and copies ran while one was open for 0% of the time, Pallas kernels for 6%

commit v1 on v0

v1 whole, which is shorter than its diff:
```python
import functools

import jax
import jax.numpy as jnp
from jax import lax
from jax.experimental import pallas as pl
from jax.experimental.pallas import tpu as pltpu
from jax.sharding import PartitionSpec as P

W = 32
F32 = jnp.float32
BF16 = jnp.bfloat16
VMEM = pl.BlockSpec(memory_space=pltpu.VMEM)
HBM = pl.BlockSpec(memory_space=pltpu.HBM)


def call(body, outs, flops, moved, ins, scratch=(), outs_in=VMEM, room=32 << 20):
    return pl.pallas_call(
        body,
        out_shape=outs,
        in_specs=ins,
        out_specs=jax.tree.map(lambda _: outs_in, outs),
        scratch_shapes=scratch,
        cost_estimate=pl.CostEstimate(flops=flops, bytes_accessed=moved, transcendentals=0),
        compiler_params=pltpu.CompilerParams(vmem_limit_bytes=room),
    )


def halves(x):
    hi = x.astype(BF16)
    return hi, (x - hi.astype(F32)).astype(BF16)


def gelu(v):
    return 0.5 * v * (1.0 + jnp.tanh(0.7978845608028654 * (v + 0.044715 * (v * v * v))))


def turned_here():
    return lax.axis_index("depth") % 2 > 0


def planes_kernel(x_ref, *q_refs):
    last = len(q_refs) - 1
    flip = turned_here()
    for k, q_ref in enumerate(q_refs):
        q_ref[...] = jnp.where(flip, x_ref[:, last - k, :], x_ref[:, k, :])


def taps_kernel(k_ref, w_ref, pad_ref):
    layers, width, taps = k_ref.shape
    flip = turned_here()
    lane = lax.broadcasted_iota(jnp.int32, (width, 128), 1)
    pad_ref[...] = jnp.zeros_like(pad_ref)
    for layer in range(layers):
        pad_ref[:, :taps] = k_ref[layer]
        for tap in range(9):
            start = tap * 3 * width
            base, shift = start // 128 * 128, start % 128
            pair = pad_ref[:, base : base + 256]
            if shift:
                pair = pltpu.roll(pair, 256 - shift, 1)
            ahead = pair[:, :128]
            turned = jnp.where(
                lane < width,
                pltpu.roll(ahead, 128 - 2 * width, 1),
                jnp.where(lane < 2 * width, ahead, pltpu.roll(ahead, 2 * width, 1)),
            )
            hi, lo = halves(jnp.where(lane < 3 * width, jnp.where(flip, turned, ahead), 0.0))
            rows = pl.ds(tap * width, width)
            w_ref[layer, rows, 0:128] = hi
            w_ref[layer, rows, 128:256] = hi
            w_ref[layer, rows, 256:384] = lo


def mlp_weights_kernel(gain_ref, a_ref, b_ref, w_hbm, w_ref, sems):
    gain = gain_ref[...]
    hidden, channels = a_ref.shape
    rows = 128
    copies = []

    def send(start, count):
        part = pl.ds(start, count)
        copies.append(pltpu.make_async_copy(w_ref.at[part], w_hbm.at[part], sems.at[len(copies)]))
        copies[-1].start()

    for r in range(0, hidden, rows):
        hi, lo = halves(a_ref[r : r + rows, :] * gain)
        w_ref[r : r + rows, :] = hi
        w_ref[hidden + r : hidden + r + rows, :] = lo
    send(0, 2 * hidden)
    base = 2 * hidden
    for half in range(hidden // channels):
        for r in range(0, channels, rows):
            hi, lo = halves(b_ref[r : r + rows, half * channels : (half + 1) * channels])
            at = base + half * channels + r
            w_ref[at : at + rows, :] = hi
            w_ref[at + hidden : at + hidden + rows, :] = lo
    send(base, 2 * hidden)
    for copy in copies:
        copy.wait()


def conv_plane(weight, three, acc_ref):
    zero = jnp.zeros_like(three[0][0])
    his = [t[0] for t in three] + [zero]
    los = [t[1] for t in three] + [zero]
    acc_ref[...] = jnp.dot(weight, jnp.concatenate(his + los + his, axis=0), preferred_element_type=F32)
    width = zero.shape[0]
    cells = zero.shape[1]

    def tap(b, c):
        return acc_ref[(b * 3 + c) * width : (b * 3 + c + 1) * width, :]

    column = lax.broadcasted_iota(jnp.int32, (width, 128), 1) % W
    sums = [
        tap(1, c) + pltpu.roll(tap(0, c), W, 1) + pltpu.roll(tap(2, c), cells - W, 1) for c in range(3)
    ]
    parts = []
    for v in range(0, cells, 128):
        left, here, right = (s[:, v : v + 128] for s in sums)
        left = jnp.where(column == 0, pltpu.roll(left, 128 - W + 1, 1), pltpu.roll(left, 1, 1))
        right = jnp.where(column == W - 1, pltpu.roll(right, W - 1, 1), pltpu.roll(right, 127, 1))
        parts.append(left + here + right)
    return jnp.concatenate(parts, axis=1)


def store_cells(out_ref, plane, value):
    size = out_ref.shape[2]
    runs = value.shape[1] // size
    for q in range(runs):
        out_ref[plane * runs + q] = value[:, q * size : (q + 1) * size]


def stage_kernel(given, work, kept, first, w_ref, *refs):
    ins, refs = refs[: len(given)], refs[len(given) :]
    acc_ref = refs[-1]
    layers = w_ref.shape[0]
    ends = any(layer == layers for layer, _ in work)
    done_ref = refs[0] if len(refs) > len(kept) + ends + 1 else None
    refs = refs[done_ref is not None :]
    where = dict(zip(given, ins, strict=True))
    kept_at = dict(zip(kept, refs[: len(kept)], strict=True))
    held = {key: halves(ref[...]) for key, ref in where.items()}
    for n, (layer, place) in enumerate(work):
        total = conv_plane(w_ref[layer - 1], [held[layer - 1, place + d] for d in (-1, 0, 1)], acc_ref.at[n % 2])
        if layer == layers:
            store_cells(refs[len(kept)], place - first, where[0, place][...] + total)
            continue
        total = gelu(total)
        held[layer, place] = halves(total)
        if (layer, place) in kept_at:
            kept_at[layer, place][...] = total
    if done_ref is not None:
        out_ref = refs[len(kept)]
        out_ref[out_ref.shape[0] - done_ref.shape[0] :] = done_ref[...]


def mlp_kernel(y_ref, w_hbm, out_ref, w_ref, hh_ref, hl_ref, sems):
    channels = y_ref.shape[0]
    hidden = hh_ref.shape[0]
    rows = 256
    copies = []

    def fetch(*starts):
        group = []
        for start in starts:
            part = pl.ds(start, rows)
            group.append(pltpu.make_async_copy(w_hbm.at[part], w_ref.at[part], sems.at[len(copies) * 8 + len(group)]))
            group[-1].start()
        copies.append(group)

    base = 2 * hidden
    for r in range(0, hidden, rows):
        fetch(r, hidden + r)
    for r in range(0, channels, rows):
        fetch(*(base + part * channels + r for part in range(2 * hidden // channels)))
    y = y_ref[...]
    scale = lax.rsqrt(jnp.mean(y * y, axis=0, keepdims=True) + 1e-06)
    hi, lo = halves(y * scale)
    seen = jnp.concatenate([hi, lo, hi], axis=0)
    for n, r in enumerate(range(0, hidden, rows)):
        for copy in copies[n]:
            copy.wait()
        top, low = w_ref[r : r + rows, :], w_ref[hidden + r : hidden + r + rows, :]
        hid = gelu(jnp.dot(jnp.concatenate([top, top, low], axis=1), seen, preferred_element_type=F32))
        hh, hl = halves(hid)
        hh_ref[r : r + rows, :] = hh
        hl_ref[r : r + rows, :] = hl
    seen = jnp.concatenate([hh_ref[...], hl_ref[...], hh_ref[...]], axis=0)
    for n, r in enumerate(range(0, channels, rows)):
        for copy in copies[hidden // rows + n]:
            copy.wait()
        parts = [w_ref[base + p * channels + r : base + p * channels + r + rows, :] for p in range(2 * hidden // channels)]
        top = parts[: hidden // channels]
        part = jnp.concatenate(top + top + parts[hidden // channels :], axis=1)
        out_ref[r : r + rows, :] = y_ref[r : r + rows, :] + jnp.dot(part, seen, preferred_element_type=F32)


def place_kernel(in_ref, out_ref):
    size = in_ref.shape[2]
    runs = out_ref.shape[2] // size
    last = out_ref.shape[1] - 1
    flip = turned_here()
    for p in range(last + 1):
        for q in range(runs):
            out_ref[:, p, q * size : (q + 1) * size] = jnp.where(
                flip, in_ref[(last - p) * runs + q], in_ref[p * runs + q]
            )

def per_device(volume, conv_weight, norm_gain, mlp_in, mlp_out):
    width, planes, cells = volume.shape
    count = lax.axis_size("depth")
    members = lax.axis_size("chan")
    kernels = conv_weight[0, :, 0]
    layers = kernels.shape[0]
    channels, hidden = mlp_out.shape[1], mlp_out.shape[2]
    size = planes * cells // members
    runs = cells // size
    plane = jax.ShapeDtypeStruct((width, cells), F32)

    pair = [(i, i ^ 1) for i in range(count)]
    along = [(i, (i + (2 if i % 2 == 0 else count - 2)) % count) for i in range(count)]
    own = call(planes_kernel, (plane,) * planes, 0, volume.size * 8, [VMEM])(volume)
    there = [lax.ppermute(q, "depth", pair) for q in own[:2]]
    taps = call(
        taps_kernel,
        jax.ShapeDtypeStruct((layers, 9 * width, 384), BF16),
        0,
        kernels.size * 8,
        [VMEM],
        [pltpu.VMEM((width, 1024), F32)],
    )(kernels)
    held = {(0, 3 + k): v for k, v in enumerate(own)}

    def stage(given, work, kept, finished=None, placed=0, first=0):
        outs = (plane,) * len(kept)
        if placed:
            outs += (jax.ShapeDtypeStruct((placed * runs, width, size), F32),)
        more = [] if finished is None else [finished]
        got = call(
            functools.partial(stage_kernel, given, work, kept, first),
            outs,
            len(work) * 2 * 288 * 384 * cells,
            (len(given) + len(outs)) * width * cells * 4,
            [VMEM] * (1 + len(given) + len(more)),
            [pltpu.VMEM((2, 9 * width, cells), F32)],
        )(taps, *[held[key] for key in given], *more)
        held.update(zip(kept, got))
        return got[-1]

    stage(((0, 3), (0, 4), (0, 5), (0, 6)), ((1, 4), (1, 5)), ((1, 4), (1, 5)))
    third, held[1, 4], held[1, 5] = lax.optimization_barrier((own[2], held[1, 4], held[1, 5]))
    there += [lax.ppermute(q, "depth", pair) for q in (third, own[3])]
    for k in range(layers):
        held[0, 2 - k] = lax.ppermute(there[k], "depth", along)
        held[0, 9 - k] = there[k + 1]
    stage(
        ((0, 1), (0, 2), (0, 3), (0, 4), (1, 4), (1, 5)),
        ((1, 3), (1, 2), (2, 4), (2, 3)),
        ((1, 2), (1, 3), (2, 3), (2, 4)),
    )
    most = stage(
        ((0, 4), (0, 5), (0, 6), (0, 7), (0, 8), (0, 9), (1, 4), (1, 5), (2, 3), (2, 4)),
        ((1, 6), (1, 7), (1, 8), (2, 5), (2, 6), (2, 7), (3, 4), (3, 5), (3, 6)),
        (),
        placed=3,
        first=4,
    )
    mixed = stage(
        ((0, 0), (0, 1), (0, 2), (0, 3), (1, 2), (1, 3), (2, 3), (2, 4)),
        ((1, 1), (2, 2), (3, 3)),
        (),
        finished=most,
        placed=4,
        first=3,
    )
    pieces = call(
        mlp_weights_kernel,
        jax.ShapeDtypeStruct((4 * hidden, channels), BF16),
        0,
        mlp_in.size * 16,
        [VMEM] * 3,
        [pltpu.VMEM((4 * hidden, channels), BF16), pltpu.SemaphoreType.DMA((2,))],
        HBM,
        52 << 20,
    )(norm_gain, mlp_in[0], mlp_out[0])

    here = lax.all_to_all(mixed, "chan", split_axis=0, concat_axis=0, tiled=True)
    out = call(
        mlp_kernel,
        jax.ShapeDtypeStruct((channels, size), F32),
        12 * hidden * channels * size,
        mlp_in.size * 8,
        [VMEM, HBM],
        [
            pltpu.VMEM((4 * hidden, channels), BF16),
            pltpu.VMEM((hidden, size), BF16),
            pltpu.VMEM((hidden, size), BF16),
            pltpu.SemaphoreType.DMA((64,)),
        ],
        room=52 << 20,
    )(here.reshape(channels, size), pieces)
    back = lax.all_to_all(out.reshape(members, width, size), "chan", split_axis=0, concat_axis=0, tiled=True)
    return call(place_kernel, jax.ShapeDtypeStruct(volume.shape, F32), 0, volume.size * 8, [VMEM])(back)


def solution(mesh):
    in_specs = (P("chan", "depth", None), P(None, None, "chan", None, None), P(), P(), P())
    out_specs = P("chan", "depth", None)
    return jax.shard_map(
        per_device, mesh=mesh, in_specs=in_specs, out_specs=out_specs, check_vma=False
    )
```

time: 77 us -> 69.1 us (0.90)
  Pallas kernels: 11.6 us -> 22.2 us
  local copies, waits for them, and re-layouts: 12.4 us -> 2.03 us
  waiting for transfers between devices: 16.8 us -> 8.77 us
    unnamed x26 -> x6, local copies, waits for them, and re-layouts: 12.4 us -> 2.03 us
    ppermute x6 -> x7, waiting for transfers between devices: 11.7 us -> 2.01 us  [the longest x3 2 us: per_device(): held[0, 2 - k] = lax.ppermute(there[k], 'depth', along)]
    pallas_call x8 -> x6, Pallas kernels: 8.29 us -> 14.3 us  [the longest x4 9.65 us: stage(): call(functools.partial(stage_kernel, given, work, kept, first), outs, len...]
    pallas_call x1, Pallas kernels: 1.99 us -> 5.95 us  [per_device(): call(mlp_kernel, jax.ShapeDtypeStruct((channels, size), F32), 12 * hidden...]
    all_to_all x1, starting transfers between devices: 8.86 us -> 11.5 us  [per_device(): lax.all_to_all(mixed, 'chan', split_axis=0, concat_axis=0, tiled=True)]
    ppermute x6 -> x7, starting transfers between devices: 11.7 us -> 9.24 us  [the longest x2 4.02 us: per_device(): there += [lax.ppermute(q, 'depth', pair) for q in (third, own[3])]]
    all_to_all x1, waiting for transfers between devices: 5.04 us -> 6.76 us  [per_device(): lax.all_to_all(mixed, 'chan', split_axis=0, concat_axis=0, tiled=True)]
  transfers between devices with their start and end apart: 7 -> 8, of which waited for: 7 -> 2; matrix products, arithmetic and copies ran while one was open for 0% -> 0% of each run, Pallas kernels for 6% -> 18%
where the time goes in v1:
time: 69.1 us; the launch traced here: 68.8 us
  Pallas kernels  22.2 us (32%)
  starting transfers between devices  20.7 us (30%)
  blocking collectives  15 us (22%)
  waiting for transfers between devices  8.77 us (13%)
  local copies, waits for them, and re-layouts  2.03 us (3%)
    all_to_all x1, blocking collectives, per_device(): lax.all_to_all(out.reshape(members, width, size), 'chan', split_axis=0, c...  15 us
    all_to_all x1, starting transfers between devices, per_device(): lax.all_to_all(mixed, 'chan', split_axis=0, concat_axis=0, tiled=True)  11.5 us
    pallas_call x4, Pallas kernels, stage(): call(functools.partial(stage_kernel, given, work, kept, first), outs, len...  9.65 us
    all_to_all x1, waiting for transfers between devices, per_device(): lax.all_to_all(mixed, 'chan', split_axis=0, concat_axis=0, tiled=True)  6.76 us
    pallas_call x1, Pallas kernels, per_device(): call(mlp_kernel, jax.ShapeDtypeStruct((channels, size), F32), 12 * hidden...  5.95 us
    pallas_call x1, Pallas kernels, per_device(): call(mlp_weights_kernel, jax.ShapeDtypeStruct((4 * hidden, channels), BF1...  4.52 us
    ppermute x2, starting transfers between devices, per_device(): there += [lax.ppermute(q, 'depth', pair) for q in (third, own[3])]  4.02 us
    ppermute x3, starting transfers between devices, per_device(): held[0, 2 - k] = lax.ppermute(there[k], 'depth', along)  2.92 us
  transfers between devices with their start and end apart: 8, of which 2 were waited for; matrix products, arithmetic and copies ran while one was open for 0% of the time, Pallas kernels for 18%

profile of v1, /device:TPU:1, one launch (start us, length us, event | category | flops | bytes accessed | tf_op | source)
XLA Modules:
  0.0 68.8 jit_solution(18022609181138928227)
XLA Ops:
  0.0 0.0 copy-start
  0.0 1.0 %copy-done = f32[32,4,1024]{2,1,0:T(4,128)S(1)} copy-done((f32[32,4,1024]{2,1,0:T(4,128)S(1)}, f32[32,4,1024]{2,1,0:T(4,128)}, u32[]{:S(2)}) %copy-start) | copy-done | bytes 524312
  1.0 0.1 shard_map.56
  1.2 2.2 %collective-permute-start.4 = (f32[32,1024]{1,0:T(8,128)S(1)}, f32[32,1024]{1,0:T(8,128)S(1)}, u32[]{:S(2)}, u32[]{:S(2)}) collective-permute-start(f32[32,1024]{1,0:T(8,128)S(1)} %get-tuple-element.19.refs_0_.refs_2_.refs_3_), channel_id=1, source_target_pairs={{0,16},{16,0},{32,48},{48,32},{64,80},{80,64},{96,112},{112,96},{1... | collective-permute-start | bytes 393224 | tf_op jit(solution)/shard_map/ppermute | solution.py:224
  3.4 0.1 collective-permute-start.2
  3.5 0.0 copy-start.1
  3.5 1.0 %copy-done.1 = f32[1,3,1,32,864]{4,3,2,1,0:T(8,128)S(1)} copy-done((f32[1,3,1,32,864]{4,3,2,1,0:T(8,128)S(1)}, f32[1,3,1,32,864]{4,3,2,1,0:T(8,128)}, u32[]{:S(2)}) %copy-start.1) | copy-done | bytes 331800
  4.5 0.9 %shard_map.55.w_ref = bf16[3,288,384]{2,1,0:T(8,128)(2,1)S(1)} custom-call(f32[3,32,864]{2,1,0:T(8,128)S(1)} %bitcast.7), custom_call_target="tpu_custom_call" | custom-call | bytes 663552 | tf_op jit(solution)/shard_map/pallas_call | solution.py:225
  5.4 1.1 %shard_map.57 = (f32[32,1024]{1,0:T(8,128)S(1)}, f32[32,1024]{1,0:T(8,128)S(1)}) custom-call(bf16[3,288,384]{2,1,0:T(8,128)(2,1)S(1)} %shard_map.55.w_ref, f32[32,1024]{1,0:T(8,128)S(1)} %get-tuple-element.19.refs_0_.refs_2_.refs_3_, f32[32,1024]{1,0:T(8,128)S(1)} %get-tuple-element.20.refs_1_.refs_3_.refs_0_, ...), custom_call_target="tpu_custom_call" | custom-call | flops 452984832 | bytes 786432 | tf_op jit(solution)/shard_map/pallas_call | solution.py:240
  6.5 1.5 %collective-permute-start = (f32[32,1024]{1,0:T(8,128)S(1)}, f32[32,1024]{1,0:T(8,128)S(1)}, u32[]{:S(2)}, u32[]{:S(2)}) collective-permute-start(f32[32,1024]{1,0:T(8,128)S(1)} %get-tuple-element.24.refs_2_.refs_1_), channel_id=1, source_target_pairs={{0,16},{16,0},{32,48},{48,32},{64,80},{80,64},{96,112},{112,96},{1... | collective-permute-start | bytes 393224 | tf_op jit(solution)/shard_map/ppermute | solution.py:253
  8.0 0.0 collective-permute-done.4
  8.0 1.2 %collective-permute-start.5 = (f32[32,1024]{1,0:T(8,128)S(1)}, f32[32,1024]{1,0:T(8,128)S(1)}, u32[]{:S(2)}, u32[]{:S(2)}) collective-permute-start(f32[32,1024]{1,0:T(8,128)S(1)} %collective-permute-done.4), channel_id=1, source_target_pairs={{0,32},{16,112},{32,64},{48,16},{64,96},{80,48},{96,0},{112,80},{1... | collective-permute-start | bytes 393224 | tf_op jit(solution)/shard_map/ppermute | solution.py:255
  9.2 0.0 collective-permute-done.2.refs_5_
  9.2 1.3 %collective-permute-start.3 = (f32[32,1024]{1,0:T(8,128)S(1)}, f32[32,1024]{1,0:T(8,128)S(1)}, u32[]{:S(2)}, u32[]{:S(2)}) collective-permute-start(f32[32,1024]{1,0:T(8,128)S(1)} %collective-permute-done.2.refs_5_), channel_id=1, source_target_pairs={{0,32},{16,112},{32,64},{48,16},{64,96},{80,48},{96,0},{112,80},{1... | collective-permute-start | bytes 393224 | tf_op jit(solution)/shard_map/ppermute | solution.py:255
  10.5 2.6 %collective-permute-start.6 = (f32[32,1024]{1,0:T(8,128)S(1)}, f32[32,1024]{1,0:T(8,128)S(1)}, u32[]{:S(2)}, u32[]{:S(2)}) collective-permute-start(f32[32,1024]{1,0:T(8,128)S(1)} %get-tuple-element.21.refs_3_.refs_2_), channel_id=1, source_target_pairs={{0,16},{16,0},{32,48},{48,32},{64,80},{80,64},{96,112},{112,96},{1... | collective-permute-start | bytes 393224 | tf_op jit(solution)/shard_map/ppermute | solution.py:253
  13.0 0.0 collective-permute-done.refs_4_
  13.0 0.4 collective-permute-start.1
  13.4 0.0 collective-permute-done.5.refs_1_.refs_2_
  13.5 2.0 %collective-permute-done.3.refs_0_.refs_1_ = f32[32,1024]{1,0:T(8,128)S(1)} collective-permute-done((f32[32,1024]{1,0:T(8,128)S(1)}, f32[32,1024]{1,0:T(8,128)S(1)}, u32[]{:S(2)}, u32[]{:S(2)}) %collective-permute-start.3) | collective-permute-done | bytes 131104 | tf_op jit(solution)/shard_map/ppermute | solution.py:255
  15.4 1.9 %shard_map.58 = (f32[32,1024]{1,0:T(8,128)S(1)}, f32[32,1024]{1,0:T(8,128)S(1)}, f32[32,1024]{1,0:T(8,128)S(1)}, f32[32,1024]{1,0:T(8,128)S(1)}) custom-call(bf16[3,288,384]{2,1,0:T(8,128)(2,1)S(1)} %shard_map.55.w_ref, f32[32,1024]{1,0:T(8,128)S(1)} %collective-permute-done.3.refs_0_.refs_1_, f32[32,1024]{1,0:T(8,128)S(1)} %collective-permute-done.5.refs_1_.refs_2_, ...), custom_call_target="tpu_custom_call" | custom-call | flops 905969664 | bytes 1310720 | tf_op jit(solution)/shard_map/pallas_call | solution.py:240
  17.4 0.0 collective-permute-done.6.refs_3_
  17.4 3.8 %shard_map.59.refs_8_ = f32[12,32,256]{2,1,0:T(8,128)S(1)} custom-call(bf16[3,288,384]{2,1,0:T(8,128)(2,1)S(1)} %shard_map.55.w_ref, f32[32,1024]{1,0:T(8,128)S(1)} %get-tuple-element.20.refs_1_.refs_3_.refs_0_, f32[32,1024]{1,0:T(8,128)S(1)} %get-tuple-element.24.refs_2_.refs_1_, f32[32,1024]{1,0:T(8,128)S(1)} %get-tuple-element.21.refs_3_.refs_2_, ...), custom_call_target="tpu_custom_call" | custom-call | flops 2038431744 | bytes 1441792 | tf_op jit(solution)/shard_map/pallas_call | solution.py:240
  21.2 0.0 copy-start.2
  21.2 0.0 collective-permute-done.1.refs_0_
  21.2 2.8 %shard_map.60 = f32[16,32,256]{2,1,0:T(8,128)} custom-call(bf16[3,288,384]{2,1,0:T(8,128)(2,1)S(1)} %shard_map.55.w_ref, f32[32,1024]{1,0:T(8,128)S(1)} %collective-permute-done.1.refs_0_, f32[32,1024]{1,0:T(8,128)S(1)} %collective-permute-done.3.refs_0_.refs_1_, f32[32,1024]{1,0:T(8,128)S(1)} %collective-permute-done.5.refs_1_.refs_2_, ...), custom_call_target="tpu_custom_call" | custom-call | flops 679477248 | bytes 1179648 | tf_op jit(solution)/shard_map/pallas_call | solution.py:240
  24.0 11.5 %all-to-all-start = ((f32[16,32,256]{2,1,0:T(8,128)}), f32[16,32,256]{2,1,0:T(8,128)S(1)}, u32[]{:S(2)}, u32[]{:S(2)}) async-start(f32[16,32,256]{2,1,0:T(8,128)} %shard_map.60), calls=%async_computation | async-start | bytes 1048576 | tf_op jit(solution)/shard_map/all_to_all | solution.py:288
  35.5 0.0 copy-done.2
  35.5 4.5 %shard_map.61.w_hbm = bf16[4096,512]{1,0:T(8,128)(2,1)} custom-call(f32[1,512]{1,0:T(1,128)S(1)} %copy-done.2, f32[1024,512]{1,0:T(8,128)} %bitcast.8, f32[512,1024]{1,0:T(8,128)} %bitcast.9), custom_call_target="tpu_custom_call" | custom-call | bytes 8388608 | tf_op jit(solution)/shard_map/pallas_call | solution.py:277
  40.0 6.8 %all-to-all-done = f32[16,32,256]{2,1,0:T(8,128)S(1)} async-done(((f32[16,32,256]{2,1,0:T(8,128)}), f32[16,32,256]{2,1,0:T(8,128)S(1)}, u32[]{:S(2)}, u32[]{:S(2)}) %all-to-all-start) | async-done | bytes 524320 | tf_op jit(solution)/shard_map/all_to_all | solution.py:288
  46.8 5.9 %shard_map.62 = f32[512,256]{1,0:T(8,128)S(1)} custom-call(f32[512,256]{1,0:T(8,128)S(1)} %bitcast.5, bf16[4096,512]{1,0:T(8,128)(2,1)} %shard_map.61.w_hbm), custom_call_target="tpu_custom_call" | custom-call | flops 1610612736 | bytes 4194304 | tf_op jit(solution)/shard_map/pallas_call | solution.py:289
  52.8 15.0 %all_to_all.10.in_ref = f32[16,32,256]{2,1,0:T(8,128)S(1)} all-to-all(f32[16,32,256]{2,1,0:T(8,128)S(1)} %bitcast.6), channel_id=1, replica_groups=mesh['depth'=8,'chan'=16] {'chan'}, dimensions={0} | all-to-all | bytes 1048576 | tf_op jit(solution)/shard_map/all_to_all | solution.py:303
  67.7 1.1 %shard_map.63 = f32[32,4,1024]{2,1,0:T(4,128)} custom-call(f32[16,32,256]{2,1,0:T(8,128)S(1)} %all_to_all.10.in_ref), custom_call_target="tpu_custom_call" | custom-call | bytes 1048576 | tf_op jit(solution)/shard_map/pallas_call | solution.py:304
Async XLA Ops:
  0.0 1.0 %copy-start = (f32[32,4,1024]{2,1,0:T(4,128)S(1)}, f32[32,4,1024]{2,1,0:T(4,128)}, u32[]{:S(2)}) copy-start(f32[32,4,1024]{2,1,0:T(4,128)} %x_ref.1) | copy-start | bytes 1572868
  1.2 6.8 %collective-permute-start.4 = (f32[32,1024]{1,0:T(8,128)S(1)}, f32[32,1024]{1,0:T(8,128)S(1)}, u32[]{:S(2)}, u32[]{:S(2)}) collective-permute-start(f32[32,1024]{1,0:T(8,128)S(1)} %get-tuple-element.19.refs_0_.refs_2_.refs_3_), channel_id=1, source_target_pairs={{0,16},{16,0},{32,48},{48,32},{64,80},{80,64},{96,112},{112,96},{1... | collective-permute-start | bytes 393224 | tf_op jit(solution)/shard_map/ppermute | solution.py:224
  3.4 5.8 %collective-permute-start.2 = (f32[32,1024]{1,0:T(8,128)S(1)}, f32[32,1024]{1,0:T(8,128)S(1)}, u32[]{:S(2)}, u32[]{:S(2)}) collective-permute-start(f32[32,1024]{1,0:T(8,128)S(1)} %get-tuple-element.20.refs_1_.refs_3_.refs_0_), channel_id=1, source_target_pairs={{0,16},{16,0},{32,48},{48,32},{64,80},{80,64},{96,112},{112,96},{1... | collective-permute-start | bytes 393224 | tf_op jit(solution)/shard_map/ppermute | solution.py:224
  3.5 1.0 %copy-start.1 = (f32[1,3,1,32,864]{4,3,2,1,0:T(8,128)S(1)}, f32[1,3,1,32,864]{4,3,2,1,0:T(8,128)}, u32[]{:S(2)}) copy-start(f32[1,3,1,32,864]{4,3,2,1,0:T(8,128)} %param.6) | copy-start | bytes 995332
  6.5 6.5 %collective-permute-start = (f32[32,1024]{1,0:T(8,128)S(1)}, f32[32,1024]{1,0:T(8,128)S(1)}, u32[]{:S(2)}, u32[]{:S(2)}) collective-permute-start(f32[32,1024]{1,0:T(8,128)S(1)} %get-tuple-element.24.refs_2_.refs_1_), channel_id=1, source_target_pairs={{0,16},{16,0},{32,48},{48,32},{64,80},{80,64},{96,112},{112,96},{1... | collective-permute-start | bytes 393224 | tf_op jit(solution)/shard_map/ppermute | solution.py:253
  8.0 5.5 %collective-permute-start.5 = (f32[32,1024]{1,0:T(8,128)S(1)}, f32[32,1024]{1,0:T(8,128)S(1)}, u32[]{:S(2)}, u32[]{:S(2)}) collective-permute-start(f32[32,1024]{1,0:T(8,128)S(1)} %collective-permute-done.4), channel_id=1, source_target_pairs={{0,32},{16,112},{32,64},{48,16},{64,96},{80,48},{96,0},{112,80},{1... | collective-permute-start | bytes 393224 | tf_op jit(solution)/shard_map/ppermute | solution.py:255
  9.2 6.3 %collective-permute-start.3 = (f32[32,1024]{1,0:T(8,128)S(1)}, f32[32,1024]{1,0:T(8,128)S(1)}, u32[]{:S(2)}, u32[]{:S(2)}) collective-permute-start(f32[32,1024]{1,0:T(8,128)S(1)} %collective-permute-done.2.refs_5_), channel_id=1, source_target_pairs={{0,32},{16,112},{32,64},{48,16},{64,96},{80,48},{96,0},{112,80},{1... | collective-permute-start | bytes 393224 | tf_op jit(solution)/shard_map/ppermute | solution.py:255
  10.5 6.9 %collective-permute-start.6 = (f32[32,1024]{1,0:T(8,128)S(1)}, f32[32,1024]{1,0:T(8,128)S(1)}, u32[]{:S(2)}, u32[]{:S(2)}) collective-permute-start(f32[32,1024]{1,0:T(8,128)S(1)} %get-tuple-element.21.refs_3_.refs_2_), channel_id=1, source_target_pairs={{0,16},{16,0},{32,48},{48,32},{64,80},{80,64},{96,112},{112,96},{1... | collective-permute-start | bytes 393224 | tf_op jit(solution)/shard_map/ppermute | solution.py:253
  13.0 8.2 %collective-permute-start.1 = (f32[32,1024]{1,0:T(8,128)S(1)}, f32[32,1024]{1,0:T(8,128)S(1)}, u32[]{:S(2)}, u32[]{:S(2)}) collective-permute-start(f32[32,1024]{1,0:T(8,128)S(1)} %collective-permute-done.refs_4_), channel_id=1, source_target_pairs={{0,32},{16,112},{32,64},{48,16},{64,96},{80,48},{96,0},{112,80},{1... | collective-permute-start | bytes 393224 | tf_op jit(solution)/shard_map/ppermute | solution.py:255
  21.2 14.3 %copy-start.2 = (f32[1,512]{1,0:T(1,128)S(1)}, f32[1,512]{1,0:T(1,128)}, u32[]{:S(2)}) copy-start(f32[1,512]{1,0:T(1,128)} %gain_ref.1) | copy-start | bytes 6148
  24.0 22.8 %all-to-all-start = ((f32[16,32,256]{2,1,0:T(8,128)}), f32[16,32,256]{2,1,0:T(8,128)S(1)}, u32[]{:S(2)}, u32[]{:S(2)}) async-start(f32[16,32,256]{2,1,0:T(8,128)} %shard_map.60), calls=%async_computation | async-start | bytes 1048576 | tf_op jit(solution)/shard_map/all_to_all | solution.py:288

commit v2 on v1

--- a/solution.py
+++ b/solution.py
@@ -11,18 +11,17 @@
 F32 = jnp.float32
 BF16 = jnp.bfloat16
 VMEM = pl.BlockSpec(memory_space=pltpu.VMEM)
-HBM = pl.BlockSpec(memory_space=pltpu.HBM)
-
-
-def call(body, outs, flops, moved, ins, scratch=(), outs_in=VMEM, room=32 << 20):
+
+
+def call(body, outs, flops, moved, ins, scratch=()):
     return pl.pallas_call(
         body,
         out_shape=outs,
         in_specs=ins,
-        out_specs=jax.tree.map(lambda _: outs_in, outs),
+        out_specs=jax.tree.map(lambda _: VMEM, outs),
         scratch_shapes=scratch,
         cost_estimate=pl.CostEstimate(flops=flops, bytes_accessed=moved, transcendentals=0),
-        compiler_params=pltpu.CompilerParams(vmem_limit_bytes=room),
+        compiler_params=pltpu.CompilerParams(vmem_limit_bytes=32 << 20),
     )
 
 
@@ -72,22 +71,14 @@
             w_ref[layer, rows, 256:384] = lo
 
 
-def mlp_weights_kernel(gain_ref, a_ref, b_ref, w_hbm, w_ref, sems):
+def mlp_weights_kernel(gain_ref, a_ref, b_ref, w_ref):
     gain = gain_ref[...]
     hidden, channels = a_ref.shape
     rows = 128
-    copies = []
-
-    def send(start, count):
-        part = pl.ds(start, count)
-        copies.append(pltpu.make_async_copy(w_ref.at[part], w_hbm.at[part], sems.at[len(copies)]))
-        copies[-1].start()
-
     for r in range(0, hidden, rows):
         hi, lo = halves(a_ref[r : r + rows, :] * gain)
         w_ref[r : r + rows, :] = hi
         w_ref[hidden + r : hidden + r + rows, :] = lo
-    send(0, 2 * hidden)
     base = 2 * hidden
     for half in range(hidden // channels):
         for r in range(0, channels, rows):
@@ -95,9 +86,6 @@
             at = base + half * channels + r
             w_ref[at : at + rows, :] = hi
             w_ref[at + hidden : at + hidden + rows, :] = lo
-    send(base, 2 * hidden)
-    for copy in copies:
-        copy.wait()
 
 
 def conv_plane(weight, three, acc_ref):
@@ -155,41 +143,23 @@
         out_ref[out_ref.shape[0] - done_ref.shape[0] :] = done_ref[...]
 
 
-def mlp_kernel(y_ref, w_hbm, out_ref, w_ref, hh_ref, hl_ref, sems):
+def mlp_kernel(y_ref, w_ref, out_ref, hh_ref, hl_ref):
     channels = y_ref.shape[0]
     hidden = hh_ref.shape[0]
     rows = 256
-    copies = []
-
-    def fetch(*starts):
-        group = []
-        for start in starts:
-            part = pl.ds(start, rows)
-            group.append(pltpu.make_async_copy(w_hbm.at[part], w_ref.at[part], sems.at[len(copies) * 8 + len(group)]))
-            group[-1].start()
-        copies.append(group)
-
     base = 2 * hidden
-    for r in range(0, hidden, rows):
-        fetch(r, hidden + r)
-    for r in range(0, channels, rows):
-        fetch(*(base + part * channels + r for part in range(2 * hidden // channels)))
     y = y_ref[...]
     scale = lax.rsqrt(jnp.mean(y * y, axis=0, keepdims=True) + 1e-06)
     hi, lo = halves(y * scale)
     seen = jnp.concatenate([hi, lo, hi], axis=0)
-    for n, r in enumerate(range(0, hidden, rows)):
-        for copy in copies[n]:
-            copy.wait()
+    for r in range(0, hidden, rows):
         top, low = w_ref[r : r + rows, :], w_ref[hidden + r : hidden + r + rows, :]
         hid = gelu(jnp.dot(jnp.concatenate([top, top, low], axis=1), seen, preferred_element_type=F32))
         hh, hl = halves(hid)
         hh_ref[r : r + rows, :] = hh
         hl_ref[r : r + rows, :] = hl
     seen = jnp.concatenate([hh_ref[...], hl_ref[...], hh_ref[...]], axis=0)
-    for n, r in enumerate(range(0, channels, rows)):
-        for copy in copies[hidden // rows + n]:
-            copy.wait()
+    for r in range(0, channels, rows):
         parts = [w_ref[base + p * channels + r : base + p * channels + r + rows, :] for p in range(2 * hidden // channels)]
         top = parts[: hidden // channels]
         part = jnp.concatenate(top + top + parts[hidden // channels :], axis=1)
@@ -254,6 +224,14 @@
     for k in range(layers):
         held[0, 2 - k] = lax.ppermute(there[k], "depth", along)
         held[0, 9 - k] = there[k + 1]
+    pieces = call(
+        mlp_weights_kernel,
+        jax.ShapeDtypeStruct((4 * hidden, channels), BF16),
+        0,
+        mlp_in.size * 16,
+        [VMEM] * 3,
+    )(norm_gain, mlp_in[0], mlp_out[0])
+    pieces, held[1, 4] = lax.optimization_barrier((pieces, held[1, 4]))
     stage(
         ((0, 1), (0, 2), (0, 3), (0, 4), (1, 4), (1, 5)),
         ((1, 3), (1, 2), (2, 4), (2, 3)),
@@ -274,31 +252,14 @@
         placed=4,
         first=3,
     )
-    pieces = call(
-        mlp_weights_kernel,
-        jax.ShapeDtypeStruct((4 * hidden, channels), BF16),
-        0,
-        mlp_in.size * 16,
-        [VMEM] * 3,
-        [pltpu.VMEM((4 * hidden, channels), BF16), pltpu.SemaphoreType.DMA((2,))],
-        HBM,
-        52 << 20,
-    )(norm_gain, mlp_in[0], mlp_out[0])
-
     here = lax.all_to_all(mixed, "chan", split_axis=0, concat_axis=0, tiled=True)
     out = call(
         mlp_kernel,
         jax.ShapeDtypeStruct((channels, size), F32),
         12 * hidden * channels * size,
         mlp_in.size * 8,
-        [VMEM, HBM],
-        [
-            pltpu.VMEM((4 * hidden, channels), BF16),
-            pltpu.VMEM((hidden, size), BF16),
-            pltpu.VMEM((hidden, size), BF16),
-            pltpu.SemaphoreType.DMA((64,)),
-        ],
-        room=52 << 20,
+        [VMEM, VMEM],
+        [pltpu.VMEM((hidden, size), BF16)] * 2,
     )(here.reshape(channels, size), pieces)
     back = lax.all_to_all(out.reshape(members, width, size), "chan", split_axis=0, concat_axis=0, tiled=True)
     return call(place_kernel, jax.ShapeDtypeStruct(volume.shape, F32), 0, volume.size * 8, [VMEM])(back)

time: 69.1 us -> 63.9 us (0.925)
  blocking collectives: 15 us -> 37.1 us
  starting transfers between devices: 20.7 us -> 8.9 us
  waiting for transfers between devices: 8.77 us -> 0.05 us
  Pallas kernels: 22.2 us -> 13.7 us
  local copies, waits for them, and re-layouts: 2.03 us -> 3.77 us
    all_to_all x0 -> x1, blocking collectives: none -> 22.2 us  [per_device(): lax.all_to_all(mixed, 'chan', split_axis=0, concat_axis=0, tiled=True)]
    all_to_all x1 -> x0, starting transfers between devices: 11.5 us -> none  [per_device(): lax.all_to_all(mixed, 'chan', split_axis=0, concat_axis=0, tiled=True)]
    all_to_all x1 -> x0, waiting for transfers between devices: 6.76 us -> none  [per_device(): lax.all_to_all(mixed, 'chan', split_axis=0, concat_axis=0, tiled=True)]
    pallas_call x1, Pallas kernels: 5.95 us -> 1.98 us  [per_device(): call(mlp_kernel, jax.ShapeDtypeStruct((channels, size), F32), 12 * hidden...]
    pallas_call x1, Pallas kernels: 4.52 us -> 0.68 us  [per_device(): call(mlp_weights_kernel, jax.ShapeDtypeStruct((4 * hidden, channels), BF1...]
    ppermute x3, waiting for transfers between devices: 2 us -> 0.04 us  [per_device(): held[0, 2 - k] = lax.ppermute(there[k], 'depth', along)]
    unnamed x6 -> x10, local copies, waits for them, and re-layouts: 2.03 us -> 3.77 us
    pallas_call x4, Pallas kernels: 9.65 us -> 8.89 us  [stage(): call(functools.partial(stage_kernel, given, work, kept, first), outs, len...]
  transfers between devices with their start and end apart: 8 -> 7, of which waited for: 2 -> 0; matrix products, arithmetic and copies ran while one was open for 0% -> 0% of each run, Pallas kernels for 18% -> 13%
where the time goes in v2:
time: 63.9 us; the launch traced here: 63.6 us
  blocking collectives  37.1 us (58%)
  Pallas kernels  13.7 us (21%)
  starting transfers between devices  8.9 us (14%)
  local copies, waits for them, and re-layouts  3.77 us (6%)
    all_to_all x1, blocking collectives, per_device(): lax.all_to_all(mixed, 'chan', split_axis=0, concat_axis=0, tiled=True)  22.2 us
    all_to_all x1, blocking collectives, per_device(): lax.all_to_all(out.reshape(members, width, size), 'chan', split_axis=0, c...  15 us
    pallas_call x4, Pallas kernels, stage(): call(functools.partial(stage_kernel, given, work, kept, first), outs, len...  8.89 us
    ppermute x2, starting transfers between devices, per_device(): there += [lax.ppermute(q, 'depth', pair) for q in (third, own[3])]  4.02 us
    unnamed x10, local copies, waits for them, and re-layouts  3.77 us
    ppermute x3, starting transfers between devices, per_device(): held[0, 2 - k] = lax.ppermute(there[k], 'depth', along)  2.58 us
    ppermute x2, starting transfers between devices, per_device(): there = [lax.ppermute(q, 'depth', pair) for q in own[:2]]  2.3 us
    pallas_call x1, Pallas kernels, per_device(): call(mlp_kernel, jax.ShapeDtypeStruct((channels, size), F32), 12 * hidden...  1.98 us
  transfers between devices with their start and end apart: 7, of which 0 were waited for; matrix products, arithmetic and copies ran while one was open for 0% of the time, Pallas kernels for 13%

profile of v2, /device:TPU:1, one launch (start us, length us, event | category | flops | bytes accessed | tf_op | source)
XLA Modules:
  0.0 63.6 jit_solution(9013843850184786106)
XLA Ops:
  0.0 0.0 copy-start
  0.0 0.0 copy-start.2
  0.0 1.2 %copy-done.2 = f32[32,4,1024]{2,1,0:T(4,128)S(1)} copy-done((f32[32,4,1024]{2,1,0:T(4,128)S(1)}, f32[32,4,1024]{2,1,0:T(4,128)}, u32[]{:S(2)}) %copy-start.2) | copy-done | bytes 524312
  1.2 0.1 shard_map.56
  1.3 2.2 %collective-permute-start.2 = (f32[32,1024]{1,0:T(8,128)S(1)}, f32[32,1024]{1,0:T(8,128)S(1)}, u32[]{:S(2)}, u32[]{:S(2)}) collective-permute-start(f32[32,1024]{1,0:T(8,128)S(1)} %get-tuple-element.22.refs_1_.refs_3_.refs_0_), channel_id=1, source_target_pairs={{0,16},{16,0},{32,48},{48,32},{64,80},{80,64},{96,112},{112,96},{1... | collective-permute-start | bytes 393224 | tf_op jit(solution)/shard_map/ppermute | solution.py:194
  3.5 0.1 collective-permute-start.4
  3.6 0.0 copy-start.3
  3.6 1.0 %copy-done.3 = f32[1,3,1,32,864]{4,3,2,1,0:T(8,128)S(1)} copy-done((f32[1,3,1,32,864]{4,3,2,1,0:T(8,128)S(1)}, f32[1,3,1,32,864]{4,3,2,1,0:T(8,128)}, u32[]{:S(2)}) %copy-start.3) | copy-done | bytes 331800
  4.6 0.0 copy-start.4
  4.6 0.9 %shard_map.55.w_ref = bf16[3,288,384]{2,1,0:T(8,128)(2,1)S(1)} custom-call(f32[3,32,864]{2,1,0:T(8,128)S(1)} %bitcast.9), custom_call_target="tpu_custom_call" | custom-call | bytes 663552 | tf_op jit(solution)/shard_map/pallas_call | solution.py:195
  5.5 1.1 %shard_map.57 = (f32[32,1024]{1,0:T(8,128)S(1)}, f32[32,1024]{1,0:T(8,128)S(1)}) custom-call(bf16[3,288,384]{2,1,0:T(8,128)(2,1)S(1)} %shard_map.55.w_ref, f32[32,1024]{1,0:T(8,128)S(1)} %get-tuple-element.21.refs_0_.refs_2_.refs_3_, f32[32,1024]{1,0:T(8,128)S(1)} %get-tuple-element.22.refs_1_.refs_3_.refs_0_, ...), custom_call_target="tpu_custom_call" | custom-call | flops 452984832 | bytes 786432 | tf_op jit(solution)/shard_map/pallas_call | solution.py:210
  6.7 1.5 %collective-permute-start = (f32[32,1024]{1,0:T(8,128)S(1)}, f32[32,1024]{1,0:T(8,128)S(1)}, u32[]{:S(2)}, u32[]{:S(2)}) collective-permute-start(f32[32,1024]{1,0:T(8,128)S(1)} %get-tuple-element.26.refs_2_.refs_1_), channel_id=1, source_target_pairs={{0,16},{16,0},{32,48},{48,32},{64,80},{80,64},{96,112},{112,96},{1... | collective-permute-start | bytes 393224 | tf_op jit(solution)/shard_map/ppermute | solution.py:223
  8.1 0.0 collective-permute-done.2.refs_5_
  8.1 1.2 %collective-permute-start.3 = (f32[32,1024]{1,0:T(8,128)S(1)}, f32[32,1024]{1,0:T(8,128)S(1)}, u32[]{:S(2)}, u32[]{:S(2)}) collective-permute-start(f32[32,1024]{1,0:T(8,128)S(1)} %collective-permute-done.2.refs_5_), channel_id=1, source_target_pairs={{0,32},{16,112},{32,64},{48,16},{64,96},{80,48},{96,0},{112,80},{1... | collective-permute-start | bytes 393224 | tf_op jit(solution)/shard_map/ppermute | solution.py:225
  9.3 0.0 collective-permute-done.4
  9.3 1.3 %collective-permute-start.5 = (f32[32,1024]{1,0:T(8,128)S(1)}, f32[32,1024]{1,0:T(8,128)S(1)}, u32[]{:S(2)}, u32[]{:S(2)}) collective-permute-start(f32[32,1024]{1,0:T(8,128)S(1)} %collective-permute-done.4), channel_id=1, source_target_pairs={{0,32},{16,112},{32,64},{48,16},{64,96},{80,48},{96,0},{112,80},{1... | collective-permute-start | bytes 393224 | tf_op jit(solution)/shard_map/ppermute | solution.py:225
  10.6 2.6 %collective-permute-start.6 = (f32[32,1024]{1,0:T(8,128)S(1)}, f32[32,1024]{1,0:T(8,128)S(1)}, u32[]{:S(2)}, u32[]{:S(2)}) collective-permute-start(f32[32,1024]{1,0:T(8,128)S(1)} %get-tuple-element.23.refs_3_.refs_2_), channel_id=1, source_target_pairs={{0,16},{16,0},{32,48},{48,32},{64,80},{80,64},{96,112},{112,96},{1... | collective-permute-start | bytes 393224 | tf_op jit(solution)/shard_map/ppermute | solution.py:223
  13.2 0.0 copy-done
  13.2 0.0 copy-done.4
  13.2 0.0 copy-start.1
  13.2 1.6 %copy-done.1 = f32[1,512,1024]{2,1,0:T(8,128)S(1)} copy-done((f32[1,512,1024]{2,1,0:T(8,128)S(1)}, f32[1,512,1024]{2,1,0:T(8,128)}, u32[]{:S(2)}) %copy-start.1) | copy-done | bytes 2097176
  14.8 0.7 %shard_map.58.w_ref = bf16[4096,512]{1,0:T(8,128)(2,1)S(1)} custom-call(f32[1,512]{1,0:T(1,128)S(1)} %copy-done.4, f32[1024,512]{1,0:T(8,128)S(1)} %bitcast.5, f32[512,1024]{1,0:T(8,128)S(1)} %bitcast.6), custom_call_target="tpu_custom_call" | custom-call | bytes 8388608 | tf_op jit(solution)/shard_map/pallas_call | solution.py:227
  15.5 0.0 collective-permute-done.refs_4_
  15.5 0.1 collective-permute-start.1
  15.6 0.0 collective-permute-done.3.refs_0_.refs_1_
  15.6 0.0 collective-permute-done.5.refs_1_.refs_2_
  15.6 1.9 %shard_map.59 = (f32[32,1024]{1,0:T(8,128)S(1)}, f32[32,1024]{1,0:T(8,128)S(1)}, f32[32,1024]{1,0:T(8,128)S(1)}, f32[32,1024]{1,0:T(8,128)S(1)}) custom-call(bf16[3,288,384]{2,1,0:T(8,128)(2,1)S(1)} %shard_map.55.w_ref, f32[32,1024]{1,0:T(8,128)S(1)} %collective-permute-done.3.refs_0_.refs_1_, f32[32,1024]{1,0:T(8,128)S(1)} %collective-permute-done.5.refs_1_.refs_2_, ...), custom_call_target="tpu_custom_call" | custom-call | flops 905969664 | bytes 1310720 | tf_op jit(solution)/shard_map/pallas_call | solution.py:210
  17.5 0.0 collective-permute-done.6.refs_3_
  17.5 3.9 %shard_map.60.refs_8_ = f32[12,32,256]{2,1,0:T(8,128)S(1)} custom-call(bf16[3,288,384]{2,1,0:T(8,128)(2,1)S(1)} %shard_map.55.w_ref, f32[32,1024]{1,0:T(8,128)S(1)} %get-tuple-element.22.refs_1_.refs_3_.refs_0_, f32[32,1024]{1,0:T(8,128)S(1)} %get-tuple-element.26.refs_2_.refs_1_, f32[32,1024]{1,0:T(8,128)S(1)} %get-tuple-element.23.refs_3_.refs_2_, ...), custom_call_target="tpu_custom_call" | custom-call | flops 2038431744 | bytes 1441792 | tf_op jit(solution)/shard_map/pallas_call | solution.py:210
  21.4 0.0 collective-permute-done.1.refs_0_
  21.4 2.0 %shard_map.61 = f32[16,32,256]{2,1,0:T(8,128)S(1)} custom-call(bf16[3,288,384]{2,1,0:T(8,128)(2,1)S(1)} %shard_map.55.w_ref, f32[32,1024]{1,0:T(8,128)S(1)} %collective-permute-done.1.refs_0_, f32[32,1024]{1,0:T(8,128)S(1)} %collective-permute-done.3.refs_0_.refs_1_, f32[32,1024]{1,0:T(8,128)S(1)} %collective-permute-done.5.refs_1_.refs_2_, ...), custom_call_target="tpu_custom_call" | custom-call | flops 679477248 | bytes 1179648 | tf_op jit(solution)/shard_map/pallas_call | solution.py:210
  23.4 22.2 %all_to_all.10 = f32[16,32,256]{2,1,0:T(8,128)S(1)} all-to-all(f32[16,32,256]{2,1,0:T(8,128)S(1)} %shard_map.61), channel_id=1, replica_groups=mesh['depth'=8,'chan'=16] {'chan'}, dimensions={0} | all-to-all | bytes 1048576 | tf_op jit(solution)/shard_map/all_to_all | solution.py:255
  45.6 2.0 %shard_map.62 = f32[512,256]{1,0:T(8,128)S(1)} custom-call(f32[512,256]{1,0:T(8,128)S(1)} %bitcast.7, bf16[4096,512]{1,0:T(8,128)(2,1)S(1)} %shard_map.58.w_ref), custom_call_target="tpu_custom_call" | custom-call | flops 1610612736 | bytes 4194304 | tf_op jit(solution)/shard_map/pallas_call | solution.py:256
  47.6 15.0 %all_to_all.11.in_ref = f32[16,32,256]{2,1,0:T(8,128)S(1)} all-to-all(f32[16,32,256]{2,1,0:T(8,128)S(1)} %bitcast.8), channel_id=1, replica_groups=mesh['depth'=8,'chan'=16] {'chan'}, dimensions={0} | all-to-all | bytes 1048576 | tf_op jit(solution)/shard_map/all_to_all | solution.py:264
  62.5 1.1 %shard_map.63 = f32[32,4,1024]{2,1,0:T(4,128)} custom-call(f32[16,32,256]{2,1,0:T(8,128)S(1)} %all_to_all.11.in_ref), custom_call_target="tpu_custom_call" | custom-call | bytes 1048576 | tf_op jit(solution)/shard_map/pallas_call | solution.py:265
Async XLA Ops:
  0.0 13.2 %copy-start = (f32[1,1024,512]{2,1,0:T(8,128)S(1)}, f32[1,1024,512]{2,1,0:T(8,128)}, u32[]{:S(2)}) copy-start(f32[1,1024,512]{2,1,0:T(8,128)} %param.8) | copy-start | bytes 6291460
  0.0 1.2 %copy-start.2 = (f32[32,4,1024]{2,1,0:T(4,128)S(1)}, f32[32,4,1024]{2,1,0:T(4,128)}, u32[]{:S(2)}) copy-start(f32[32,4,1024]{2,1,0:T(4,128)} %x_ref.1) | copy-start | bytes 1572868
  1.3 6.8 %collective-permute-start.2 = (f32[32,1024]{1,0:T(8,128)S(1)}, f32[32,1024]{1,0:T(8,128)S(1)}, u32[]{:S(2)}, u32[]{:S(2)}) collective-permute-start(f32[32,1024]{1,0:T(8,128)S(1)} %get-tuple-element.22.refs_1_.refs_3_.refs_0_), channel_id=1, source_target_pairs={{0,16},{16,0},{32,48},{48,32},{64,80},{80,64},{96,112},{112,96},{1... | collective-permute-start | bytes 393224 | tf_op jit(solution)/shard_map/ppermute | solution.py:194
  3.5 5.8 %collective-permute-start.4 = (f32[32,1024]{1,0:T(8,128)S(1)}, f32[32,1024]{1,0:T(8,128)S(1)}, u32[]{:S(2)}, u32[]{:S(2)}) collective-permute-start(f32[32,1024]{1,0:T(8,128)S(1)} %get-tuple-element.21.refs_0_.refs_2_.refs_3_), channel_id=1, source_target_pairs={{0,16},{16,0},{32,48},{48,32},{64,80},{80,64},{96,112},{112,96},{1... | collective-permute-start | bytes 393224 | tf_op jit(solution)/shard_map/ppermute | solution.py:194
  3.6 1.0 %copy-start.3 = (f32[1,3,1,32,864]{4,3,2,1,0:T(8,128)S(1)}, f32[1,3,1,32,864]{4,3,2,1,0:T(8,128)}, u32[]{:S(2)}) copy-start(f32[1,3,1,32,864]{4,3,2,1,0:T(8,128)} %param.6) | copy-start | bytes 995332
  4.6 8.6 %copy-start.4 = (f32[1,512]{1,0:T(1,128)S(1)}, f32[1,512]{1,0:T(1,128)}, u32[]{:S(2)}) copy-start(f32[1,512]{1,0:T(1,128)} %gain_ref.1) | copy-start | bytes 6148
  6.7 8.8 %collective-permute-start = (f32[32,1024]{1,0:T(8,128)S(1)}, f32[32,1024]{1,0:T(8,128)S(1)}, u32[]{:S(2)}, u32[]{:S(2)}) collective-permute-start(f32[32,1024]{1,0:T(8,128)S(1)} %get-tuple-element.26.refs_2_.refs_1_), channel_id=1, source_target_pairs={{0,16},{16,0},{32,48},{48,32},{64,80},{80,64},{96,112},{112,96},{1... | collective-permute-start | bytes 393224 | tf_op jit(solution)/shard_map/ppermute | solution.py:223
  8.1 7.5 %collective-permute-start.3 = (f32[32,1024]{1,0:T(8,128)S(1)}, f32[32,1024]{1,0:T(8,128)S(1)}, u32[]{:S(2)}, u32[]{:S(2)}) collective-permute-start(f32[32,1024]{1,0:T(8,128)S(1)} %collective-permute-done.2.refs_5_), channel_id=1, source_target_pairs={{0,32},{16,112},{32,64},{48,16},{64,96},{80,48},{96,0},{112,80},{1... | collective-permute-start | bytes 393224 | tf_op jit(solution)/shard_map/ppermute | solution.py:225
  9.3 6.3 %collective-permute-start.5 = (f32[32,1024]{1,0:T(8,128)S(1)}, f32[32,1024]{1,0:T(8,128)S(1)}, u32[]{:S(2)}, u32[]{:S(2)}) collective-permute-start(f32[32,1024]{1,0:T(8,128)S(1)} %collective-permute-done.4), channel_id=1, source_target_pairs={{0,32},{16,112},{32,64},{48,16},{64,96},{80,48},{96,0},{112,80},{1... | collective-permute-start | bytes 393224 | tf_op jit(solution)/shard_map/ppermute | solution.py:225
  10.6 6.9 %collective-permute-start.6 = (f32[32,1024]{1,0:T(8,128)S(1)}, f32[32,1024]{1,0:T(8,128)S(1)}, u32[]{:S(2)}, u32[]{:S(2)}) collective-permute-start(f32[32,1024]{1,0:T(8,128)S(1)} %get-tuple-element.23.refs_3_.refs_2_), channel_id=1, source_target_pairs={{0,16},{16,0},{32,48},{48,32},{64,80},{80,64},{96,112},{112,96},{1... | collective-permute-start | bytes 393224 | tf_op jit(solution)/shard_map/ppermute | solution.py:223
  13.2 1.6 %copy-start.1 = (f32[1,512,1024]{2,1,0:T(8,128)S(1)}, f32[1,512,1024]{2,1,0:T(8,128)}, u32[]{:S(2)}) copy-start(f32[1,512,1024]{2,1,0:T(8,128)} %param.9) | copy-start | bytes 6291460
  15.5 5.9 %collective-permute-start.1 = (f32[32,1024]{1,0:T(8,128)S(1)}, f32[32,1024]{1,0:T(8,128)S(1)}, u32[]{:S(2)}, u32[]{:S(2)}) collective-permute-start(f32[32,1024]{1,0:T(8,128)S(1)} %collective-permute-done.refs_4_), channel_id=1, source_target_pairs={{0,32},{16,112},{32,64},{48,16},{64,96},{80,48},{96,0},{112,80},{1... | collective-permute-start | bytes 393224 | tf_op jit(solution)/shard_map/ppermute | solution.py:225

commit v3 on v2

--- a/solution.py
+++ b/solution.py
@@ -13,13 +13,14 @@
 VMEM = pl.BlockSpec(memory_space=pltpu.VMEM)
 
 
-def call(body, outs, flops, moved, ins, scratch=()):
+def call(body, outs, flops, moved, ins, scratch=(), aliases=None):
     return pl.pallas_call(
         body,
         out_shape=outs,
         in_specs=ins,
         out_specs=jax.tree.map(lambda _: VMEM, outs),
         scratch_shapes=scratch,
+        input_output_aliases=aliases or {},
         cost_estimate=pl.CostEstimate(flops=flops, bytes_accessed=moved, transcendentals=0),
         compiler_params=pltpu.CompilerParams(vmem_limit_bytes=32 << 20),
     )
@@ -59,11 +60,7 @@
             if shift:
                 pair = pltpu.roll(pair, 256 - shift, 1)
             ahead = pair[:, :128]
-            turned = jnp.where(
-                lane < width,
-                pltpu.roll(ahead, 128 - 2 * width, 1),
-                jnp.where(lane < 2 * width, ahead, pltpu.roll(ahead, 2 * width, 1)),
-            )
+            turned = jnp.where(lane // width == 1, ahead, pltpu.roll(ahead, 2 * width, 1))
             hi, lo = halves(jnp.where(lane < 3 * width, jnp.where(flip, turned, ahead), 0.0))
             rows = pl.ds(tap * width, width)
             w_ref[layer, rows, 0:128] = hi
@@ -71,21 +68,23 @@
             w_ref[layer, rows, 256:384] = lo
 
 
-def mlp_weights_kernel(gain_ref, a_ref, b_ref, w_ref):
+def first_weights_kernel(gain_ref, a_ref, w_ref):
     gain = gain_ref[...]
-    hidden, channels = a_ref.shape
+    hidden = a_ref.shape[0]
     rows = 128
     for r in range(0, hidden, rows):
         hi, lo = halves(a_ref[r : r + rows, :] * gain)
         w_ref[r : r + rows, :] = hi
         w_ref[hidden + r : hidden + r + rows, :] = lo
-    base = 2 * hidden
-    for half in range(hidden // channels):
-        for r in range(0, channels, rows):
-            hi, lo = halves(b_ref[r : r + rows, half * channels : (half + 1) * channels])
-            at = base + half * channels + r
-            w_ref[at : at + rows, :] = hi
-            w_ref[at + hidden : at + hidden + rows, :] = lo
+
+
+def second_weights_kernel(b_ref, w_ref):
+    channels = b_ref.shape[0]
+    rows = 128
+    for r in range(0, channels, rows):
+        hi, lo = halves(b_ref[r : r + rows, :])
+        w_ref[r : r + rows, :] = hi
+        w_ref[channels + r : channels + r + rows, :] = lo
 
 
 def conv_plane(weight, three, acc_ref):
@@ -119,13 +118,11 @@
         out_ref[plane * runs + q] = value[:, q * size : (q + 1) * size]
 
 
-def stage_kernel(given, work, kept, first, w_ref, *refs):
+def stage_kernel(given, work, kept, first, resumes, w_ref, *refs):
     ins, refs = refs[: len(given)], refs[len(given) :]
     acc_ref = refs[-1]
     layers = w_ref.shape[0]
-    ends = any(layer == layers for layer, _ in work)
-    done_ref = refs[0] if len(refs) > len(kept) + ends + 1 else None
-    refs = refs[done_ref is not None :]
+    refs = refs[resumes:]
     where = dict(zip(given, ins, strict=True))
     kept_at = dict(zip(kept, refs[: len(kept)], strict=True))
     held = {key: halves(ref[...]) for key, ref in where.items()}
@@ -138,31 +135,26 @@
         held[layer, place] = halves(total)
         if (layer, place) in kept_at:
             kept_at[layer, place][...] = total
-    if done_ref is not None:
-        out_ref = refs[len(kept)]
-        out_ref[out_ref.shape[0] - done_ref.shape[0] :] = done_ref[...]
-
-
-def mlp_kernel(y_ref, w_ref, out_ref, hh_ref, hl_ref):
+
+
+def mlp_kernel(y_ref, a_ref, b_ref, out_ref, hh_ref, hl_ref):
     channels = y_ref.shape[0]
     hidden = hh_ref.shape[0]
     rows = 256
-    base = 2 * hidden
     y = y_ref[...]
     scale = lax.rsqrt(jnp.mean(y * y, axis=0, keepdims=True) + 1e-06)
     hi, lo = halves(y * scale)
     seen = jnp.concatenate([hi, lo, hi], axis=0)
     for r in range(0, hidden, rows):
-        top, low = w_ref[r : r + rows, :], w_ref[hidden + r : hidden + r + rows, :]
+        top, low = a_ref[r : r + rows, :], a_ref[hidden + r : hidden + r + rows, :]
         hid = gelu(jnp.dot(jnp.concatenate([top, top, low], axis=1), seen, preferred_element_type=F32))
         hh, hl = halves(hid)
         hh_ref[r : r + rows, :] = hh
         hl_ref[r : r + rows, :] = hl
     seen = jnp.concatenate([hh_ref[...], hl_ref[...], hh_ref[...]], axis=0)
     for r in range(0, channels, rows):
-        parts = [w_ref[base + p * channels + r : base + p * channels + r + rows, :] for p in range(2 * hidden // channels)]
-        top = parts[: hidden // channels]
-        part = jnp.concatenate(top + top + parts[hidden // channels :], axis=1)
+        top, low = b_ref[r : r + rows, :], b_ref[channels + r : channels + r + rows, :]
+        part = jnp.concatenate([top, top, low], axis=1)
         out_ref[r : r + rows, :] = y_ref[r : r + rows, :] + jnp.dot(part, seen, preferred_element_type=F32)
 
 
@@ -185,7 +177,6 @@
     layers = kernels.shape[0]
     channels, hidden = mlp_out.shape[1], mlp_out.shape[2]
     size = planes * cells // members
-    runs = cells // size
     plane = jax.ShapeDtypeStruct((width, cells), F32)
 
     pair = [(i, i ^ 1) for i in range(count)]
@@ -202,55 +193,44 @@
     )(kernels)
     held = {(0, 3 + k): v for k, v in enumerate(own)}
 
-    def stage(given, work, kept, finished=None, placed=0, first=0):
+    def stage(given, work, kept, finished=None):
         outs = (plane,) * len(kept)
-        if placed:
-            outs += (jax.ShapeDtypeStruct((placed * runs, width, size), F32),)
+        if any(layer == layers for layer, _ in work):
+            outs += (jax.ShapeDtypeStruct((members, width, size), F32),)
         more = [] if finished is None else [finished]
         got = call(
-            functools.partial(stage_kernel, given, work, kept, first),
+            functools.partial(stage_kernel, given, work, kept, layers, len(more)),
             outs,
             len(work) * 2 * 288 * 384 * cells,
             (len(given) + len(outs)) * width * cells * 4,
             [VMEM] * (1 + len(given) + len(more)),
             [pltpu.VMEM((2, 9 * width, cells), F32)],
+            {1 + len(given): len(kept)} if more else None,
         )(taps, *[held[key] for key in given], *more)
         held.update(zip(kept, got))
         return got[-1]
 
     stage(((0, 3), (0, 4), (0, 5), (0, 6)), ((1, 4), (1, 5)), ((1, 4), (1, 5)))
+    weights = jax.ShapeDtypeStruct((2 * hidden, channels), BF16)
+    w_in = call(first_weights_kernel, weights, 0, mlp_in.size * 8, [VMEM] * 2)(norm_gain, mlp_in[0])
     third, held[1, 4], held[1, 5] = lax.optimization_barrier((own[2], held[1, 4], held[1, 5]))
-    there += [lax.ppermute(q, "depth", pair) for q in (third, own[3])]
+    weights = jax.ShapeDtypeStruct((2 * channels, hidden), BF16)
+    w_out = call(second_weights_kernel, weights, 0, mlp_out.size * 8, [VMEM])(mlp_out[0])
+    fourth, w_out = lax.optimization_barrier((own[3], w_out))
+    there[1], w_in = lax.optimization_barrier((there[1], w_in))
+    there += [lax.ppermute(q, "depth", pair) for q in (third, fourth)]
     for k in range(layers):
         held[0, 2 - k] = lax.ppermute(there[k], "depth", along)
         held[0, 9 - k] = there[k + 1]
-    pieces = call(
-        mlp_weights_kernel,
-        jax.ShapeDtypeStruct((4 * hidden, channels), BF16),
-        0,
-        mlp_in.size * 16,
-        [VMEM] * 3,
-    )(norm_gain, mlp_in[0], mlp_out[0])
-    pieces, held[1, 4] = lax.optimization_barrier((pieces, held[1, 4]))
-    stage(
-        ((0, 1), (0, 2), (0, 3), (0, 4), (1, 4), (1, 5)),
-        ((1, 3), (1, 2), (2, 4), (2, 3)),
-        ((1, 2), (1, 3), (2, 3), (2, 4)),
-    )
+    stage(((0, 2), (0, 3), (0, 4), (1, 4), (1, 5)), ((1, 3), (2, 4)), ((1, 3), (2, 4)))
+    stage(((0, 1), (0, 2), (0, 3), (1, 3), (1, 4)), ((1, 2), (2, 3)), ((1, 2), (2, 3)))
     most = stage(
         ((0, 4), (0, 5), (0, 6), (0, 7), (0, 8), (0, 9), (1, 4), (1, 5), (2, 3), (2, 4)),
         ((1, 6), (1, 7), (1, 8), (2, 5), (2, 6), (2, 7), (3, 4), (3, 5), (3, 6)),
         (),
-        placed=3,
-        first=4,
     )
     mixed = stage(
-        ((0, 0), (0, 1), (0, 2), (0, 3), (1, 2), (1, 3), (2, 3), (2, 4)),
-        ((1, 1), (2, 2), (3, 3)),
-        (),
-        finished=most,
-        placed=4,
-        first=3,
+        ((0, 0), (0, 1), (0, 2), (0, 3), (1, 2), (1, 3), (2, 3), (2, 4)), ((1, 1), (2, 2), (3, 3)), (), most
     )
     here = lax.all_to_all(mixed, "chan", split_axis=0, concat_axis=0, tiled=True)
     out = call(
@@ -258,9 +238,9 @@
         jax.ShapeDtypeStruct((channels, size), F32),
         12 * hidden * channels * size,
         mlp_in.size * 8,
-        [VMEM, VMEM],
+        [VMEM] * 3,
         [pltpu.VMEM((hidden, size), BF16)] * 2,
-    )(here.reshape(channels, size), pieces)
+    )(here.reshape(channels, size), w_in, w_out)
     back = lax.all_to_all(out.reshape(members, width, size), "chan", split_axis=0, concat_axis=0, tiled=True)
     return call(place_kernel, jax.ShapeDtypeStruct(volume.shape, F32), 0, volume.size * 8, [VMEM])(back)
 

time: 63.9 us -> 63.2 us (0.989)
  local copies, waits for them, and re-layouts: 3.77 us -> 2.18 us
  waiting for transfers between devices: 0.05 us -> 1.12 us
  Pallas kernels: 13.7 us -> 14.5 us
    unnamed x10, local copies, waits for them, and re-layouts: 3.77 us -> 2.18 us
    ppermute x3, waiting for transfers between devices: 0.04 us -> 1.11 us  [per_device(): held[0, 2 - k] = lax.ppermute(there[k], 'depth', along)]
    pallas_call x5 -> x7, Pallas kernels: 9.56 us -> 10.4 us  [the longest x5 9.68 us: stage(): call(functools.partial(stage_kernel, given, work, kept, layers, len(more)...]
    all_to_all x1, blocking collectives: 22.2 us -> 21.5 us  [per_device(): lax.all_to_all(mixed, 'chan', split_axis=0, concat_axis=0, tiled=True)]
  transfers between devices with their start and end apart: 7 -> 7, of which waited for: 0 -> 1; matrix products, arithmetic and copies ran while one was open for 0% -> 0% of each run, Pallas kernels for 13% -> 15%
where the time goes in v3:
time: 63.2 us; the launch traced here: 63 us
  blocking collectives  36.5 us (58%)
  Pallas kernels  14.5 us (23%)
  starting transfers between devices  8.55 us (14%)
  local copies, waits for them, and re-layouts  2.18 us (3%)
  waiting for transfers between devices  1.12 us (2%)
    all_to_all x1, blocking collectives, per_device(): lax.all_to_all(mixed, 'chan', split_axis=0, concat_axis=0, tiled=True)  21.5 us
    all_to_all x1, blocking collectives, per_device(): lax.all_to_all(out.reshape(members, width, size), 'chan', split_axis=0, c...  15 us
    pallas_call x5, Pallas kernels, stage(): call(functools.partial(stage_kernel, given, work, kept, layers, len(more)...  9.68 us
    ppermute x2, starting transfers between devices, per_device(): there += [lax.ppermute(q, 'depth', pair) for q in (third, fourth)]  3.76 us
    ppermute x3, starting transfers between devices, per_device(): held[0, 2 - k] = lax.ppermute(there[k], 'depth', along)  2.49 us
    ppermute x2, starting transfers between devices, per_device(): there = [lax.ppermute(q, 'depth', pair) for q in own[:2]]  2.3 us
    unnamed x10, local copies, waits for them, and re-layouts  2.18 us
    pallas_call x1, Pallas kernels, per_device(): call(mlp_kernel, jax.ShapeDtypeStruct((channels, size), F32), 12 * hidden...  2.03 us
  transfers between devices with their start and end apart: 7, of which 1 were waited for; matrix products, arithmetic and copies ran while one was open for 0% of the time, Pallas kernels for 15%

profile of v3, /device:TPU:1, one launch (start us, length us, event | category | flops | bytes accessed | tf_op | source)
XLA Modules:
  0.0 63.0 jit_solution(4814404582208131987)
XLA Ops:
  0.0 0.0 copy-start.1
  0.0 0.0 copy-start.2
  0.0 1.2 %copy-done.2 = f32[32,4,1024]{2,1,0:T(4,128)S(1)} copy-done((f32[32,4,1024]{2,1,0:T(4,128)S(1)}, f32[32,4,1024]{2,1,0:T(4,128)}, u32[]{:S(2)}) %copy-start.2) | copy-done | bytes 524312
  1.2 0.1 shard_map.56
  1.3 2.2 %collective-permute-start.4 = (f32[32,1024]{1,0:T(8,128)S(1)}, f32[32,1024]{1,0:T(8,128)S(1)}, u32[]{:S(2)}, u32[]{:S(2)}) collective-permute-start(f32[32,1024]{1,0:T(8,128)S(1)} %get-tuple-element.23.refs_0_.refs_1_.refs_2_.refs_3_), channel_id=1, source_target_pairs={{0,16},{16,0},{32,48},{48,32},{64,80},{80,64},{96,112},{112,96},{1... | collective-permute-start | bytes 393224 | tf_op jit(solution)/shard_map/ppermute | solution.py:185
  3.5 0.1 collective-permute-start.2
  3.6 0.0 copy-start.3
  3.6 1.0 %copy-done.3 = f32[1,3,1,32,864]{4,3,2,1,0:T(8,128)S(1)} copy-done((f32[1,3,1,32,864]{4,3,2,1,0:T(8,128)S(1)}, f32[1,3,1,32,864]{4,3,2,1,0:T(8,128)}, u32[]{:S(2)}) %copy-start.3) | copy-done | bytes 331800
  4.6 0.0 copy-start.4
  4.6 0.9 %shard_map.55.w_ref = bf16[3,288,384]{2,1,0:T(8,128)(2,1)S(1)} custom-call(f32[3,32,864]{2,1,0:T(8,128)S(1)} %bitcast.9), custom_call_target="tpu_custom_call" | custom-call | bytes 663552 | tf_op jit(solution)/shard_map/pallas_call | solution.py:186
  5.5 1.1 %shard_map.57 = (f32[32,1024]{1,0:T(8,128)S(1)}, f32[32,1024]{1,0:T(8,128)S(1)}) custom-call(bf16[3,288,384]{2,1,0:T(8,128)(2,1)S(1)} %shard_map.55.w_ref, f32[32,1024]{1,0:T(8,128)S(1)} %get-tuple-element.23.refs_0_.refs_1_.refs_2_.refs_3_, f32[32,1024]{1,0:T(8,128)S(1)} %get-tuple-element.24.refs_1_.refs_2_.refs_0_, ...), custom_call_target="tpu_custom_call" | custom-call | flops 452984832 | bytes 786432 | tf_op jit(solution)/shard_map/pallas_call | solution.py:201
  6.7 1.5 %collective-permute-start = (f32[32,1024]{1,0:T(8,128)S(1)}, f32[32,1024]{1,0:T(8,128)S(1)}, u32[]{:S(2)}, u32[]{:S(2)}) collective-permute-start(f32[32,1024]{1,0:T(8,128)S(1)} %get-tuple-element.28.refs_2_.refs_1_), channel_id=1, source_target_pairs={{0,16},{16,0},{32,48},{48,32},{64,80},{80,64},{96,112},{112,96},{1... | collective-permute-start | bytes 393224 | tf_op jit(solution)/shard_map/ppermute | solution.py:221
  8.1 0.0 collective-permute-done.4
  8.1 1.2 %collective-permute-start.5 = (f32[32,1024]{1,0:T(8,128)S(1)}, f32[32,1024]{1,0:T(8,128)S(1)}, u32[]{:S(2)}, u32[]{:S(2)}) collective-permute-start(f32[32,1024]{1,0:T(8,128)S(1)} %collective-permute-done.4), channel_id=1, source_target_pairs={{0,32},{16,112},{32,64},{48,16},{64,96},{80,48},{96,0},{112,80},{1... | collective-permute-start | bytes 393224 | tf_op jit(solution)/shard_map/ppermute | solution.py:223
  9.3 0.0 copy-done.1
  9.3 0.0 copy-done.4
  9.3 0.0 copy-start
  9.3 0.3 shard_map.58.a_ref
  9.7 0.0 collective-permute-done.2.refs_5_
  9.7 1.3 %collective-permute-start.3 = (f32[32,1024]{1,0:T(8,128)S(1)}, f32[32,1024]{1,0:T(8,128)S(1)}, u32[]{:S(2)}, u32[]{:S(2)}) collective-permute-start(f32[32,1024]{1,0:T(8,128)S(1)} %collective-permute-done.2.refs_5_), channel_id=1, source_target_pairs={{0,32},{16,112},{32,64},{48,16},{64,96},{80,48},{96,0},{112,80},{1... | collective-permute-start | bytes 393224 | tf_op jit(solution)/shard_map/ppermute | solution.py:223
  11.0 0.0 copy-done
  11.0 0.4 shard_map.61.b_ref
  11.3 2.3 %collective-permute-start.6 = (f32[32,1024]{1,0:T(8,128)S(1)}, f32[32,1024]{1,0:T(8,128)S(1)}, u32[]{:S(2)}, u32[]{:S(2)}) collective-permute-start(f32[32,1024]{1,0:T(8,128)S(1)} %get-tuple-element.36.refs_3_.refs_2_), channel_id=1, source_target_pairs={{0,16},{16,0},{32,48},{48,32},{64,80},{80,64},{96,112},{112,96},{1... | collective-permute-start | bytes 393224 | tf_op jit(solution)/shard_map/ppermute | solution.py:221
  13.7 0.0 collective-permute-done.refs_4_
  13.7 0.0 collective-permute-start.1
  13.7 0.0 collective-permute-done.5.refs_0_.refs_1_.refs_2_
  13.7 1.4 %shard_map.59 = (f32[32,1024]{1,0:T(8,128)S(1)}, f32[32,1024]{1,0:T(8,128)S(1)}) custom-call(bf16[3,288,384]{2,1,0:T(8,128)(2,1)S(1)} %shard_map.55.w_ref, f32[32,1024]{1,0:T(8,128)S(1)} %collective-permute-done.5.refs_0_.refs_1_.refs_2_, f32[32,1024]{1,0:T(8,128)S(1)} %get-tuple-element.23.refs_0_.refs_1_.refs_2_.refs_3_, ...), custom_call_target="tpu_custom_call" | custom-call | flops 452984832 | bytes 917504 | tf_op jit(solution)/shard_map/pallas_call | solution.py:201
  15.0 1.1 %collective-permute-done.3.refs_0_.refs_1_ = f32[32,1024]{1,0:T(8,128)S(1)} collective-permute-done((f32[32,1024]{1,0:T(8,128)S(1)}, f32[32,1024]{1,0:T(8,128)S(1)}, u32[]{:S(2)}, u32[]{:S(2)}) %collective-permute-start.3) | collective-permute-done | bytes 131104 | tf_op jit(solution)/shard_map/ppermute | solution.py:223
  16.1 1.4 %shard_map.60 = (f32[32,1024]{1,0:T(8,128)S(1)}, f32[32,1024]{1,0:T(8,128)S(1)}) custom-call(bf16[3,288,384]{2,1,0:T(8,128)(2,1)S(1)} %shard_map.55.w_ref, f32[32,1024]{1,0:T(8,128)S(1)} %collective-permute-done.3.refs_0_.refs_1_, f32[32,1024]{1,0:T(8,128)S(1)} %collective-permute-done.5.refs_0_.refs_1_.refs_2_, ...), custom_call_target="tpu_custom_call" | custom-call | flops 452984832 | bytes 917504 | tf_op jit(solution)/shard_map/pallas_call | solution.py:201
  17.5 0.0 collective-permute-done.6.refs_3_
  17.5 3.8 %shard_map.62.refs_8_ = f32[16,32,256]{2,1,0:T(8,128)S(1)} custom-call(bf16[3,288,384]{2,1,0:T(8,128)(2,1)S(1)} %shard_map.55.w_ref, f32[32,1024]{1,0:T(8,128)S(1)} %get-tuple-element.24.refs_1_.refs_2_.refs_0_, f32[32,1024]{1,0:T(8,128)S(1)} %get-tuple-element.28.refs_2_.refs_1_, f32[32,1024]{1,0:T(8,128)S(1)} %get-tuple-element.36.refs_3_.refs_2_, ...), custom_call_target="tpu_custom_call" | custom-call | flops 2038431744 | bytes 1441792 | tf_op jit(solution)/shard_map/pallas_call | solution.py:201
  21.4 0.0 collective-permute-done.1.refs_0_
  21.4 2.0 %shard_map.63 = f32[16,32,256]{2,1,0:T(8,128)S(1)} custom-call(bf16[3,288,384]{2,1,0:T(8,128)(2,1)S(1)} %shard_map.55.w_ref, f32[32,1024]{1,0:T(8,128)S(1)} %collective-permute-done.1.refs_0_, f32[32,1024]{1,0:T(8,128)S(1)} %collective-permute-done.3.refs_0_.refs_1_, ...), custom_call_target="tpu_custom_call", output_to_operand_aliasing={{}: (9, {})} | custom-call | flops 679477248 | bytes 1179648 | tf_op jit(solution)/shard_map/pallas_call | solution.py:201
  23.4 21.5 %all_to_all.10 = f32[16,32,256]{2,1,0:T(8,128)S(1)} all-to-all(f32[16,32,256]{2,1,0:T(8,128)S(1)} %shard_map.63), channel_id=1, replica_groups=mesh['depth'=8,'chan'=16] {'chan'}, dimensions={0} | all-to-all | bytes 1048576 | tf_op jit(solution)/shard_map/all_to_all | solution.py:235
  44.9 2.0 %shard_map.64 = f32[512,256]{1,0:T(8,128)S(1)} custom-call(f32[512,256]{1,0:T(8,128)S(1)} %bitcast.7, bf16[2048,512]{1,0:T(8,128)(2,1)S(1)} %shard_map.58.a_ref, bf16[1024,1024]{1,0:T(8,128)(2,1)S(1)} %shard_map.61.b_ref), custom_call_target="tpu_custom_call" | custom-call | flops 1610612736 | bytes 4194304 | tf_op jit(solution)/shard_map/pallas_call | solution.py:236
  46.9 15.0 %all_to_all.11.in_ref = f32[16,32,256]{2,1,0:T(8,128)S(1)} all-to-all(f32[16,32,256]{2,1,0:T(8,128)S(1)} %bitcast.8), channel_id=1, replica_groups=mesh['depth'=8,'chan'=16] {'chan'}, dimensions={0} | all-to-all | bytes 1048576 | tf_op jit(solution)/shard_map/all_to_all | solution.py:244
  61.9 1.1 %shard_map.65 = f32[32,4,1024]{2,1,0:T(4,128)} custom-call(f32[16,32,256]{2,1,0:T(8,128)S(1)} %all_to_all.11.in_ref), custom_call_target="tpu_custom_call" | custom-call | bytes 1048576 | tf_op jit(solution)/shard_map/pallas_call | solution.py:245
Async XLA Ops:
  0.0 9.3 %copy-start.1 = (f32[1,1024,512]{2,1,0:T(8,128)S(1)}, f32[1,1024,512]{2,1,0:T(8,128)}, u32[]{:S(2)}) copy-start(f32[1,1024,512]{2,1,0:T(8,128)} %param.8) | copy-start | bytes 6291460
  0.0 1.2 %copy-start.2 = (f32[32,4,1024]{2,1,0:T(4,128)S(1)}, f32[32,4,1024]{2,1,0:T(4,128)}, u32[]{:S(2)}) copy-start(f32[32,4,1024]{2,1,0:T(4,128)} %x_ref.1) | copy-start | bytes 1572868
  1.3 6.8 %collective-permute-start.4 = (f32[32,1024]{1,0:T(8,128)S(1)}, f32[32,1024]{1,0:T(8,128)S(1)}, u32[]{:S(2)}, u32[]{:S(2)}) collective-permute-start(f32[32,1024]{1,0:T(8,128)S(1)} %get-tuple-element.23.refs_0_.refs_1_.refs_2_.refs_3_), channel_id=1, source_target_pairs={{0,16},{16,0},{32,48},{48,32},{64,80},{80,64},{96,112},{112,96},{1... | collective-permute-start | bytes 393224 | tf_op jit(solution)/shard_map/ppermute | solution.py:185
  3.5 6.1 %collective-permute-start.2 = (f32[32,1024]{1,0:T(8,128)S(1)}, f32[32,1024]{1,0:T(8,128)S(1)}, u32[]{:S(2)}, u32[]{:S(2)}) collective-permute-start(f32[32,1024]{1,0:T(8,128)S(1)} %get-tuple-element.24.refs_1_.refs_2_.refs_0_), channel_id=1, source_target_pairs={{0,16},{16,0},{32,48},{48,32},{64,80},{80,64},{96,112},{112,96},{1... | collective-permute-start | bytes 393224 | tf_op jit(solution)/shard_map/ppermute | solution.py:185
  3.6 1.0 %copy-start.3 = (f32[1,3,1,32,864]{4,3,2,1,0:T(8,128)S(1)}, f32[1,3,1,32,864]{4,3,2,1,0:T(8,128)}, u32[]{:S(2)}) copy-start(f32[1,3,1,32,864]{4,3,2,1,0:T(8,128)} %param.6) | copy-start | bytes 995332
  4.6 4.7 %copy-start.4 = (f32[1,512]{1,0:T(1,128)S(1)}, f32[1,512]{1,0:T(1,128)}, u32[]{:S(2)}) copy-start(f32[1,512]{1,0:T(1,128)} %gain_ref.1) | copy-start | bytes 6148
  6.7 7.0 %collective-permute-start = (f32[32,1024]{1,0:T(8,128)S(1)}, f32[32,1024]{1,0:T(8,128)S(1)}, u32[]{:S(2)}, u32[]{:S(2)}) collective-permute-start(f32[32,1024]{1,0:T(8,128)S(1)} %get-tuple-element.28.refs_2_.refs_1_), channel_id=1, source_target_pairs={{0,16},{16,0},{32,48},{48,32},{64,80},{80,64},{96,112},{112,96},{1... | collective-permute-start | bytes 393224 | tf_op jit(solution)/shard_map/ppermute | solution.py:221
  8.1 5.6 %collective-permute-start.5 = (f32[32,1024]{1,0:T(8,128)S(1)}, f32[32,1024]{1,0:T(8,128)S(1)}, u32[]{:S(2)}, u32[]{:S(2)}) collective-permute-start(f32[32,1024]{1,0:T(8,128)S(1)} %collective-permute-done.4), channel_id=1, source_target_pairs={{0,32},{16,112},{32,64},{48,16},{64,96},{80,48},{96,0},{112,80},{1... | collective-permute-start | bytes 393224 | tf_op jit(solution)/shard_map/ppermute | solution.py:223
  9.3 1.6 %copy-start = (f32[1,512,1024]{2,1,0:T(8,128)S(1)}, f32[1,512,1024]{2,1,0:T(8,128)}, u32[]{:S(2)}) copy-start(f32[1,512,1024]{2,1,0:T(8,128)} %param.9) | copy-start | bytes 6291460
  9.7 6.5 %collective-permute-start.3 = (f32[32,1024]{1,0:T(8,128)S(1)}, f32[32,1024]{1,0:T(8,128)S(1)}, u32[]{:S(2)}, u32[]{:S(2)}) collective-permute-start(f32[32,1024]{1,0:T(8,128)S(1)} %collective-permute-done.2.refs_5_), channel_id=1, source_target_pairs={{0,32},{16,112},{32,64},{48,16},{64,96},{80,48},{96,0},{112,80},{1... | collective-permute-start | bytes 393224 | tf_op jit(solution)/shard_map/ppermute | solution.py:223
  11.3 6.2 %collective-permute-start.6 = (f32[32,1024]{1,0:T(8,128)S(1)}, f32[32,1024]{1,0:T(8,128)S(1)}, u32[]{:S(2)}, u32[]{:S(2)}) collective-permute-start(f32[32,1024]{1,0:T(8,128)S(1)} %get-tuple-element.36.refs_3_.refs_2_), channel_id=1, source_target_pairs={{0,16},{16,0},{32,48},{48,32},{64,80},{80,64},{96,112},{112,96},{1... | collective-permute-start | bytes 393224 | tf_op jit(solution)/shard_map/ppermute | solution.py:221
  13.7 7.7 %collective-permute-start.1 = (f32[32,1024]{1,0:T(8,128)S(1)}, f32[32,1024]{1,0:T(8,128)S(1)}, u32[]{:S(2)}, u32[]{:S(2)}) collective-permute-start(f32[32,1024]{1,0:T(8,128)S(1)} %collective-permute-done.refs_4_), channel_id=1, source_target_pairs={{0,32},{16,112},{32,64},{48,16},{64,96},{80,48},{96,0},{112,80},{1... | collective-permute-start | bytes 393224 | tf_op jit(solution)/shard_map/ppermute | solution.py:223

commit v4 on v3

--- a/solution.py
+++ b/solution.py
@@ -39,11 +39,35 @@
     return lax.axis_index("depth") % 2 > 0
 
 
-def planes_kernel(x_ref, *q_refs):
-    last = len(q_refs) - 1
+def rearranged(pieces, back):
+    block = lax.broadcasted_iota(jnp.int32, pieces[0].shape, 1) // W
+    count = len(pieces)
+    runs = 128 // W
+    moved = []
+    for v in range(count):
+        total = None
+        for b in range(runs):
+            if back:
+                row = v * runs + b
+                source, at = row % count, row // count
+            else:
+                row = b * count + v
+                source, at = row // runs, row % runs
+            piece = pieces[source]
+            if at != b:
+                piece = pltpu.roll(piece, (b - at) * W % 128, 1)
+            total = piece if total is None else jnp.where(block == b, piece, total)
+        moved.append(total)
+    return moved
+
+
+def planes_kernel(places, x_ref, *q_refs):
+    last = x_ref.shape[1] - 1
     flip = turned_here()
-    for k, q_ref in enumerate(q_refs):
-        q_ref[...] = jnp.where(flip, x_ref[:, last - k, :], x_ref[:, k, :])
+    for k, q_ref in zip(places, q_refs, strict=True):
+        plane = jnp.where(flip, x_ref[:, last - k, :], x_ref[:, k, :])
+        pieces = [plane[:, v : v + 128] for v in range(0, plane.shape[1], 128)]
+        q_ref[...] = jnp.concatenate(rearranged(pieces, False), axis=1)
 
 
 def taps_kernel(k_ref, w_ref, pad_ref):
@@ -92,19 +116,21 @@
     his = [t[0] for t in three] + [zero]
     los = [t[1] for t in three] + [zero]
     acc_ref[...] = jnp.dot(weight, jnp.concatenate(his + los + his, axis=0), preferred_element_type=F32)
-    width = zero.shape[0]
-    cells = zero.shape[1]
-
-    def tap(b, c):
-        return acc_ref[(b * 3 + c) * width : (b * 3 + c + 1) * width, :]
+    width, cells = zero.shape
+    count = cells // 128
+
+    def tap(b, c, v):
+        return acc_ref[(b * 3 + c) * width : (b * 3 + c + 1) * width, v * 128 : (v + 1) * 128]
+
+    def rows(c, v):
+        above = tap(0, c, v - 1) if v else pltpu.roll(tap(0, c, count - 1), W, 1)
+        below = tap(2, c, v + 1) if v < count - 1 else pltpu.roll(tap(2, c, 0), 128 - W, 1)
+        return tap(1, c, v) + above + below
 
     column = lax.broadcasted_iota(jnp.int32, (width, 128), 1) % W
-    sums = [
-        tap(1, c) + pltpu.roll(tap(0, c), W, 1) + pltpu.roll(tap(2, c), cells - W, 1) for c in range(3)
-    ]
     parts = []
-    for v in range(0, cells, 128):
-        left, here, right = (s[:, v : v + 128] for s in sums)
+    for v in range(count):
+        left, here, right = (rows(c, v) for c in range(3))
         left = jnp.where(column == 0, pltpu.roll(left, 128 - W + 1, 1), pltpu.roll(left, 1, 1))
         right = jnp.where(column == W - 1, pltpu.roll(right, W - 1, 1), pltpu.roll(right, 127, 1))
         parts.append(left + here + right)
@@ -164,10 +190,11 @@
     last = out_ref.shape[1] - 1
     flip = turned_here()
     for p in range(last + 1):
-        for q in range(runs):
-            out_ref[:, p, q * size : (q + 1) * size] = jnp.where(
-                flip, in_ref[(last - p) * runs + q], in_ref[p * runs + q]
-            )
+        start = jnp.where(flip, last - p, p) * runs
+        pieces = [in_ref[start + q, :, v : v + 128] for q in range(runs) for v in range(0, size, 128)]
+        for v, piece in enumerate(rearranged(pieces, True)):
+            out_ref[:, p, v * 128 : (v + 1) * 128] = piece
+
 
 def per_device(volume, conv_weight, norm_gain, mlp_in, mlp_out):
     width, planes, cells = volume.shape
@@ -181,7 +208,10 @@
 
     pair = [(i, i ^ 1) for i in range(count)]
     along = [(i, (i + (2 if i % 2 == 0 else count - 2)) % count) for i in range(count)]
-    own = call(planes_kernel, (plane,) * planes, 0, volume.size * 8, [VMEM])(volume)
+    own = []
+    for places in ((0,), tuple(range(1, planes))):
+        body = functools.partial(planes_kernel, places)
+        own += call(body, (plane,) * len(places), 0, len(places) * width * cells * 8, [VMEM])(volume)
     there = [lax.ppermute(q, "depth", pair) for q in own[:2]]
     taps = call(
         taps_kernel,
@@ -223,14 +253,16 @@
         held[0, 2 - k] = lax.ppermute(there[k], "depth", along)
         held[0, 9 - k] = there[k + 1]
     stage(((0, 2), (0, 3), (0, 4), (1, 4), (1, 5)), ((1, 3), (2, 4)), ((1, 3), (2, 4)))
-    stage(((0, 1), (0, 2), (0, 3), (1, 3), (1, 4)), ((1, 2), (2, 3)), ((1, 2), (2, 3)))
     most = stage(
-        ((0, 4), (0, 5), (0, 6), (0, 7), (0, 8), (0, 9), (1, 4), (1, 5), (2, 3), (2, 4)),
-        ((1, 6), (1, 7), (1, 8), (2, 5), (2, 6), (2, 7), (3, 4), (3, 5), (3, 6)),
+        ((0, 5), (0, 6), (0, 7), (0, 8), (0, 9), (1, 4), (1, 5), (2, 4)),
+        ((1, 6), (1, 7), (1, 8), (2, 5), (2, 6), (2, 7), (3, 5), (3, 6)),
+        ((2, 5),),
+    )
+    mixed = stage(
+        ((0, 0), (0, 1), (0, 2), (0, 3), (0, 4), (1, 3), (1, 4), (2, 4), (2, 5)),
+        ((1, 2), (1, 1), (2, 3), (2, 2), (3, 4), (3, 3)),
         (),
-    )
-    mixed = stage(
-        ((0, 0), (0, 1), (0, 2), (0, 3), (1, 2), (1, 3), (2, 3), (2, 4)), ((1, 1), (2, 2), (3, 3)), (), most
+        most,
     )
     here = lax.all_to_all(mixed, "chan", split_axis=0, concat_axis=0, tiled=True)
     out = call(

time: 63.2 us -> 61.8 us (0.978)
  Pallas kernels: 14.5 us -> 12.8 us
  blocking collectives: 36.5 us -> 37.5 us
    pallas_call x5 -> x4, Pallas kernels: 9.68 us -> 7.12 us  [stage(): call(functools.partial(stage_kernel, given, work, kept, layers, len(more)...]
    all_to_all x1, blocking collectives: 21.5 us -> 22.5 us  [per_device(): lax.all_to_all(mixed, 'chan', split_axis=0, concat_axis=0, tiled=True)]
    ppermute x2, starting transfers between devices: 3.76 us -> 3.04 us  [per_device(): there += [lax.ppermute(q, 'depth', pair) for q in (third, fourth)]]
  transfers between devices with their start and end apart: 7 -> 7, of which waited for: 1 -> 1; matrix products, arithmetic and copies ran while one was open for 0% -> 0% of each run, Pallas kernels for 15% -> 11%
where the time goes in v4:
time: 61.8 us; the launch traced here: 61.5 us
  blocking collectives  37.5 us (61%)
  Pallas kernels  12.8 us (21%)
  starting transfers between devices  8.44 us (14%)
  local copies, waits for them, and re-layouts  2.02 us (3%)
    all_to_all x1, blocking collectives, per_device(): lax.all_to_all(mixed, 'chan', split_axis=0, concat_axis=0, tiled=True)  22.5 us
    all_to_all x1, blocking collectives, per_device(): lax.all_to_all(out.reshape(members, width, size), 'chan', split_axis=0, c...  15 us
    pallas_call x4, Pallas kernels, stage(): call(functools.partial(stage_kernel, given, work, kept, layers, len(more)...  7.12 us
    ppermute x3, starting transfers between devices, per_device(): held[0, 2 - k] = lax.ppermute(there[k], 'depth', along)  3.1 us
    ppermute x2, starting transfers between devices, per_device(): there += [lax.ppermute(q, 'depth', pair) for q in (third, fourth)]  3.04 us
    ppermute x2, starting transfers between devices, per_device(): there = [lax.ppermute(q, 'depth', pair) for q in own[:2]]  2.3 us
    unnamed x10, local copies, waits for them, and re-layouts  2.02 us
    pallas_call x1, Pallas kernels, per_device(): call(mlp_kernel, jax.ShapeDtypeStruct((channels, size), F32), 12 * hidden...  1.99 us
  transfers between devices with their start and end apart: 7, of which 1 were waited for; matrix products, arithmetic and copies ran while one was open for 0% of the time, Pallas kernels for 11%

profile of v4, /device:TPU:1, one launch (start us, length us, event | category | flops | bytes accessed | tf_op | source)
XLA Modules:
  0.0 61.5 jit_solution(8371225324944054746)
XLA Ops:
  0.0 0.0 copy-start
  0.0 1.0 %copy-done = f32[32,4,1024]{2,1,0:T(4,128)S(1)} copy-done((f32[32,4,1024]{2,1,0:T(4,128)S(1)}, f32[32,4,1024]{2,1,0:T(4,128)}, u32[]{:S(2)}) %copy-start) | copy-done | bytes 524312
  1.0 0.0 copy-start.1
  1.0 0.2 shard_map.57.refs_0_.refs_1_.refs_3_
  1.2 2.2 %collective-permute-start.4 = (f32[32,1024]{1,0:T(8,128)S(1)}, f32[32,1024]{1,0:T(8,128)S(1)}, u32[]{:S(2)}, u32[]{:S(2)}) collective-permute-start(f32[32,1024]{1,0:T(8,128)S(1)} %shard_map.57.refs_0_.refs_1_.refs_3_), channel_id=1, source_target_pairs={{0,16},{16,0},{32,48},{48,32},{64,80},{80,64},{96,112},{112,96},{1... | collective-permute-start | bytes 393224 | tf_op jit(solution)/shard_map/ppermute | solution.py:215
  3.4 0.4 shard_map.56
  3.9 0.1 collective-permute-start.2
  3.9 0.0 copy-start.3
  4.0 1.0 %copy-done.3 = f32[1,3,1,32,864]{4,3,2,1,0:T(8,128)S(1)} copy-done((f32[1,3,1,32,864]{4,3,2,1,0:T(8,128)S(1)}, f32[1,3,1,32,864]{4,3,2,1,0:T(8,128)}, u32[]{:S(2)}) %copy-start.3) | copy-done | bytes 331800
  4.9 0.9 %shard_map.55.w_ref = bf16[3,288,384]{2,1,0:T(8,128)(2,1)S(1)} custom-call(f32[3,32,864]{2,1,0:T(8,128)S(1)} %bitcast.9), custom_call_target="tpu_custom_call" | custom-call | bytes 663552 | tf_op jit(solution)/shard_map/pallas_call | solution.py:216
  5.9 0.9 %shard_map.58 = (f32[32,1024]{1,0:T(8,128)S(1)}, f32[32,1024]{1,0:T(8,128)S(1)}) custom-call(bf16[3,288,384]{2,1,0:T(8,128)(2,1)S(1)} %shard_map.55.w_ref, f32[32,1024]{1,0:T(8,128)S(1)} %shard_map.57.refs_0_.refs_1_.refs_3_, f32[32,1024]{1,0:T(8,128)S(1)} %get-tuple-element.22.refs_1_.refs_2_.refs_4_, f32[32,1024]{1,0:T(8,128)S(1)} %get-tuple-element.26.refs_2_.refs_0_, ...), custom_call_target="tpu_custom_call" | custom-call | flops 452984832 | bytes 786432 | tf_op jit(solution)/shard_map/pallas_call | solution.py:231
  6.8 1.5 %collective-permute-start = (f32[32,1024]{1,0:T(8,128)S(1)}, f32[32,1024]{1,0:T(8,128)S(1)}, u32[]{:S(2)}, u32[]{:S(2)}) collective-permute-start(f32[32,1024]{1,0:T(8,128)S(1)} %get-tuple-element.26.refs_2_.refs_0_), channel_id=1, source_target_pairs={{0,16},{16,0},{32,48},{48,32},{64,80},{80,64},{96,112},{112,96},{1... | collective-permute-start | bytes 393224 | tf_op jit(solution)/shard_map/ppermute | solution.py:251
  8.3 0.0 collective-permute-done.4
  8.3 1.2 %collective-permute-start.5 = (f32[32,1024]{1,0:T(8,128)S(1)}, f32[32,1024]{1,0:T(8,128)S(1)}, u32[]{:S(2)}, u32[]{:S(2)}) collective-permute-start(f32[32,1024]{1,0:T(8,128)S(1)} %collective-permute-done.4), channel_id=1, source_target_pairs={{0,32},{16,112},{32,64},{48,16},{64,96},{80,48},{96,0},{112,80},{1... | collective-permute-start | bytes 393224 | tf_op jit(solution)/shard_map/ppermute | solution.py:253
  9.5 0.0 copy-done.1
  9.5 0.0 copy-start.2
  9.5 0.0 copy-start.4
  9.6 0.4 shard_map.61.b_ref
  9.9 1.5 %collective-permute-start.6 = (f32[32,1024]{1,0:T(8,128)S(1)}, f32[32,1024]{1,0:T(8,128)S(1)}, u32[]{:S(2)}, u32[]{:S(2)}) collective-permute-start(f32[32,1024]{1,0:T(8,128)S(1)} %get-tuple-element.32.refs_3_.refs_1_), channel_id=1, source_target_pairs={{0,16},{16,0},{32,48},{48,32},{64,80},{80,64},{96,112},{112,96},{1... | collective-permute-start | bytes 393224 | tf_op jit(solution)/shard_map/ppermute | solution.py:251
  11.4 0.0 copy-done.2
  11.4 0.0 copy-done.4
  11.5 0.3 shard_map.59.a_ref
  11.8 0.0 collective-permute-done.2.refs_4_
  11.8 1.0 %collective-permute-start.3 = (f32[32,1024]{1,0:T(8,128)S(1)}, f32[32,1024]{1,0:T(8,128)S(1)}, u32[]{:S(2)}, u32[]{:S(2)}) collective-permute-start(f32[32,1024]{1,0:T(8,128)S(1)} %collective-permute-done.2.refs_4_), channel_id=1, source_target_pairs={{0,32},{16,112},{32,64},{48,16},{64,96},{80,48},{96,0},{112,80},{1... | collective-permute-start | bytes 393224 | tf_op jit(solution)/shard_map/ppermute | solution.py:253
  12.8 0.0 collective-permute-done.refs_3_
  12.8 0.9 %collective-permute-start.1 = (f32[32,1024]{1,0:T(8,128)S(1)}, f32[32,1024]{1,0:T(8,128)S(1)}, u32[]{:S(2)}, u32[]{:S(2)}) collective-permute-start(f32[32,1024]{1,0:T(8,128)S(1)} %collective-permute-done.refs_3_), channel_id=1, source_target_pairs={{0,32},{16,112},{32,64},{48,16},{64,96},{80,48},{96,0},{112,80},{1... | collective-permute-start | bytes 393224 | tf_op jit(solution)/shard_map/ppermute | solution.py:253
  13.7 0.0 collective-permute-done.5.refs_0_.refs_2_
  13.7 1.2 %shard_map.60 = (f32[32,1024]{1,0:T(8,128)S(1)}, f32[32,1024]{1,0:T(8,128)S(1)}) custom-call(bf16[3,288,384]{2,1,0:T(8,128)(2,1)S(1)} %shard_map.55.w_ref, f32[32,1024]{1,0:T(8,128)S(1)} %collective-permute-done.5.refs_0_.refs_2_, f32[32,1024]{1,0:T(8,128)S(1)} %shard_map.57.refs_0_.refs_1_.refs_3_, ...), custom_call_target="tpu_custom_call" | custom-call | flops 452984832 | bytes 917504 | tf_op jit(solution)/shard_map/pallas_call | solution.py:231
  14.9 0.0 collective-permute-done.6.refs_2_
  14.9 2.8 %shard_map.62 = (f32[32,1024]{1,0:T(8,128)S(1)}, f32[16,32,256]{2,1,0:T(8,128)S(1)}) custom-call(bf16[3,288,384]{2,1,0:T(8,128)(2,1)S(1)} %shard_map.55.w_ref, f32[32,1024]{1,0:T(8,128)S(1)} %get-tuple-element.26.refs_2_.refs_0_, f32[32,1024]{1,0:T(8,128)S(1)} %get-tuple-element.32.refs_3_.refs_1_, f32[32,1024]{1,0:T(8,128)S(1)} %collective-permute-done.6.refs_2_, ...), custom_call_target="tpu_custom_call" | custom-call | flops 1811939328 | bytes 1310720 | tf_op jit(solution)/shard_map/pallas_call | solution.py:231
  17.7 0.6 collective-permute-done.1.refs_0_
  18.3 0.0 collective-permute-done.3.refs_1_
  18.3 2.2 %shard_map.63 = f32[16,32,256]{2,1,0:T(8,128)S(1)} custom-call(bf16[3,288,384]{2,1,0:T(8,128)(2,1)S(1)} %shard_map.55.w_ref, f32[32,1024]{1,0:T(8,128)S(1)} %collective-permute-done.1.refs_0_, f32[32,1024]{1,0:T(8,128)S(1)} %collective-permute-done.3.refs_1_, f32[32,1024]{1,0:T(8,128)S(1)} %collective-permute-done.5.refs_0_.refs_2_, ...), custom_call_target="tpu_custom_call", output_to_operand_aliasing={{}: (10, {})} | custom-call | flops 1358954496 | bytes 1310720 | tf_op jit(solution)/shard_map/pallas_call | solution.py:231
  20.5 22.5 %all_to_all.10 = f32[16,32,256]{2,1,0:T(8,128)S(1)} all-to-all(f32[16,32,256]{2,1,0:T(8,128)S(1)} %shard_map.63), channel_id=1, replica_groups=mesh['depth'=8,'chan'=16] {'chan'}, dimensions={0} | all-to-all | bytes 1048576 | tf_op jit(solution)/shard_map/all_to_all | solution.py:267
  43.0 2.0 %shard_map.64 = f32[512,256]{1,0:T(8,128)S(1)} custom-call(f32[512,256]{1,0:T(8,128)S(1)} %bitcast.7, bf16[2048,512]{1,0:T(8,128)(2,1)S(1)} %shard_map.59.a_ref, bf16[1024,1024]{1,0:T(8,128)(2,1)S(1)} %shard_map.61.b_ref), custom_call_target="tpu_custom_call" | custom-call | flops 1610612736 | bytes 4194304 | tf_op jit(solution)/shard_map/pallas_call | solution.py:268
  45.0 15.0 %all_to_all.11.in_ref = f32[16,32,256]{2,1,0:T(8,128)S(1)} all-to-all(f32[16,32,256]{2,1,0:T(8,128)S(1)} %bitcast.8), channel_id=1, replica_groups=mesh['depth'=8,'chan'=16] {'chan'}, dimensions={0} | all-to-all | bytes 1048576 | tf_op jit(solution)/shard_map/all_to_all | solution.py:276
  60.0 1.5 %shard_map.65 = f32[32,4,1024]{2,1,0:T(4,128)} custom-call(f32[16,32,256]{2,1,0:T(8,128)S(1)} %all_to_all.11.in_ref), custom_call_target="tpu_custom_call" | custom-call | bytes 1048576 | tf_op jit(solution)/shard_map/pallas_call | solution.py:277
Async XLA Ops:
  0.0 1.0 %copy-start = (f32[32,4,1024]{2,1,0:T(4,128)S(1)}, f32[32,4,1024]{2,1,0:T(4,128)}, u32[]{:S(2)}) copy-start(f32[32,4,1024]{2,1,0:T(4,128)} %x_ref.3) | copy-start | bytes 1572868
  1.0 8.5 %copy-start.1 = (f32[1,512,1024]{2,1,0:T(8,128)S(1)}, f32[1,512,1024]{2,1,0:T(8,128)}, u32[]{:S(2)}) copy-start(f32[1,512,1024]{2,1,0:T(8,128)} %param.9) | copy-start | bytes 6291460
  1.2 7.1 %collective-permute-start.4 = (f32[32,1024]{1,0:T(8,128)S(1)}, f32[32,1024]{1,0:T(8,128)S(1)}, u32[]{:S(2)}, u32[]{:S(2)}) collective-permute-start(f32[32,1024]{1,0:T(8,128)S(1)} %shard_map.57.refs_0_.refs_1_.refs_3_), channel_id=1, source_target_pairs={{0,16},{16,0},{32,48},{48,32},{64,80},{80,64},{96,112},{112,96},{1... | collective-permute-start | bytes 393224 | tf_op jit(solution)/shard_map/ppermute | solution.py:215
  3.9 7.9 %collective-permute-start.2 = (f32[32,1024]{1,0:T(8,128)S(1)}, f32[32,1024]{1,0:T(8,128)S(1)}, u32[]{:S(2)}, u32[]{:S(2)}) collective-permute-start(f32[32,1024]{1,0:T(8,128)S(1)} %get-tuple-element.22.refs_1_.refs_2_.refs_4_), channel_id=1, source_target_pairs={{0,16},{16,0},{32,48},{48,32},{64,80},{80,64},{96,112},{112,96},{1... | collective-permute-start | bytes 393224 | tf_op jit(solution)/shard_map/ppermute | solution.py:215
  3.9 1.0 %copy-start.3 = (f32[1,3,1,32,864]{4,3,2,1,0:T(8,128)S(1)}, f32[1,3,1,32,864]{4,3,2,1,0:T(8,128)}, u32[]{:S(2)}) copy-start(f32[1,3,1,32,864]{4,3,2,1,0:T(8,128)} %param.6) | copy-start | bytes 995332
  6.8 6.0 %collective-permute-start = (f32[32,1024]{1,0:T(8,128)S(1)}, f32[32,1024]{1,0:T(8,128)S(1)}, u32[]{:S(2)}, u32[]{:S(2)}) collective-permute-start(f32[32,1024]{1,0:T(8,128)S(1)} %get-tuple-element.26.refs_2_.refs_0_), channel_id=1, source_target_pairs={{0,16},{16,0},{32,48},{48,32},{64,80},{80,64},{96,112},{112,96},{1... | collective-permute-start | bytes 393224 | tf_op jit(solution)/shard_map/ppermute | solution.py:251
  8.3 5.4 %collective-permute-start.5 = (f32[32,1024]{1,0:T(8,128)S(1)}, f32[32,1024]{1,0:T(8,128)S(1)}, u32[]{:S(2)}, u32[]{:S(2)}) collective-permute-start(f32[32,1024]{1,0:T(8,128)S(1)} %collective-permute-done.4), channel_id=1, source_target_pairs={{0,32},{16,112},{32,64},{48,16},{64,96},{80,48},{96,0},{112,80},{1... | collective-permute-start | bytes 393224 | tf_op jit(solution)/shard_map/ppermute | solution.py:253
  9.5 1.9 %copy-start.2 = (f32[1,1024,512]{2,1,0:T(8,128)S(1)}, f32[1,1024,512]{2,1,0:T(8,128)}, u32[]{:S(2)}) copy-start(f32[1,1024,512]{2,1,0:T(8,128)} %param.8) | copy-start | bytes 6291460
  9.5 1.9 %copy-start.4 = (f32[1,512]{1,0:T(1,128)S(1)}, f32[1,512]{1,0:T(1,128)}, u32[]{:S(2)}) copy-start(f32[1,512]{1,0:T(1,128)} %gain_ref.1) | copy-start | bytes 6148
  9.9 5.0 %collective-permute-start.6 = (f32[32,1024]{1,0:T(8,128)S(1)}, f32[32,1024]{1,0:T(8,128)S(1)}, u32[]{:S(2)}, u32[]{:S(2)}) collective-permute-start(f32[32,1024]{1,0:T(8,128)S(1)} %get-tuple-element.32.refs_3_.refs_1_), channel_id=1, source_target_pairs={{0,16},{16,0},{32,48},{48,32},{64,80},{80,64},{96,112},{112,96},{1... | collective-permute-start | bytes 393224 | tf_op jit(solution)/shard_map/ppermute | solution.py:251
  11.8 6.5 %collective-permute-start.3 = (f32[32,1024]{1,0:T(8,128)S(1)}, f32[32,1024]{1,0:T(8,128)S(1)}, u32[]{:S(2)}, u32[]{:S(2)}) collective-permute-start(f32[32,1024]{1,0:T(8,128)S(1)} %collective-permute-done.2.refs_4_), channel_id=1, source_target_pairs={{0,32},{16,112},{32,64},{48,16},{64,96},{80,48},{96,0},{112,80},{1... | collective-permute-start | bytes 393224 | tf_op jit(solution)/shard_map/ppermute | solution.py:253
  12.8 5.5 %collective-permute-start.1 = (f32[32,1024]{1,0:T(8,128)S(1)}, f32[32,1024]{1,0:T(8,128)S(1)}, u32[]{:S(2)}, u32[]{:S(2)}) collective-permute-start(f32[32,1024]{1,0:T(8,128)S(1)} %collective-permute-done.refs_3_), channel_id=1, source_target_pairs={{0,32},{16,112},{32,64},{48,16},{64,96},{80,48},{96,0},{112,80},{1... | collective-permute-start | bytes 393224 | tf_op jit(solution)/shard_map/ppermute | solution.py:253

commit v5 on v4

--- a/solution.py
+++ b/solution.py
@@ -8,17 +8,19 @@
 from jax.sharding import PartitionSpec as P
 
 W = 32
+PARTS = 4
 F32 = jnp.float32
 BF16 = jnp.bfloat16
 VMEM = pl.BlockSpec(memory_space=pltpu.VMEM)
-
-
-def call(body, outs, flops, moved, ins, scratch=(), aliases=None):
+HBM = pl.BlockSpec(memory_space=pltpu.HBM)
+
+
+def call(body, outs, flops, moved, ins, scratch=(), aliases=None, outs_in=VMEM):
     return pl.pallas_call(
         body,
         out_shape=outs,
         in_specs=ins,
-        out_specs=jax.tree.map(lambda _: VMEM, outs),
+        out_specs=jax.tree.map(lambda _: outs_in, outs),
         scratch_shapes=scratch,
         input_output_aliases=aliases or {},
         cost_estimate=pl.CostEstimate(flops=flops, bytes_accessed=moved, transcendentals=0),
@@ -184,16 +186,25 @@
         out_ref[r : r + rows, :] = y_ref[r : r + rows, :] + jnp.dot(part, seen, preferred_element_type=F32)
 
 
-def place_kernel(in_ref, out_ref):
+def place_kernel(in_ref, out_hbm, held_ref, sems):
     size = in_ref.shape[2]
-    runs = out_ref.shape[2] // size
-    last = out_ref.shape[1] - 1
+    width, planes, cells = out_hbm.shape
+    runs = cells // size
     flip = turned_here()
-    for p in range(last + 1):
-        start = jnp.where(flip, last - p, p) * runs
-        pieces = [in_ref[start + q, :, v : v + 128] for q in range(runs) for v in range(0, size, 128)]
-        for v, piece in enumerate(rearranged(pieces, True)):
-            out_ref[:, p, v * 128 : (v + 1) * 128] = piece
+    rows = width // sems.shape[0]
+    copies = []
+    for n in range(width // rows):
+        part = slice(n * rows, (n + 1) * rows)
+        for p in range(planes):
+            start = jnp.where(flip, planes - 1 - p, p) * runs
+            pieces = [in_ref[start + q, part, v : v + 128] for q in range(runs) for v in range(0, size, 128)]
+            for v, piece in enumerate(rearranged(pieces, True)):
+                held_ref[part, p, v * 128 : (v + 1) * 128] = piece
+        part = pl.ds(n * rows, rows)
+        copies.append(pltpu.make_async_copy(held_ref.at[part], out_hbm.at[part], sems.at[n]))
+        copies[-1].start()
+    for copy in copies:
+        copy.wait()
 
 
 def per_device(volume, conv_weight, norm_gain, mlp_in, mlp_out):
@@ -211,7 +222,7 @@
     own = []
     for places in ((0,), tuple(range(1, planes))):
         body = functools.partial(planes_kernel, places)
-        own += call(body, (plane,) * len(places), 0, len(places) * width * cells * 8, [VMEM])(volume)
+        own += call(body, (plane,) * len(places), 10**9, len(places) * width * cells * 8, [VMEM])(volume)
     there = [lax.ppermute(q, "depth", pair) for q in own[:2]]
     taps = call(
         taps_kernel,
@@ -274,7 +285,15 @@
         [pltpu.VMEM((hidden, size), BF16)] * 2,
     )(here.reshape(channels, size), w_in, w_out)
     back = lax.all_to_all(out.reshape(members, width, size), "chan", split_axis=0, concat_axis=0, tiled=True)
-    return call(place_kernel, jax.ShapeDtypeStruct(volume.shape, F32), 0, volume.size * 8, [VMEM])(back)
+    return call(
+        place_kernel,
+        jax.ShapeDtypeStruct(volume.shape, F32),
+        0,
+        volume.size * 8,
+        [VMEM],
+        [pltpu.VMEM(volume.shape, F32), pltpu.SemaphoreType.DMA((PARTS,))],
+        outs_in=HBM,
+    )(back)
 
 
 def solution(mesh):

time: 61.8 us -> 61.4 us (level)
  local copies, waits for them, and re-layouts: 2.02 us -> 1.06 us
    unnamed x10, local copies, waits for them, and re-layouts: 2.02 us -> 1.06 us
  transfers between devices with their start and end apart: 7 -> 7, of which waited for: 1 -> 2; matrix products, arithmetic and copies ran while one was open for 0% -> 0% of each run, Pallas kernels for 11% -> 11%
where the time goes in v5:
time: 61.4 us; the launch traced here: 61.1 us
  blocking collectives  38.1 us (62%)
  Pallas kernels  12.5 us (20%)
  starting transfers between devices  8.72 us (14%)
  local copies, waits for them, and re-layouts  1.06 us (2%)
    all_to_all x1, blocking collectives, per_device(): lax.all_to_all(mixed, 'chan', split_axis=0, concat_axis=0, tiled=True)  23.2 us
    all_to_all x1, blocking collectives, per_device(): lax.all_to_all(out.reshape(members, width, size), 'chan', split_axis=0, c...  15 us
    pallas_call x4, Pallas kernels, stage(): call(functools.partial(stage_kernel, given, work, kept, layers, len(more)...  7.12 us
    ppermute x2, starting transfers between devices, per_device(): there += [lax.ppermute(q, 'depth', pair) for q in (third, fourth)]  3.32 us
    ppermute x3, starting transfers between devices, per_device(): held[0, 2 - k] = lax.ppermute(there[k], 'depth', along)  3.1 us
    ppermute x2, starting transfers between devices, per_device(): there = [lax.ppermute(q, 'depth', pair) for q in own[:2]]  2.3 us
    pallas_call x1, Pallas kernels, per_device(): call(mlp_kernel, jax.ShapeDtypeStruct((channels, size), F32), 12 * hidden...  1.99 us
  transfers between devices with their start and end apart: 7, of which 2 were waited for; matrix products, arithmetic and copies ran while one was open for 0% of the time, Pallas kernels for 11%

profile of v5, /device:TPU:1, one launch (start us, length us, event | category | flops | bytes accessed | tf_op | source)
XLA Modules:
  0.0 61.1 jit_solution(13701707865648965605)
XLA Ops:
  0.0 0.0 copy-start.4
  0.0 1.0 %copy-done.4 = f32[32,4,1024]{2,1,0:T(4,128)S(1)} copy-done((f32[32,4,1024]{2,1,0:T(4,128)S(1)}, f32[32,4,1024]{2,1,0:T(4,128)}, u32[]{:S(2)}) %copy-start.4) | copy-done | bytes 524312
  1.0 0.2 shard_map.57.refs_0_.refs_1_.refs_3_
  1.2 0.0 copy-start.2
  1.3 2.2 %collective-permute-start.4 = (f32[32,1024]{1,0:T(8,128)S(1)}, f32[32,1024]{1,0:T(8,128)S(1)}, u32[]{:S(2)}, u32[]{:S(2)}) collective-permute-start(f32[32,1024]{1,0:T(8,128)S(1)} %shard_map.57.refs_0_.refs_1_.refs_3_), channel_id=1, source_target_pairs={{0,16},{16,0},{32,48},{48,32},{64,80},{80,64},{96,112},{112,96},{1... | collective-permute-start | bytes 393224 | tf_op jit(solution)/shard_map/ppermute | solution.py:226
  3.5 0.4 shard_map.56
  3.9 0.0 copy-start
  3.9 0.1 collective-permute-start.2
  4.0 0.0 copy-done.2
  4.0 0.9 %shard_map.55.w_ref = bf16[3,288,384]{2,1,0:T(8,128)(2,1)S(1)} custom-call(f32[3,32,864]{2,1,0:T(8,128)S(1)} %bitcast.9), custom_call_target="tpu_custom_call" | custom-call | bytes 663552 | tf_op jit(solution)/shard_map/pallas_call | solution.py:227
  4.9 0.9 %shard_map.58 = (f32[32,1024]{1,0:T(8,128)S(1)}, f32[32,1024]{1,0:T(8,128)S(1)}) custom-call(bf16[3,288,384]{2,1,0:T(8,128)(2,1)S(1)} %shard_map.55.w_ref, f32[32,1024]{1,0:T(8,128)S(1)} %shard_map.57.refs_0_.refs_1_.refs_3_, f32[32,1024]{1,0:T(8,128)S(1)} %get-tuple-element.22.refs_1_.refs_2_.refs_4_, f32[32,1024]{1,0:T(8,128)S(1)} %get-tuple-element.26.refs_2_.refs_0_, ...), custom_call_target="tpu_custom_call" | custom-call | flops 452984832 | bytes 786432 | tf_op jit(solution)/shard_map/pallas_call | solution.py:242
  5.8 1.5 %collective-permute-start = (f32[32,1024]{1,0:T(8,128)S(1)}, f32[32,1024]{1,0:T(8,128)S(1)}, u32[]{:S(2)}, u32[]{:S(2)}) collective-permute-start(f32[32,1024]{1,0:T(8,128)S(1)} %get-tuple-element.26.refs_2_.refs_0_), channel_id=1, source_target_pairs={{0,16},{16,0},{32,48},{48,32},{64,80},{80,64},{96,112},{112,96},{1... | collective-permute-start | bytes 393224 | tf_op jit(solution)/shard_map/ppermute | solution.py:262
  7.4 0.0 collective-permute-done.4
  7.4 1.2 %collective-permute-start.5 = (f32[32,1024]{1,0:T(8,128)S(1)}, f32[32,1024]{1,0:T(8,128)S(1)}, u32[]{:S(2)}, u32[]{:S(2)}) collective-permute-start(f32[32,1024]{1,0:T(8,128)S(1)} %collective-permute-done.4), channel_id=1, source_target_pairs={{0,32},{16,112},{32,64},{48,16},{64,96},{80,48},{96,0},{112,80},{1... | collective-permute-start | bytes 393224 | tf_op jit(solution)/shard_map/ppermute | solution.py:264
  8.6 0.0 copy-done
  8.6 0.0 copy-start.1
  8.6 0.0 copy-start.3
  8.6 0.4 shard_map.61.b_ref
  9.0 1.8 %collective-permute-start.6 = (f32[32,1024]{1,0:T(8,128)S(1)}, f32[32,1024]{1,0:T(8,128)S(1)}, u32[]{:S(2)}, u32[]{:S(2)}) collective-permute-start(f32[32,1024]{1,0:T(8,128)S(1)} %get-tuple-element.32.refs_3_.refs_1_), channel_id=1, source_target_pairs={{0,16},{16,0},{32,48},{48,32},{64,80},{80,64},{96,112},{112,96},{1... | collective-permute-start | bytes 393224 | tf_op jit(solution)/shard_map/ppermute | solution.py:262
  10.8 0.0 copy-done.1
  10.8 0.0 copy-done.3
  10.8 0.3 shard_map.59.a_ref
  11.1 0.0 collective-permute-done.2.refs_4_
  11.1 0.7 %collective-permute-start.3 = (f32[32,1024]{1,0:T(8,128)S(1)}, f32[32,1024]{1,0:T(8,128)S(1)}, u32[]{:S(2)}, u32[]{:S(2)}) collective-permute-start(f32[32,1024]{1,0:T(8,128)S(1)} %collective-permute-done.2.refs_4_), channel_id=1, source_target_pairs={{0,32},{16,112},{32,64},{48,16},{64,96},{80,48},{96,0},{112,80},{1... | collective-permute-start | bytes 393224 | tf_op jit(solution)/shard_map/ppermute | solution.py:264
  11.8 0.4 collective-permute-done.refs_3_
  12.2 1.2 %collective-permute-start.1 = (f32[32,1024]{1,0:T(8,128)S(1)}, f32[32,1024]{1,0:T(8,128)S(1)}, u32[]{:S(2)}, u32[]{:S(2)}) collective-permute-start(f32[32,1024]{1,0:T(8,128)S(1)} %collective-permute-done.refs_3_), channel_id=1, source_target_pairs={{0,32},{16,112},{32,64},{48,16},{64,96},{80,48},{96,0},{112,80},{1... | collective-permute-start | bytes 393224 | tf_op jit(solution)/shard_map/ppermute | solution.py:264
  13.4 0.0 collective-permute-done.5.refs_0_.refs_2_
  13.4 1.2 %shard_map.60 = (f32[32,1024]{1,0:T(8,128)S(1)}, f32[32,1024]{1,0:T(8,128)S(1)}) custom-call(bf16[3,288,384]{2,1,0:T(8,128)(2,1)S(1)} %shard_map.55.w_ref, f32[32,1024]{1,0:T(8,128)S(1)} %collective-permute-done.5.refs_0_.refs_2_, f32[32,1024]{1,0:T(8,128)S(1)} %shard_map.57.refs_0_.refs_1_.refs_3_, ...), custom_call_target="tpu_custom_call" | custom-call | flops 452984832 | bytes 917504 | tf_op jit(solution)/shard_map/pallas_call | solution.py:242
  14.7 0.0 collective-permute-done.6.refs_2_
  14.7 2.8 %shard_map.62 = (f32[32,1024]{1,0:T(8,128)S(1)}, f32[16,32,256]{2,1,0:T(8,128)S(1)}) custom-call(bf16[3,288,384]{2,1,0:T(8,128)(2,1)S(1)} %shard_map.55.w_ref, f32[32,1024]{1,0:T(8,128)S(1)} %get-tuple-element.26.refs_2_.refs_0_, f32[32,1024]{1,0:T(8,128)S(1)} %get-tuple-element.32.refs_3_.refs_1_, f32[32,1024]{1,0:T(8,128)S(1)} %collective-permute-done.6.refs_2_, ...), custom_call_target="tpu_custom_call" | custom-call | flops 1811939328 | bytes 1310720 | tf_op jit(solution)/shard_map/pallas_call | solution.py:242
  17.5 0.1 collective-permute-done.1.refs_0_
  17.6 0.0 collective-permute-done.3.refs_1_
  17.6 2.2 %shard_map.63 = f32[16,32,256]{2,1,0:T(8,128)S(1)} custom-call(bf16[3,288,384]{2,1,0:T(8,128)(2,1)S(1)} %shard_map.55.w_ref, f32[32,1024]{1,0:T(8,128)S(1)} %collective-permute-done.1.refs_0_, f32[32,1024]{1,0:T(8,128)S(1)} %collective-permute-done.3.refs_1_, f32[32,1024]{1,0:T(8,128)S(1)} %collective-permute-done.5.refs_0_.refs_2_, ...), custom_call_target="tpu_custom_call", output_to_operand_aliasing={{}: (10, {})} | custom-call | flops 1358954496 | bytes 1310720 | tf_op jit(solution)/shard_map/pallas_call | solution.py:242
  19.8 23.2 %all_to_all.10 = f32[16,32,256]{2,1,0:T(8,128)S(1)} all-to-all(f32[16,32,256]{2,1,0:T(8,128)S(1)} %shard_map.63), channel_id=1, replica_groups=mesh['depth'=8,'chan'=16] {'chan'}, dimensions={0} | all-to-all | bytes 1048576 | tf_op jit(solution)/shard_map/all_to_all | solution.py:278
  43.0 2.0 %shard_map.64 = f32[512,256]{1,0:T(8,128)S(1)} custom-call(f32[512,256]{1,0:T(8,128)S(1)} %bitcast.7, bf16[2048,512]{1,0:T(8,128)(2,1)S(1)} %shard_map.59.a_ref, bf16[1024,1024]{1,0:T(8,128)(2,1)S(1)} %shard_map.61.b_ref), custom_call_target="tpu_custom_call" | custom-call | flops 1610612736 | bytes 4194304 | tf_op jit(solution)/shard_map/pallas_call | solution.py:279
  45.0 15.0 %all_to_all.11.in_ref = f32[16,32,256]{2,1,0:T(8,128)S(1)} all-to-all(f32[16,32,256]{2,1,0:T(8,128)S(1)} %bitcast.8), channel_id=1, replica_groups=mesh['depth'=8,'chan'=16] {'chan'}, dimensions={0} | all-to-all | bytes 1048576 | tf_op jit(solution)/shard_map/all_to_all | solution.py:287
  60.0 1.2 %shard_map.65 = f32[32,4,1024]{2,1,0:T(4,128)} custom-call(f32[16,32,256]{2,1,0:T(8,128)S(1)} %all_to_all.11.in_ref), custom_call_target="tpu_custom_call" | custom-call | bytes 1048576 | tf_op jit(solution)/shard_map/pallas_call | solution.py:288
Async XLA Ops:
  0.0 1.0 %copy-start.4 = (f32[32,4,1024]{2,1,0:T(4,128)S(1)}, f32[32,4,1024]{2,1,0:T(4,128)}, u32[]{:S(2)}) copy-start(f32[32,4,1024]{2,1,0:T(4,128)} %x_ref.3) | copy-start | bytes 1572868
  1.2 2.7 %copy-start.2 = (f32[1,3,1,32,864]{4,3,2,1,0:T(8,128)S(1)}, f32[1,3,1,32,864]{4,3,2,1,0:T(8,128)}, u32[]{:S(2)}) copy-start(f32[1,3,1,32,864]{4,3,2,1,0:T(8,128)} %param.6) | copy-start | bytes 995332
  1.3 6.1 %collective-permute-start.4 = (f32[32,1024]{1,0:T(8,128)S(1)}, f32[32,1024]{1,0:T(8,128)S(1)}, u32[]{:S(2)}, u32[]{:S(2)}) collective-permute-start(f32[32,1024]{1,0:T(8,128)S(1)} %shard_map.57.refs_0_.refs_1_.refs_3_), channel_id=1, source_target_pairs={{0,16},{16,0},{32,48},{48,32},{64,80},{80,64},{96,112},{112,96},{1... | collective-permute-start | bytes 393224 | tf_op jit(solution)/shard_map/ppermute | solution.py:226
  3.9 4.7 %copy-start = (f32[1,512,1024]{2,1,0:T(8,128)S(1)}, f32[1,512,1024]{2,1,0:T(8,128)}, u32[]{:S(2)}) copy-start(f32[1,512,1024]{2,1,0:T(8,128)} %param.9) | copy-start | bytes 6291460
  3.9 7.2 %collective-permute-start.2 = (f32[32,1024]{1,0:T(8,128)S(1)}, f32[32,1024]{1,0:T(8,128)S(1)}, u32[]{:S(2)}, u32[]{:S(2)}) collective-permute-start(f32[32,1024]{1,0:T(8,128)S(1)} %get-tuple-element.22.refs_1_.refs_2_.refs_4_), channel_id=1, source_target_pairs={{0,16},{16,0},{32,48},{48,32},{64,80},{80,64},{96,112},{112,96},{1... | collective-permute-start | bytes 393224 | tf_op jit(solution)/shard_map/ppermute | solution.py:226
  5.8 6.4 %collective-permute-start = (f32[32,1024]{1,0:T(8,128)S(1)}, f32[32,1024]{1,0:T(8,128)S(1)}, u32[]{:S(2)}, u32[]{:S(2)}) collective-permute-start(f32[32,1024]{1,0:T(8,128)S(1)} %get-tuple-element.26.refs_2_.refs_0_), channel_id=1, source_target_pairs={{0,16},{16,0},{32,48},{48,32},{64,80},{80,64},{96,112},{112,96},{1... | collective-permute-start | bytes 393224 | tf_op jit(solution)/shard_map/ppermute | solution.py:262
  7.4 6.1 %collective-permute-start.5 = (f32[32,1024]{1,0:T(8,128)S(1)}, f32[32,1024]{1,0:T(8,128)S(1)}, u32[]{:S(2)}, u32[]{:S(2)}) collective-permute-start(f32[32,1024]{1,0:T(8,128)S(1)} %collective-permute-done.4), channel_id=1, source_target_pairs={{0,32},{16,112},{32,64},{48,16},{64,96},{80,48},{96,0},{112,80},{1... | collective-permute-start | bytes 393224 | tf_op jit(solution)/shard_map/ppermute | solution.py:264
  8.6 2.2 %copy-start.1 = (f32[1,1024,512]{2,1,0:T(8,128)S(1)}, f32[1,1024,512]{2,1,0:T(8,128)}, u32[]{:S(2)}) copy-start(f32[1,1024,512]{2,1,0:T(8,128)} %param.8) | copy-start | bytes 6291460
  8.6 2.2 %copy-start.3 = (f32[1,512]{1,0:T(1,128)S(1)}, f32[1,512]{1,0:T(1,128)}, u32[]{:S(2)}) copy-start(f32[1,512]{1,0:T(1,128)} %gain_ref.1) | copy-start | bytes 6148
  9.0 5.7 %collective-permute-start.6 = (f32[32,1024]{1,0:T(8,128)S(1)}, f32[32,1024]{1,0:T(8,128)S(1)}, u32[]{:S(2)}, u32[]{:S(2)}) collective-permute-start(f32[32,1024]{1,0:T(8,128)S(1)} %get-tuple-element.32.refs_3_.refs_1_), channel_id=1, source_target_pairs={{0,16},{16,0},{32,48},{48,32},{64,80},{80,64},{96,112},{112,96},{1... | collective-permute-start | bytes 393224 | tf_op jit(solution)/shard_map/ppermute | solution.py:262
  11.1 6.5 %collective-permute-start.3 = (f32[32,1024]{1,0:T(8,128)S(1)}, f32[32,1024]{1,0:T(8,128)S(1)}, u32[]{:S(2)}, u32[]{:S(2)}) collective-permute-start(f32[32,1024]{1,0:T(8,128)S(1)} %collective-permute-done.2.refs_4_), channel_id=1, source_target_pairs={{0,32},{16,112},{32,64},{48,16},{64,96},{80,48},{96,0},{112,80},{1... | collective-permute-start | bytes 393224 | tf_op jit(solution)/shard_map/ppermute | solution.py:264
  12.2 5.4 %collective-permute-start.1 = (f32[32,1024]{1,0:T(8,128)S(1)}, f32[32,1024]{1,0:T(8,128)S(1)}, u32[]{:S(2)}, u32[]{:S(2)}) collective-permute-start(f32[32,1024]{1,0:T(8,128)S(1)} %collective-permute-done.refs_3_), channel_id=1, source_target_pairs={{0,32},{16,112},{32,64},{48,16},{64,96},{80,48},{96,0},{112,80},{1... | collective-permute-start | bytes 393224 | tf_op jit(solution)/shard_map/ppermute | solution.py:264

commit v6 on v5

--- a/solution.py
+++ b/solution.py
@@ -63,12 +63,18 @@
     return moved
 
 
-def planes_kernel(places, x_ref, *q_refs):
-    last = x_ref.shape[1] - 1
+def planes_kernel(places, x_hbm, *refs):
+    q_refs, (held_ref, sems) = refs[:-2], refs[-2:]
+    last = x_hbm.shape[1] - 1
     flip = turned_here()
-    for k, q_ref in zip(places, q_refs, strict=True):
-        plane = jnp.where(flip, x_ref[:, last - k, :], x_ref[:, k, :])
-        pieces = [plane[:, v : v + 128] for v in range(0, plane.shape[1], 128)]
+    copies = []
+    for n, k in enumerate(places):
+        place = jnp.where(flip, last - k, k)
+        copies.append(pltpu.make_async_copy(x_hbm.at[:, place, :], held_ref.at[n], sems.at[n]))
+        copies[-1].start()
+    for n, q_ref in enumerate(q_refs):
+        copies[n].wait()
+        pieces = [held_ref[n, :, v : v + 128] for v in range(0, q_ref.shape[1], 128)]
         q_ref[...] = jnp.concatenate(rearranged(pieces, False), axis=1)
 
 
@@ -222,7 +228,14 @@
     own = []
     for places in ((0,), tuple(range(1, planes))):
         body = functools.partial(planes_kernel, places)
-        own += call(body, (plane,) * len(places), 10**9, len(places) * width * cells * 8, [VMEM])(volume)
+        own += call(
+            body,
+            (plane,) * len(places),
+            10**9,
+            len(places) * width * cells * 8,
+            [HBM],
+            [pltpu.VMEM((len(places), width, cells), F32), pltpu.SemaphoreType.DMA((len(places),))],
+        )(pltpu.with_memory_space_constraint(volume, pltpu.HBM))
     there = [lax.ppermute(q, "depth", pair) for q in own[:2]]
     taps = call(
         taps_kernel,

time: 61.4 us -> 61.4 us (level)
  Pallas kernels: 12.5 us -> 14.5 us
  local copies, waits for them, and re-layouts: 1.06 us -> 0.02 us
    pallas_call x2, Pallas kernels: 0.58 us -> 2.58 us  [per_device(): call(body, (plane,) * len(places), 10 ** 9, len(places) * width * cells *...]
    unnamed x10 -> x8, local copies, waits for them, and re-layouts: 1.06 us -> 0.02 us
  transfers between devices with their start and end apart: 7 -> 7, of which waited for: 2 -> 1; matrix products, arithmetic and copies ran while one was open for 0% -> 0% of each run, Pallas kernels for 11% -> 13%
where the time goes in v6:
time: 61.4 us; the launch traced here: 61.2 us
  blocking collectives  37.5 us (61%)
  Pallas kernels  14.5 us (24%)
  starting transfers between devices  8.44 us (14%)
    all_to_all x1, blocking collectives, per_device(): lax.all_to_all(mixed, 'chan', split_axis=0, concat_axis=0, tiled=True)  22.5 us
    all_to_all x1, blocking collectives, per_device(): lax.all_to_all(out.reshape(members, width, size), 'chan', split_axis=0, c...  15 us
    pallas_call x4, Pallas kernels, stage(): call(functools.partial(stage_kernel, given, work, kept, layers, len(more)...  7.13 us
    ppermute x3, starting transfers between devices, per_device(): held[0, 2 - k] = lax.ppermute(there[k], 'depth', along)  3.1 us
    ppermute x2, starting transfers between devices, per_device(): there += [lax.ppermute(q, 'depth', pair) for q in (third, fourth)]  3.02 us
    pallas_call x2, Pallas kernels, per_device(): call(body, (plane,) * len(places), 10 ** 9, len(places) * width * cells *...  2.58 us
    ppermute x2, starting transfers between devices, per_device(): there = [lax.ppermute(q, 'depth', pair) for q in own[:2]]  2.32 us
    pallas_call x1, Pallas kernels, per_device(): call(mlp_kernel, jax.ShapeDtypeStruct((channels, size), F32), 12 * hidden...  1.99 us
  transfers between devices with their start and end apart: 7, of which 1 were waited for; matrix products, arithmetic and copies ran while one was open for 0% of the time, Pallas kernels for 13%

profile of v6, /device:TPU:1, one launch (start us, length us, event | category | flops | bytes accessed | tf_op | source)
XLA Modules:
  0.0 61.2 jit_solution(1200348278338964605)
XLA Ops:
  0.0 1.1 %shard_map.57.refs_0_.refs_1_.refs_3_ = f32[32,1024]{1,0:T(8,128)S(1)} custom-call(f32[32,4,1024]{2,1,0:T(4,128)} %x_hbm.3), custom_call_target="tpu_custom_call" | custom-call | flops 1000000000 | bytes 262144 | tf_op jit(solution)/shard_map/pallas_call | solution.py:231
  1.1 0.0 copy-start.2
  1.1 2.2 %collective-permute-start.4 = (f32[32,1024]{1,0:T(8,128)S(1)}, f32[32,1024]{1,0:T(8,128)S(1)}, u32[]{:S(2)}, u32[]{:S(2)}) collective-permute-start(f32[32,1024]{1,0:T(8,128)S(1)} %shard_map.57.refs_0_.refs_1_.refs_3_), channel_id=1, source_target_pairs={{0,16},{16,0},{32,48},{48,32},{64,80},{80,64},{96,112},{112,96},{1... | collective-permute-start | bytes 393224 | tf_op jit(solution)/shard_map/ppermute | solution.py:239
  3.3 1.5 %shard_map.56 = (f32[32,1024]{1,0:T(8,128)S(1)}, f32[32,1024]{1,0:T(8,128)S(1)}, f32[32,1024]{1,0:T(8,128)S(1)}) custom-call(f32[32,4,1024]{2,1,0:T(4,128)} %x_hbm.3), custom_call_target="tpu_custom_call" | custom-call | flops 1000000000 | bytes 786432 | tf_op jit(solution)/shard_map/pallas_call | solution.py:231
  4.8 0.0 copy-start
  4.8 0.1 collective-permute-start.2
  4.9 0.0 copy-done.2
  4.9 0.9 %shard_map.55.w_ref = bf16[3,288,384]{2,1,0:T(8,128)(2,1)S(1)} custom-call(f32[3,32,864]{2,1,0:T(8,128)S(1)} %bitcast.9), custom_call_target="tpu_custom_call" | custom-call | bytes 663552 | tf_op jit(solution)/shard_map/pallas_call | solution.py:240
  5.9 0.9 %shard_map.58 = (f32[32,1024]{1,0:T(8,128)S(1)}, f32[32,1024]{1,0:T(8,128)S(1)}) custom-call(bf16[3,288,384]{2,1,0:T(8,128)(2,1)S(1)} %shard_map.55.w_ref, f32[32,1024]{1,0:T(8,128)S(1)} %shard_map.57.refs_0_.refs_1_.refs_3_, f32[32,1024]{1,0:T(8,128)S(1)} %get-tuple-element.22.refs_1_.refs_2_.refs_4_, f32[32,1024]{1,0:T(8,128)S(1)} %get-tuple-element.26.refs_2_.refs_0_, ...), custom_call_target="tpu_custom_call" | custom-call | flops 452984832 | bytes 786432 | tf_op jit(solution)/shard_map/pallas_call | solution.py:255
  6.8 1.5 %collective-permute-start = (f32[32,1024]{1,0:T(8,128)S(1)}, f32[32,1024]{1,0:T(8,128)S(1)}, u32[]{:S(2)}, u32[]{:S(2)}) collective-permute-start(f32[32,1024]{1,0:T(8,128)S(1)} %get-tuple-element.26.refs_2_.refs_0_), channel_id=1, source_target_pairs={{0,16},{16,0},{32,48},{48,32},{64,80},{80,64},{96,112},{112,96},{1... | collective-permute-start | bytes 393224 | tf_op jit(solution)/shard_map/ppermute | solution.py:275
  8.3 0.0 collective-permute-done.4
  8.3 1.2 %collective-permute-start.5 = (f32[32,1024]{1,0:T(8,128)S(1)}, f32[32,1024]{1,0:T(8,128)S(1)}, u32[]{:S(2)}, u32[]{:S(2)}) collective-permute-start(f32[32,1024]{1,0:T(8,128)S(1)} %collective-permute-done.4), channel_id=1, source_target_pairs={{0,32},{16,112},{32,64},{48,16},{64,96},{80,48},{96,0},{112,80},{1... | collective-permute-start | bytes 393224 | tf_op jit(solution)/shard_map/ppermute | solution.py:277
  9.5 0.0 copy-done
  9.6 0.0 copy-start.1
  9.6 0.0 copy-start.3
  9.6 0.4 shard_map.61.b_ref
  9.9 1.5 %collective-permute-start.6 = (f32[32,1024]{1,0:T(8,128)S(1)}, f32[32,1024]{1,0:T(8,128)S(1)}, u32[]{:S(2)}, u32[]{:S(2)}) collective-permute-start(f32[32,1024]{1,0:T(8,128)S(1)} %get-tuple-element.32.refs_3_.refs_1_), channel_id=1, source_target_pairs={{0,16},{16,0},{32,48},{48,32},{64,80},{80,64},{96,112},{112,96},{1... | collective-permute-start | bytes 393224 | tf_op jit(solution)/shard_map/ppermute | solution.py:275
  11.4 0.0 copy-done.1
  11.5 0.0 copy-done.3
  11.5 0.3 shard_map.59.a_ref
  11.8 0.0 collective-permute-done.2.refs_4_
  11.8 1.0 %collective-permute-start.3 = (f32[32,1024]{1,0:T(8,128)S(1)}, f32[32,1024]{1,0:T(8,128)S(1)}, u32[]{:S(2)}, u32[]{:S(2)}) collective-permute-start(f32[32,1024]{1,0:T(8,128)S(1)} %collective-permute-done.2.refs_4_), channel_id=1, source_target_pairs={{0,32},{16,112},{32,64},{48,16},{64,96},{80,48},{96,0},{112,80},{1... | collective-permute-start | bytes 393224 | tf_op jit(solution)/shard_map/ppermute | solution.py:277
  12.8 0.0 collective-permute-done.refs_3_
  12.8 0.9 %collective-permute-start.1 = (f32[32,1024]{1,0:T(8,128)S(1)}, f32[32,1024]{1,0:T(8,128)S(1)}, u32[]{:S(2)}, u32[]{:S(2)}) collective-permute-start(f32[32,1024]{1,0:T(8,128)S(1)} %collective-permute-done.refs_3_), channel_id=1, source_target_pairs={{0,32},{16,112},{32,64},{48,16},{64,96},{80,48},{96,0},{112,80},{1... | collective-permute-start | bytes 393224 | tf_op jit(solution)/shard_map/ppermute | solution.py:277
  13.7 0.0 collective-permute-done.5.refs_0_.refs_2_
  13.7 1.2 %shard_map.60 = (f32[32,1024]{1,0:T(8,128)S(1)}, f32[32,1024]{1,0:T(8,128)S(1)}) custom-call(bf16[3,288,384]{2,1,0:T(8,128)(2,1)S(1)} %shard_map.55.w_ref, f32[32,1024]{1,0:T(8,128)S(1)} %collective-permute-done.5.refs_0_.refs_2_, f32[32,1024]{1,0:T(8,128)S(1)} %shard_map.57.refs_0_.refs_1_.refs_3_, ...), custom_call_target="tpu_custom_call" | custom-call | flops 452984832 | bytes 917504 | tf_op jit(solution)/shard_map/pallas_call | solution.py:255
  14.9 0.0 collective-permute-done.6.refs_2_
  14.9 2.8 %shard_map.62 = (f32[32,1024]{1,0:T(8,128)S(1)}, f32[16,32,256]{2,1,0:T(8,128)S(1)}) custom-call(bf16[3,288,384]{2,1,0:T(8,128)(2,1)S(1)} %shard_map.55.w_ref, f32[32,1024]{1,0:T(8,128)S(1)} %get-tuple-element.26.refs_2_.refs_0_, f32[32,1024]{1,0:T(8,128)S(1)} %get-tuple-element.32.refs_3_.refs_1_, f32[32,1024]{1,0:T(8,128)S(1)} %collective-permute-done.6.refs_2_, ...), custom_call_target="tpu_custom_call" | custom-call | flops 1811939328 | bytes 1310720 | tf_op jit(solution)/shard_map/pallas_call | solution.py:255
  17.7 0.6 collective-permute-done.1.refs_0_
  18.3 0.0 collective-permute-done.3.refs_1_
  18.3 2.2 %shard_map.63 = f32[16,32,256]{2,1,0:T(8,128)S(1)} custom-call(bf16[3,288,384]{2,1,0:T(8,128)(2,1)S(1)} %shard_map.55.w_ref, f32[32,1024]{1,0:T(8,128)S(1)} %collective-permute-done.1.refs_0_, f32[32,1024]{1,0:T(8,128)S(1)} %collective-permute-done.3.refs_1_, f32[32,1024]{1,0:T(8,128)S(1)} %collective-permute-done.5.refs_0_.refs_2_, ...), custom_call_target="tpu_custom_call", output_to_operand_aliasing={{}: (10, {})} | custom-call | flops 1358954496 | bytes 1310720 | tf_op jit(solution)/shard_map/pallas_call | solution.py:255
  20.5 22.5 %all_to_all.10 = f32[16,32,256]{2,1,0:T(8,128)S(1)} all-to-all(f32[16,32,256]{2,1,0:T(8,128)S(1)} %shard_map.63), channel_id=1, replica_groups=mesh['depth'=8,'chan'=16] {'chan'}, dimensions={0} | all-to-all | bytes 1048576 | tf_op jit(solution)/shard_map/all_to_all | solution.py:291
  43.0 2.0 %shard_map.64 = f32[512,256]{1,0:T(8,128)S(1)} custom-call(f32[512,256]{1,0:T(8,128)S(1)} %bitcast.7, bf16[2048,512]{1,0:T(8,128)(2,1)S(1)} %shard_map.59.a_ref, bf16[1024,1024]{1,0:T(8,128)(2,1)S(1)} %shard_map.61.b_ref), custom_call_target="tpu_custom_call" | custom-call | flops 1610612736 | bytes 4194304 | tf_op jit(solution)/shard_map/pallas_call | solution.py:292
  45.0 15.0 %all_to_all.11.in_ref = f32[16,32,256]{2,1,0:T(8,128)S(1)} all-to-all(f32[16,32,256]{2,1,0:T(8,128)S(1)} %bitcast.8), channel_id=1, replica_groups=mesh['depth'=8,'chan'=16] {'chan'}, dimensions={0} | all-to-all | bytes 1048576 | tf_op jit(solution)/shard_map/all_to_all | solution.py:300
  60.0 1.2 %shard_map.65 = f32[32,4,1024]{2,1,0:T(4,128)} custom-call(f32[16,32,256]{2,1,0:T(8,128)S(1)} %all_to_all.11.in_ref), custom_call_target="tpu_custom_call" | custom-call | bytes 1048576 | tf_op jit(solution)/shard_map/pallas_call | solution.py:301
Async XLA Ops:
  1.1 3.8 %copy-start.2 = (f32[1,3,1,32,864]{4,3,2,1,0:T(8,128)S(1)}, f32[1,3,1,32,864]{4,3,2,1,0:T(8,128)}, u32[]{:S(2)}) copy-start(f32[1,3,1,32,864]{4,3,2,1,0:T(8,128)} %param.6) | copy-start | bytes 995332
  1.1 7.2 %collective-permute-start.4 = (f32[32,1024]{1,0:T(8,128)S(1)}, f32[32,1024]{1,0:T(8,128)S(1)}, u32[]{:S(2)}, u32[]{:S(2)}) collective-permute-start(f32[32,1024]{1,0:T(8,128)S(1)} %shard_map.57.refs_0_.refs_1_.refs_3_), channel_id=1, source_target_pairs={{0,16},{16,0},{32,48},{48,32},{64,80},{80,64},{96,112},{112,96},{1... | collective-permute-start | bytes 393224 | tf_op jit(solution)/shard_map/ppermute | solution.py:239
  4.8 4.7 %copy-start = (f32[1,512,1024]{2,1,0:T(8,128)S(1)}, f32[1,512,1024]{2,1,0:T(8,128)}, u32[]{:S(2)}) copy-start(f32[1,512,1024]{2,1,0:T(8,128)} %param.9) | copy-start | bytes 6291460
  4.8 7.0 %collective-permute-start.2 = (f32[32,1024]{1,0:T(8,128)S(1)}, f32[32,1024]{1,0:T(8,128)S(1)}, u32[]{:S(2)}, u32[]{:S(2)}) collective-permute-start(f32[32,1024]{1,0:T(8,128)S(1)} %get-tuple-element.22.refs_1_.refs_2_.refs_4_), channel_id=1, source_target_pairs={{0,16},{16,0},{32,48},{48,32},{64,80},{80,64},{96,112},{112,96},{1... | collective-permute-start | bytes 393224 | tf_op jit(solution)/shard_map/ppermute | solution.py:239
  6.8 6.0 %collective-permute-start = (f32[32,1024]{1,0:T(8,128)S(1)}, f32[32,1024]{1,0:T(8,128)S(1)}, u32[]{:S(2)}, u32[]{:S(2)}) collective-permute-start(f32[32,1024]{1,0:T(8,128)S(1)} %get-tuple-element.26.refs_2_.refs_0_), channel_id=1, source_target_pairs={{0,16},{16,0},{32,48},{48,32},{64,80},{80,64},{96,112},{112,96},{1... | collective-permute-start | bytes 393224 | tf_op jit(solution)/shard_map/ppermute | solution.py:275
  8.3 5.4 %collective-permute-start.5 = (f32[32,1024]{1,0:T(8,128)S(1)}, f32[32,1024]{1,0:T(8,128)S(1)}, u32[]{:S(2)}, u32[]{:S(2)}) collective-permute-start(f32[32,1024]{1,0:T(8,128)S(1)} %collective-permute-done.4), channel_id=1, source_target_pairs={{0,32},{16,112},{32,64},{48,16},{64,96},{80,48},{96,0},{112,80},{1... | collective-permute-start | bytes 393224 | tf_op jit(solution)/shard_map/ppermute | solution.py:277
  9.6 1.9 %copy-start.1 = (f32[1,1024,512]{2,1,0:T(8,128)S(1)}, f32[1,1024,512]{2,1,0:T(8,128)}, u32[]{:S(2)}) copy-start(f32[1,1024,512]{2,1,0:T(8,128)} %param.8) | copy-start | bytes 6291460
  9.6 1.9 %copy-start.3 = (f32[1,512]{1,0:T(1,128)S(1)}, f32[1,512]{1,0:T(1,128)}, u32[]{:S(2)}) copy-start(f32[1,512]{1,0:T(1,128)} %gain_ref.1) | copy-start | bytes 6148
  9.9 5.0 %collective-permute-start.6 = (f32[32,1024]{1,0:T(8,128)S(1)}, f32[32,1024]{1,0:T(8,128)S(1)}, u32[]{:S(2)}, u32[]{:S(2)}) collective-permute-start(f32[32,1024]{1,0:T(8,128)S(1)} %get-tuple-element.32.refs_3_.refs_1_), channel_id=1, source_target_pairs={{0,16},{16,0},{32,48},{48,32},{64,80},{80,64},{96,112},{112,96},{1... | collective-permute-start | bytes 393224 | tf_op jit(solution)/shard_map/ppermute | solution.py:275
  11.8 6.5 %collective-permute-start.3 = (f32[32,1024]{1,0:T(8,128)S(1)}, f32[32,1024]{1,0:T(8,128)S(1)}, u32[]{:S(2)}, u32[]{:S(2)}) collective-permute-start(f32[32,1024]{1,0:T(8,128)S(1)} %collective-permute-done.2.refs_4_), channel_id=1, source_target_pairs={{0,32},{16,112},{32,64},{48,16},{64,96},{80,48},{96,0},{112,80},{1... | collective-permute-start | bytes 393224 | tf_op jit(solution)/shard_map/ppermute | solution.py:277
  12.8 5.5 %collective-permute-start.1 = (f32[32,1024]{1,0:T(8,128)S(1)}, f32[32,1024]{1,0:T(8,128)S(1)}, u32[]{:S(2)}, u32[]{:S(2)}) collective-permute-start(f32[32,1024]{1,0:T(8,128)S(1)} %collective-permute-done.refs_3_), channel_id=1, source_target_pairs={{0,32},{16,112},{32,64},{48,16},{64,96},{80,48},{96,0},{112,80},{1... | collective-permute-start | bytes 393224 | tf_op jit(solution)/shard_map/ppermute | solution.py:277

commit v7 on v5

--- a/solution.py
+++ b/solution.py
@@ -45,21 +45,21 @@
     block = lax.broadcasted_iota(jnp.int32, pieces[0].shape, 1) // W
     count = len(pieces)
     runs = 128 // W
-    moved = []
-    for v in range(count):
-        total = None
-        for b in range(runs):
-            if back:
-                row = v * runs + b
-                source, at = row % count, row // count
-            else:
-                row = b * count + v
-                source, at = row // runs, row % runs
-            piece = pieces[source]
-            if at != b:
-                piece = pltpu.roll(piece, (b - at) * W % 128, 1)
-            total = piece if total is None else jnp.where(block == b, piece, total)
-        moved.append(total)
+    half = count // runs
+    moved = [None] * count
+    for s in range(half):
+        group = [pieces[s * runs + n] if back else pieces[n * half + s] for n in range(runs)]
+        step = runs // 2
+        while step:
+            lower = block // step % 2 == 0
+            for n in range(runs):
+                if n // step % 2 == 0:
+                    a, b = group[n], group[n + step]
+                    group[n] = jnp.where(lower, a, pltpu.roll(b, step * W, 1))
+                    group[n + step] = jnp.where(lower, pltpu.roll(a, 128 - step * W, 1), b)
+            step //= 2
+        for n in range(runs):
+            moved[n * half + s if back else s * runs + n] = group[n]
     return moved
 
 
@@ -113,13 +113,19 @@
         w_ref[channels + r : channels + r + rows, :] = lo
 
 
+def tiles(pieces):
+    return [halves(jnp.concatenate(pieces[n : n + 2], axis=1)) for n in range(0, len(pieces), 2)]
+
+
+def split(plane):
+    return [plane[:, v : v + 128] for v in range(0, plane.shape[1], 128)]
+
+
 def conv_plane(weight, three, acc_ref):
-    zero = jnp.zeros_like(three[0][0])
-    his = [t[0] for t in three] + [zero]
-    los = [t[1] for t in three] + [zero]
-    acc_ref[...] = jnp.dot(weight, jnp.concatenate(his + los + his, axis=0), preferred_element_type=F32)
-    width, cells = zero.shape
-    count = cells // 128
+    width, size = three[0][0][0].shape
+    zero = jnp.zeros((width, size), BF16)
+    count = acc_ref.shape[1] // 128
+    column = lax.broadcasted_iota(jnp.int32, (width, 128), 1) % W
 
     def tap(b, c, v):
         return acc_ref[(b * 3 + c) * width : (b * 3 + c + 1) * width, v * 128 : (v + 1) * 128]
@@ -129,21 +135,32 @@
         below = tap(2, c, v + 1) if v < count - 1 else pltpu.roll(tap(2, c, 0), 128 - W, 1)
         return tap(1, c, v) + above + below
 
-    column = lax.broadcasted_iota(jnp.int32, (width, 128), 1) % W
-    parts = []
-    for v in range(count):
-        left, here, right = (rows(c, v) for c in range(3))
-        left = jnp.where(column == 0, pltpu.roll(left, 128 - W + 1, 1), pltpu.roll(left, 1, 1))
-        right = jnp.where(column == W - 1, pltpu.roll(right, W - 1, 1), pltpu.roll(right, 127, 1))
-        parts.append(left + here + right)
-    return jnp.concatenate(parts, axis=1)
-
-
-def store_cells(out_ref, plane, value):
+    ready = set()
+    parts = [None] * count
+    last = len(three[0]) - 1
+    for n in (last, *range(last)):
+        his = [t[n][0] for t in three] + [zero]
+        los = [t[n][1] for t in three] + [zero]
+        acc_ref[:, n * size : (n + 1) * size] = jnp.dot(
+            weight, jnp.concatenate(his + los + his, axis=0), preferred_element_type=F32
+        )
+        ready |= {n * size // 128, n * size // 128 + 1}
+        for v in range(count):
+            if parts[v] is not None or not {(v - 1) % count, v, (v + 1) % count} <= ready:
+                continue
+            left, here, right = (rows(c, v) for c in range(3))
+            left = jnp.where(column == 0, pltpu.roll(left, 128 - W + 1, 1), pltpu.roll(left, 1, 1))
+            right = jnp.where(column == W - 1, pltpu.roll(right, W - 1, 1), pltpu.roll(right, 127, 1))
+            parts[v] = left + here + right
+    return parts
+
+
+def store_cells(out_ref, plane, pieces):
     size = out_ref.shape[2]
-    runs = value.shape[1] // size
-    for q in range(runs):
-        out_ref[plane * runs + q] = value[:, q * size : (q + 1) * size]
+    each = size // 128
+    for v, piece in enumerate(pieces):
+        at = v % each * 128
+        out_ref[plane * (len(pieces) // each) + v // each, :, at : at + 128] = piece
 
 
 def stage_kernel(given, work, kept, first, resumes, w_ref, *refs):
@@ -153,16 +170,18 @@
     refs = refs[resumes:]
     where = dict(zip(given, ins, strict=True))
     kept_at = dict(zip(kept, refs[: len(kept)], strict=True))
-    held = {key: halves(ref[...]) for key, ref in where.items()}
+    held = {key: tiles(split(ref[...])) for key, ref in where.items()}
     for n, (layer, place) in enumerate(work):
-        total = conv_plane(w_ref[layer - 1], [held[layer - 1, place + d] for d in (-1, 0, 1)], acc_ref.at[n % 2])
+        pieces = conv_plane(w_ref[layer - 1], [held[layer - 1, place + d] for d in (-1, 0, 1)], acc_ref.at[n % 4])
         if layer == layers:
-            store_cells(refs[len(kept)], place - first, where[0, place][...] + total)
+            base = split(where[0, place][...])
+            store_cells(refs[len(kept)], place - first, [b + t for b, t in zip(base, pieces, strict=True)])
             continue
-        total = gelu(total)
-        held[layer, place] = halves(total)
+        pieces = [gelu(t) for t in pieces]
+        held[layer, place] = tiles(pieces)
         if (layer, place) in kept_at:
-            kept_at[layer, place][...] = total
+            for v, piece in enumerate(pieces):
+                kept_at[layer, place][:, v * 128 : (v + 1) * 128] = piece
 
 
 def mlp_kernel(y_ref, a_ref, b_ref, out_ref, hh_ref, hl_ref):
@@ -245,7 +264,7 @@
             len(work) * 2 * 288 * 384 * cells,
             (len(given) + len(outs)) * width * cells * 4,
             [VMEM] * (1 + len(given) + len(more)),
-            [pltpu.VMEM((2, 9 * width, cells), F32)],
+            [pltpu.VMEM((4, 9 * width, cells), F32)],
             {1 + len(given): len(kept)} if more else None,
         )(taps, *[held[key] for key in given], *more)
         held.update(zip(kept, got))

time: 61.4 us -> 62.2 us (1.013)
  Pallas kernels: 12.5 us -> 13.3 us
    pallas_call x1, Pallas kernels: 1.19 us -> 2 us  [per_device(): call(place_kernel, jax.ShapeDtypeStruct(volume.shape, F32), 0, volume.siz...]
where the time goes in v7:
time: 62.2 us; the launch traced here: 62 us
  blocking collectives  38.1 us (61%)
  Pallas kernels  13.3 us (21%)
  starting transfers between devices  8.72 us (14%)
  local copies, waits for them, and re-layouts  1.06 us (2%)
    all_to_all x1, blocking collectives, per_device(): lax.all_to_all(mixed, 'chan', split_axis=0, concat_axis=0, tiled=True)  23.2 us
    all_to_all x1, blocking collectives, per_device(): lax.all_to_all(out.reshape(members, width, size), 'chan', split_axis=0, c...  15 us
    pallas_call x4, Pallas kernels, stage(): call(functools.partial(stage_kernel, given, work, kept, layers, len(more)...  7.07 us
    ppermute x2, starting transfers between devices, per_device(): there += [lax.ppermute(q, 'depth', pair) for q in (third, fourth)]  3.3 us
    ppermute x3, starting transfers between devices, per_device(): held[0, 2 - k] = lax.ppermute(there[k], 'depth', along)  3.11 us
    ppermute x2, starting transfers between devices, per_device(): there = [lax.ppermute(q, 'depth', pair) for q in own[:2]]  2.3 us
    pallas_call x1, Pallas kernels, per_device(): call(place_kernel, jax.ShapeDtypeStruct(volume.shape, F32), 0, volume.siz...  2 us
    pallas_call x1, Pallas kernels, per_device(): call(mlp_kernel, jax.ShapeDtypeStruct((channels, size), F32), 12 * hidden...  1.99 us
  transfers between devices with their start and end apart: 7, of which 2 were waited for; matrix products, arithmetic and copies ran while one was open for 0% of the time, Pallas kernels for 11%

profile of v7, /device:TPU:1, one launch (start us, length us, event | category | flops | bytes accessed | tf_op | source)
XLA Modules:
  0.0 62.0 jit_solution(4360227846183146884)
XLA Ops:
  0.0 0.0 copy-start.4
  0.0 1.0 %copy-done.4 = f32[32,4,1024]{2,1,0:T(4,128)S(1)} copy-done((f32[32,4,1024]{2,1,0:T(4,128)S(1)}, f32[32,4,1024]{2,1,0:T(4,128)}, u32[]{:S(2)}) %copy-start.4) | copy-done | bytes 524312
  1.0 0.2 shard_map.57.refs_0_.refs_1_.refs_3_
  1.2 0.0 copy-start.2
  1.3 2.2 %collective-permute-start.4 = (f32[32,1024]{1,0:T(8,128)S(1)}, f32[32,1024]{1,0:T(8,128)S(1)}, u32[]{:S(2)}, u32[]{:S(2)}) collective-permute-start(f32[32,1024]{1,0:T(8,128)S(1)} %shard_map.57.refs_0_.refs_1_.refs_3_), channel_id=1, source_target_pairs={{0,16},{16,0},{32,48},{48,32},{64,80},{80,64},{96,112},{112,96},{1... | collective-permute-start | bytes 393224 | tf_op jit(solution)/shard_map/ppermute | solution.py:245
  3.5 0.4 shard_map.56
  3.9 0.0 copy-start
  3.9 0.1 collective-permute-start.2
  4.0 0.0 copy-done.2
  4.0 0.9 %shard_map.55.w_ref = bf16[3,288,384]{2,1,0:T(8,128)(2,1)S(1)} custom-call(f32[3,32,864]{2,1,0:T(8,128)S(1)} %bitcast.9), custom_call_target="tpu_custom_call" | custom-call | bytes 663552 | tf_op jit(solution)/shard_map/pallas_call | solution.py:246
  4.9 0.9 %shard_map.58 = (f32[32,1024]{1,0:T(8,128)S(1)}, f32[32,1024]{1,0:T(8,128)S(1)}) custom-call(bf16[3,288,384]{2,1,0:T(8,128)(2,1)S(1)} %shard_map.55.w_ref, f32[32,1024]{1,0:T(8,128)S(1)} %shard_map.57.refs_0_.refs_1_.refs_3_, f32[32,1024]{1,0:T(8,128)S(1)} %get-tuple-element.22.refs_1_.refs_2_.refs_4_, f32[32,1024]{1,0:T(8,128)S(1)} %get-tuple-element.26.refs_2_.refs_0_, ...), custom_call_target="tpu_custom_call" | custom-call | flops 452984832 | bytes 786432 | tf_op jit(solution)/shard_map/pallas_call | solution.py:261
  5.9 1.5 %collective-permute-start = (f32[32,1024]{1,0:T(8,128)S(1)}, f32[32,1024]{1,0:T(8,128)S(1)}, u32[]{:S(2)}, u32[]{:S(2)}) collective-permute-start(f32[32,1024]{1,0:T(8,128)S(1)} %get-tuple-element.26.refs_2_.refs_0_), channel_id=1, source_target_pairs={{0,16},{16,0},{32,48},{48,32},{64,80},{80,64},{96,112},{112,96},{1... | collective-permute-start | bytes 393224 | tf_op jit(solution)/shard_map/ppermute | solution.py:281
  7.4 0.0 collective-permute-done.4
  7.4 1.2 %collective-permute-start.5 = (f32[32,1024]{1,0:T(8,128)S(1)}, f32[32,1024]{1,0:T(8,128)S(1)}, u32[]{:S(2)}, u32[]{:S(2)}) collective-permute-start(f32[32,1024]{1,0:T(8,128)S(1)} %collective-permute-done.4), channel_id=1, source_target_pairs={{0,32},{16,112},{32,64},{48,16},{64,96},{80,48},{96,0},{112,80},{1... | collective-permute-start | bytes 393224 | tf_op jit(solution)/shard_map/ppermute | solution.py:283
  8.6 0.0 copy-done
  8.6 0.0 copy-start.1
  8.6 0.0 copy-start.3
  8.6 0.4 shard_map.61.b_ref
  9.0 1.8 %collective-permute-start.6 = (f32[32,1024]{1,0:T(8,128)S(1)}, f32[32,1024]{1,0:T(8,128)S(1)}, u32[]{:S(2)}, u32[]{:S(2)}) collective-permute-start(f32[32,1024]{1,0:T(8,128)S(1)} %get-tuple-element.32.refs_3_.refs_1_), channel_id=1, source_target_pairs={{0,16},{16,0},{32,48},{48,32},{64,80},{80,64},{96,112},{112,96},{1... | collective-permute-start | bytes 393224 | tf_op jit(solution)/shard_map/ppermute | solution.py:281
  10.8 0.0 copy-done.1
  10.8 0.0 copy-done.3
  10.8 0.3 shard_map.59.a_ref
  11.1 0.0 collective-permute-done.2.refs_4_
  11.1 0.7 %collective-permute-start.3 = (f32[32,1024]{1,0:T(8,128)S(1)}, f32[32,1024]{1,0:T(8,128)S(1)}, u32[]{:S(2)}, u32[]{:S(2)}) collective-permute-start(f32[32,1024]{1,0:T(8,128)S(1)} %collective-permute-done.2.refs_4_), channel_id=1, source_target_pairs={{0,32},{16,112},{32,64},{48,16},{64,96},{80,48},{96,0},{112,80},{1... | collective-permute-start | bytes 393224 | tf_op jit(solution)/shard_map/ppermute | solution.py:283
  11.8 0.4 collective-permute-done.refs_3_
  12.3 1.2 %collective-permute-start.1 = (f32[32,1024]{1,0:T(8,128)S(1)}, f32[32,1024]{1,0:T(8,128)S(1)}, u32[]{:S(2)}, u32[]{:S(2)}) collective-permute-start(f32[32,1024]{1,0:T(8,128)S(1)} %collective-permute-done.refs_3_), channel_id=1, source_target_pairs={{0,32},{16,112},{32,64},{48,16},{64,96},{80,48},{96,0},{112,80},{1... | collective-permute-start | bytes 393224 | tf_op jit(solution)/shard_map/ppermute | solution.py:283
  13.5 0.0 collective-permute-done.5.refs_0_.refs_2_
  13.5 1.2 %shard_map.60 = (f32[32,1024]{1,0:T(8,128)S(1)}, f32[32,1024]{1,0:T(8,128)S(1)}) custom-call(bf16[3,288,384]{2,1,0:T(8,128)(2,1)S(1)} %shard_map.55.w_ref, f32[32,1024]{1,0:T(8,128)S(1)} %collective-permute-done.5.refs_0_.refs_2_, f32[32,1024]{1,0:T(8,128)S(1)} %shard_map.57.refs_0_.refs_1_.refs_3_, ...), custom_call_target="tpu_custom_call" | custom-call | flops 452984832 | bytes 917504 | tf_op jit(solution)/shard_map/pallas_call | solution.py:261
  14.7 0.0 collective-permute-done.6.refs_2_
  14.7 2.8 %shard_map.62 = (f32[32,1024]{1,0:T(8,128)S(1)}, f32[16,32,256]{2,1,0:T(8,128)S(1)}) custom-call(bf16[3,288,384]{2,1,0:T(8,128)(2,1)S(1)} %shard_map.55.w_ref, f32[32,1024]{1,0:T(8,128)S(1)} %get-tuple-element.26.refs_2_.refs_0_, f32[32,1024]{1,0:T(8,128)S(1)} %get-tuple-element.32.refs_3_.refs_1_, f32[32,1024]{1,0:T(8,128)S(1)} %collective-permute-done.6.refs_2_, ...), custom_call_target="tpu_custom_call" | custom-call | flops 1811939328 | bytes 1310720 | tf_op jit(solution)/shard_map/pallas_call | solution.py:261
  17.5 0.2 collective-permute-done.1.refs_0_
  17.6 0.0 collective-permute-done.3.refs_1_
  17.6 2.2 %shard_map.63 = f32[16,32,256]{2,1,0:T(8,128)S(1)} custom-call(bf16[3,288,384]{2,1,0:T(8,128)(2,1)S(1)} %shard_map.55.w_ref, f32[32,1024]{1,0:T(8,128)S(1)} %collective-permute-done.1.refs_0_, f32[32,1024]{1,0:T(8,128)S(1)} %collective-permute-done.3.refs_1_, f32[32,1024]{1,0:T(8,128)S(1)} %collective-permute-done.5.refs_0_.refs_2_, ...), custom_call_target="tpu_custom_call", output_to_operand_aliasing={{}: (10, {})} | custom-call | flops 1358954496 | bytes 1310720 | tf_op jit(solution)/shard_map/pallas_call | solution.py:261
  19.8 23.2 %all_to_all.10 = f32[16,32,256]{2,1,0:T(8,128)S(1)} all-to-all(f32[16,32,256]{2,1,0:T(8,128)S(1)} %shard_map.63), channel_id=1, replica_groups=mesh['depth'=8,'chan'=16] {'chan'}, dimensions={0} | all-to-all | bytes 1048576 | tf_op jit(solution)/shard_map/all_to_all | solution.py:297
  43.0 2.0 %shard_map.64 = f32[512,256]{1,0:T(8,128)S(1)} custom-call(f32[512,256]{1,0:T(8,128)S(1)} %bitcast.7, bf16[2048,512]{1,0:T(8,128)(2,1)S(1)} %shard_map.59.a_ref, bf16[1024,1024]{1,0:T(8,128)(2,1)S(1)} %shard_map.61.b_ref), custom_call_target="tpu_custom_call" | custom-call | flops 1610612736 | bytes 4194304 | tf_op jit(solution)/shard_map/pallas_call | solution.py:298
  45.0 15.0 %all_to_all.11.in_ref = f32[16,32,256]{2,1,0:T(8,128)S(1)} all-to-all(f32[16,32,256]{2,1,0:T(8,128)S(1)} %bitcast.8), channel_id=1, replica_groups=mesh['depth'=8,'chan'=16] {'chan'}, dimensions={0} | all-to-all | bytes 1048576 | tf_op jit(solution)/shard_map/all_to_all | solution.py:306
  60.0 2.0 %shard_map.65 = f32[32,4,1024]{2,1,0:T(4,128)} custom-call(f32[16,32,256]{2,1,0:T(8,128)S(1)} %all_to_all.11.in_ref), custom_call_target="tpu_custom_call" | custom-call | bytes 1048576 | tf_op jit(solution)/shard_map/pallas_call | solution.py:307
Async XLA Ops:
  0.0 1.0 %copy-start.4 = (f32[32,4,1024]{2,1,0:T(4,128)S(1)}, f32[32,4,1024]{2,1,0:T(4,128)}, u32[]{:S(2)}) copy-start(f32[32,4,1024]{2,1,0:T(4,128)} %x_ref.3) | copy-start | bytes 1572868
  1.2 2.8 %copy-start.2 = (f32[1,3,1,32,864]{4,3,2,1,0:T(8,128)S(1)}, f32[1,3,1,32,864]{4,3,2,1,0:T(8,128)}, u32[]{:S(2)}) copy-start(f32[1,3,1,32,864]{4,3,2,1,0:T(8,128)} %param.6) | copy-start | bytes 995332
  1.3 6.1 %collective-permute-start.4 = (f32[32,1024]{1,0:T(8,128)S(1)}, f32[32,1024]{1,0:T(8,128)S(1)}, u32[]{:S(2)}, u32[]{:S(2)}) collective-permute-start(f32[32,1024]{1,0:T(8,128)S(1)} %shard_map.57.refs_0_.refs_1_.refs_3_), channel_id=1, source_target_pairs={{0,16},{16,0},{32,48},{48,32},{64,80},{80,64},{96,112},{112,96},{1... | collective-permute-start | bytes 393224 | tf_op jit(solution)/shard_map/ppermute | solution.py:245
  3.9 4.7 %copy-start = (f32[1,512,1024]{2,1,0:T(8,128)S(1)}, f32[1,512,1024]{2,1,0:T(8,128)}, u32[]{:S(2)}) copy-start(f32[1,512,1024]{2,1,0:T(8,128)} %param.9) | copy-start | bytes 6291460
  3.9 7.2 %collective-permute-start.2 = (f32[32,1024]{1,0:T(8,128)S(1)}, f32[32,1024]{1,0:T(8,128)S(1)}, u32[]{:S(2)}, u32[]{:S(2)}) collective-permute-start(f32[32,1024]{1,0:T(8,128)S(1)} %get-tuple-element.22.refs_1_.refs_2_.refs_4_), channel_id=1, source_target_pairs={{0,16},{16,0},{32,48},{48,32},{64,80},{80,64},{96,112},{112,96},{1... | collective-permute-start | bytes 393224 | tf_op jit(solution)/shard_map/ppermute | solution.py:245
  5.9 6.4 %collective-permute-start = (f32[32,1024]{1,0:T(8,128)S(1)}, f32[32,1024]{1,0:T(8,128)S(1)}, u32[]{:S(2)}, u32[]{:S(2)}) collective-permute-start(f32[32,1024]{1,0:T(8,128)S(1)} %get-tuple-element.26.refs_2_.refs_0_), channel_id=1, source_target_pairs={{0,16},{16,0},{32,48},{48,32},{64,80},{80,64},{96,112},{112,96},{1... | collective-permute-start | bytes 393224 | tf_op jit(solution)/shard_map/ppermute | solution.py:281
  7.4 6.1 %collective-permute-start.5 = (f32[32,1024]{1,0:T(8,128)S(1)}, f32[32,1024]{1,0:T(8,128)S(1)}, u32[]{:S(2)}, u32[]{:S(2)}) collective-permute-start(f32[32,1024]{1,0:T(8,128)S(1)} %collective-permute-done.4), channel_id=1, source_target_pairs={{0,32},{16,112},{32,64},{48,16},{64,96},{80,48},{96,0},{112,80},{1... | collective-permute-start | bytes 393224 | tf_op jit(solution)/shard_map/ppermute | solution.py:283
  8.6 2.2 %copy-start.1 = (f32[1,1024,512]{2,1,0:T(8,128)S(1)}, f32[1,1024,512]{2,1,0:T(8,128)}, u32[]{:S(2)}) copy-start(f32[1,1024,512]{2,1,0:T(8,128)} %param.8) | copy-start | bytes 6291460
  8.6 2.2 %copy-start.3 = (f32[1,512]{1,0:T(1,128)S(1)}, f32[1,512]{1,0:T(1,128)}, u32[]{:S(2)}) copy-start(f32[1,512]{1,0:T(1,128)} %gain_ref.1) | copy-start | bytes 6148
  9.0 5.7 %collective-permute-start.6 = (f32[32,1024]{1,0:T(8,128)S(1)}, f32[32,1024]{1,0:T(8,128)S(1)}, u32[]{:S(2)}, u32[]{:S(2)}) collective-permute-start(f32[32,1024]{1,0:T(8,128)S(1)} %get-tuple-element.32.refs_3_.refs_1_), channel_id=1, source_target_pairs={{0,16},{16,0},{32,48},{48,32},{64,80},{80,64},{96,112},{112,96},{1... | collective-permute-start | bytes 393224 | tf_op jit(solution)/shard_map/ppermute | solution.py:281
  11.1 6.5 %collective-permute-start.3 = (f32[32,1024]{1,0:T(8,128)S(1)}, f32[32,1024]{1,0:T(8,128)S(1)}, u32[]{:S(2)}, u32[]{:S(2)}) collective-permute-start(f32[32,1024]{1,0:T(8,128)S(1)} %collective-permute-done.2.refs_4_), channel_id=1, source_target_pairs={{0,32},{16,112},{32,64},{48,16},{64,96},{80,48},{96,0},{112,80},{1... | collective-permute-start | bytes 393224 | tf_op jit(solution)/shard_map/ppermute | solution.py:283
  12.3 5.4 %collective-permute-start.1 = (f32[32,1024]{1,0:T(8,128)S(1)}, f32[32,1024]{1,0:T(8,128)S(1)}, u32[]{:S(2)}, u32[]{:S(2)}) collective-permute-start(f32[32,1024]{1,0:T(8,128)S(1)} %collective-permute-done.refs_3_), channel_id=1, source_target_pairs={{0,32},{16,112},{32,64},{48,16},{64,96},{80,48},{96,0},{112,80},{1... | collective-permute-start | bytes 393224 | tf_op jit(solution)/shard_map/ppermute | solution.py:283

commit v8 on v5

--- a/solution.py
+++ b/solution.py
@@ -254,11 +254,11 @@
     stage(((0, 3), (0, 4), (0, 5), (0, 6)), ((1, 4), (1, 5)), ((1, 4), (1, 5)))
     weights = jax.ShapeDtypeStruct((2 * hidden, channels), BF16)
     w_in = call(first_weights_kernel, weights, 0, mlp_in.size * 8, [VMEM] * 2)(norm_gain, mlp_in[0])
-    third, held[1, 4], held[1, 5] = lax.optimization_barrier((own[2], held[1, 4], held[1, 5]))
+    third, held[1, 4], held[1, 5], w_in = lax.optimization_barrier((own[2], held[1, 4], held[1, 5], w_in))
     weights = jax.ShapeDtypeStruct((2 * channels, hidden), BF16)
     w_out = call(second_weights_kernel, weights, 0, mlp_out.size * 8, [VMEM])(mlp_out[0])
     fourth, w_out = lax.optimization_barrier((own[3], w_out))
-    there[1], w_in = lax.optimization_barrier((there[1], w_in))
+    there[1], w_out = lax.optimization_barrier((there[1], w_out))
     there += [lax.ppermute(q, "depth", pair) for q in (third, fourth)]
     for k in range(layers):
         held[0, 2 - k] = lax.ppermute(there[k], "depth", along)

time: 61.4 us -> 61 us (level)
  starting transfers between devices: 8.72 us -> 7.75 us
  waiting for transfers between devices: 0.58 us -> 1.48 us
    ppermute x2, waiting for transfers between devices: 0.42 us -> 1.37 us  [per_device(): there += [lax.ppermute(q, 'depth', pair) for q in (third, fourth)]]
    ppermute x3, starting transfers between devices: 3.1 us -> 2.41 us  [per_device(): held[0, 2 - k] = lax.ppermute(there[k], 'depth', along)]
  transfers between devices with their start and end apart: 7 -> 7, of which waited for: 2 -> 2; matrix products, arithmetic and copies ran while one was open for 0% -> 0% of each run, Pallas kernels for 11% -> 12%
where the time goes in v8:
time: 61 us; the launch traced here: 60.8 us
  blocking collectives  37.8 us (62%)
  Pallas kernels  12.6 us (21%)
  starting transfers between devices  7.75 us (13%)
  waiting for transfers between devices  1.48 us (2%)
  local copies, waits for them, and re-layouts  1.07 us (2%)
    all_to_all x1, blocking collectives, per_device(): lax.all_to_all(mixed, 'chan', split_axis=0, concat_axis=0, tiled=True)  22.8 us
    all_to_all x1, blocking collectives, per_device(): lax.all_to_all(out.reshape(members, width, size), 'chan', split_axis=0, c...  15 us
    pallas_call x4, Pallas kernels, stage(): call(functools.partial(stage_kernel, given, work, kept, layers, len(more)...  7.12 us
    ppermute x2, starting transfers between devices, per_device(): there += [lax.ppermute(q, 'depth', pair) for q in (third, fourth)]  3.03 us
    ppermute x3, starting transfers between devices, per_device(): held[0, 2 - k] = lax.ppermute(there[k], 'depth', along)  2.41 us
    ppermute x2, starting transfers between devices, per_device(): there = [lax.ppermute(q, 'depth', pair) for q in own[:2]]  2.3 us
    pallas_call x1, Pallas kernels, per_device(): call(mlp_kernel, jax.ShapeDtypeStruct((channels, size), F32), 12 * hidden...  2.03 us
    ppermute x2, waiting for transfers between devices, per_device(): there += [lax.ppermute(q, 'depth', pair) for q in (third, fourth)]  1.37 us
  transfers between devices with their start and end apart: 7, of which 2 were waited for; matrix products, arithmetic and copies ran while one was open for 0% of the time, Pallas kernels for 12%

profile of v8, /device:TPU:1, one launch (start us, length us, event | category | flops | bytes accessed | tf_op | source)
XLA Modules:
  0.0 60.8 jit_solution(15070159267956323112)
XLA Ops:
  0.0 0.0 copy-start.4
  0.0 1.0 %copy-done.4 = f32[32,4,1024]{2,1,0:T(4,128)S(1)} copy-done((f32[32,4,1024]{2,1,0:T(4,128)S(1)}, f32[32,4,1024]{2,1,0:T(4,128)}, u32[]{:S(2)}) %copy-start.4) | copy-done | bytes 524312
  1.0 0.2 shard_map.57.refs_0_.refs_1_.refs_3_
  1.2 0.0 copy-start.2
  1.3 2.2 %collective-permute-start.4 = (f32[32,1024]{1,0:T(8,128)S(1)}, f32[32,1024]{1,0:T(8,128)S(1)}, u32[]{:S(2)}, u32[]{:S(2)}) collective-permute-start(f32[32,1024]{1,0:T(8,128)S(1)} %shard_map.57.refs_0_.refs_1_.refs_3_), channel_id=1, source_target_pairs={{0,16},{16,0},{32,48},{48,32},{64,80},{80,64},{96,112},{112,96},{1... | collective-permute-start | bytes 393224 | tf_op jit(solution)/shard_map/ppermute | solution.py:226
  3.5 0.4 shard_map.56
  3.9 0.0 copy-start.1
  3.9 0.0 copy-start.3
  3.9 0.1 collective-permute-start.2
  4.0 0.0 copy-done.2
  4.0 0.9 %shard_map.55.w_ref = bf16[3,288,384]{2,1,0:T(8,128)(2,1)S(1)} custom-call(f32[3,32,864]{2,1,0:T(8,128)S(1)} %bitcast.9), custom_call_target="tpu_custom_call" | custom-call | bytes 663552 | tf_op jit(solution)/shard_map/pallas_call | solution.py:227
  4.9 0.9 %shard_map.58 = (f32[32,1024]{1,0:T(8,128)S(1)}, f32[32,1024]{1,0:T(8,128)S(1)}) custom-call(bf16[3,288,384]{2,1,0:T(8,128)(2,1)S(1)} %shard_map.55.w_ref, f32[32,1024]{1,0:T(8,128)S(1)} %shard_map.57.refs_0_.refs_1_.refs_3_, f32[32,1024]{1,0:T(8,128)S(1)} %get-tuple-element.23.refs_1_.refs_2_.refs_4_, f32[32,1024]{1,0:T(8,128)S(1)} %get-tuple-element.27.refs_2_.refs_0_, ...), custom_call_target="tpu_custom_call" | custom-call | flops 452984832 | bytes 786432 | tf_op jit(solution)/shard_map/pallas_call | solution.py:242
  5.9 0.0 copy-done.1
  5.9 0.0 copy-done.3
  5.9 0.0 copy-start
  5.9 0.3 shard_map.59.a_ref
  6.2 1.5 %collective-permute-start = (f32[32,1024]{1,0:T(8,128)S(1)}, f32[32,1024]{1,0:T(8,128)S(1)}, u32[]{:S(2)}, u32[]{:S(2)}) collective-permute-start(f32[32,1024]{1,0:T(8,128)S(1)} %get-tuple-element.27.refs_2_.refs_0_), channel_id=1, source_target_pairs={{0,16},{16,0},{32,48},{48,32},{64,80},{80,64},{96,112},{112,96},{1... | collective-permute-start | bytes 393224 | tf_op jit(solution)/shard_map/ppermute | solution.py:262
  7.8 0.0 collective-permute-done.4
  7.8 1.2 %collective-permute-start.5 = (f32[32,1024]{1,0:T(8,128)S(1)}, f32[32,1024]{1,0:T(8,128)S(1)}, u32[]{:S(2)}, u32[]{:S(2)}) collective-permute-start(f32[32,1024]{1,0:T(8,128)S(1)} %collective-permute-done.4), channel_id=1, source_target_pairs={{0,32},{16,112},{32,64},{48,16},{64,96},{80,48},{96,0},{112,80},{1... | collective-permute-start | bytes 393224 | tf_op jit(solution)/shard_map/ppermute | solution.py:264
  9.0 0.0 copy-done
  9.0 0.4 shard_map.60.b_ref
  9.4 1.5 %collective-permute-start.6 = (f32[32,1024]{1,0:T(8,128)S(1)}, f32[32,1024]{1,0:T(8,128)S(1)}, u32[]{:S(2)}, u32[]{:S(2)}) collective-permute-start(f32[32,1024]{1,0:T(8,128)S(1)} %get-tuple-element.34.refs_3_.refs_1_), channel_id=1, source_target_pairs={{0,16},{16,0},{32,48},{48,32},{64,80},{80,64},{96,112},{112,96},{1... | collective-permute-start | bytes 393224 | tf_op jit(solution)/shard_map/ppermute | solution.py:262
  10.9 0.0 collective-permute-done.2.refs_4_
  10.9 0.0 collective-permute-start.3
  10.9 1.4 %collective-permute-done.refs_3_ = f32[32,1024]{1,0:T(8,128)S(1)} collective-permute-done((f32[32,1024]{1,0:T(8,128)S(1)}, f32[32,1024]{1,0:T(8,128)S(1)}, u32[]{:S(2)}, u32[]{:S(2)}) %collective-permute-start) | collective-permute-done | bytes 131104 | tf_op jit(solution)/shard_map/ppermute | solution.py:262
  12.3 1.2 %collective-permute-start.1 = (f32[32,1024]{1,0:T(8,128)S(1)}, f32[32,1024]{1,0:T(8,128)S(1)}, u32[]{:S(2)}, u32[]{:S(2)}) collective-permute-start(f32[32,1024]{1,0:T(8,128)S(1)} %collective-permute-done.refs_3_), channel_id=1, source_target_pairs={{0,32},{16,112},{32,64},{48,16},{64,96},{80,48},{96,0},{112,80},{1... | collective-permute-start | bytes 393224 | tf_op jit(solution)/shard_map/ppermute | solution.py:264
  13.4 0.0 collective-permute-done.5.refs_0_.refs_2_
  13.5 1.2 %shard_map.61 = (f32[32,1024]{1,0:T(8,128)S(1)}, f32[32,1024]{1,0:T(8,128)S(1)}) custom-call(bf16[3,288,384]{2,1,0:T(8,128)(2,1)S(1)} %shard_map.55.w_ref, f32[32,1024]{1,0:T(8,128)S(1)} %collective-permute-done.5.refs_0_.refs_2_, f32[32,1024]{1,0:T(8,128)S(1)} %shard_map.57.refs_0_.refs_1_.refs_3_, ...), custom_call_target="tpu_custom_call" | custom-call | flops 452984832 | bytes 917504 | tf_op jit(solution)/shard_map/pallas_call | solution.py:242
  14.7 0.0 collective-permute-done.6.refs_2_
  14.7 2.8 %shard_map.62 = (f32[32,1024]{1,0:T(8,128)S(1)}, f32[16,32,256]{2,1,0:T(8,128)S(1)}) custom-call(bf16[3,288,384]{2,1,0:T(8,128)(2,1)S(1)} %shard_map.55.w_ref, f32[32,1024]{1,0:T(8,128)S(1)} %get-tuple-element.27.refs_2_.refs_0_, f32[32,1024]{1,0:T(8,128)S(1)} %get-tuple-element.34.refs_3_.refs_1_, f32[32,1024]{1,0:T(8,128)S(1)} %collective-permute-done.6.refs_2_, ...), custom_call_target="tpu_custom_call" | custom-call | flops 1811939328 | bytes 1310720 | tf_op jit(solution)/shard_map/pallas_call | solution.py:242
  17.5 0.1 collective-permute-done.1.refs_0_
  17.6 0.0 collective-permute-done.3.refs_1_
  17.6 2.2 %shard_map.63 = f32[16,32,256]{2,1,0:T(8,128)S(1)} custom-call(bf16[3,288,384]{2,1,0:T(8,128)(2,1)S(1)} %shard_map.55.w_ref, f32[32,1024]{1,0:T(8,128)S(1)} %collective-permute-done.1.refs_0_, f32[32,1024]{1,0:T(8,128)S(1)} %collective-permute-done.3.refs_1_, f32[32,1024]{1,0:T(8,128)S(1)} %collective-permute-done.5.refs_0_.refs_2_, ...), custom_call_target="tpu_custom_call", output_to_operand_aliasing={{}: (10, {})} | custom-call | flops 1358954496 | bytes 1310720 | tf_op jit(solution)/shard_map/pallas_call | solution.py:242
  19.8 22.8 %all_to_all.10 = f32[16,32,256]{2,1,0:T(8,128)S(1)} all-to-all(f32[16,32,256]{2,1,0:T(8,128)S(1)} %shard_map.63), channel_id=1, replica_groups=mesh['depth'=8,'chan'=16] {'chan'}, dimensions={0} | all-to-all | bytes 1048576 | tf_op jit(solution)/shard_map/all_to_all | solution.py:278
  42.6 2.0 %shard_map.64 = f32[512,256]{1,0:T(8,128)S(1)} custom-call(f32[512,256]{1,0:T(8,128)S(1)} %bitcast.7, bf16[2048,512]{1,0:T(8,128)(2,1)S(1)} %shard_map.59.a_ref, bf16[1024,1024]{1,0:T(8,128)(2,1)S(1)} %shard_map.60.b_ref), custom_call_target="tpu_custom_call" | custom-call | flops 1610612736 | bytes 4194304 | tf_op jit(solution)/shard_map/pallas_call | solution.py:279
  44.6 15.0 %all_to_all.11.in_ref = f32[16,32,256]{2,1,0:T(8,128)S(1)} all-to-all(f32[16,32,256]{2,1,0:T(8,128)S(1)} %bitcast.8), channel_id=1, replica_groups=mesh['depth'=8,'chan'=16] {'chan'}, dimensions={0} | all-to-all | bytes 1048576 | tf_op jit(solution)/shard_map/all_to_all | solution.py:287
  59.6 1.2 %shard_map.65 = f32[32,4,1024]{2,1,0:T(4,128)} custom-call(f32[16,32,256]{2,1,0:T(8,128)S(1)} %all_to_all.11.in_ref), custom_call_target="tpu_custom_call" | custom-call | bytes 1048576 | tf_op jit(solution)/shard_map/pallas_call | solution.py:288
Async XLA Ops:
  0.0 1.0 %copy-start.4 = (f32[32,4,1024]{2,1,0:T(4,128)S(1)}, f32[32,4,1024]{2,1,0:T(4,128)}, u32[]{:S(2)}) copy-start(f32[32,4,1024]{2,1,0:T(4,128)} %x_ref.3) | copy-start | bytes 1572868
  1.2 2.7 %copy-start.2 = (f32[1,3,1,32,864]{4,3,2,1,0:T(8,128)S(1)}, f32[1,3,1,32,864]{4,3,2,1,0:T(8,128)}, u32[]{:S(2)}) copy-start(f32[1,3,1,32,864]{4,3,2,1,0:T(8,128)} %param.6) | copy-start | bytes 995332
  1.3 6.5 %collective-permute-start.4 = (f32[32,1024]{1,0:T(8,128)S(1)}, f32[32,1024]{1,0:T(8,128)S(1)}, u32[]{:S(2)}, u32[]{:S(2)}) collective-permute-start(f32[32,1024]{1,0:T(8,128)S(1)} %shard_map.57.refs_0_.refs_1_.refs_3_), channel_id=1, source_target_pairs={{0,16},{16,0},{32,48},{48,32},{64,80},{80,64},{96,112},{112,96},{1... | collective-permute-start | bytes 393224 | tf_op jit(solution)/shard_map/ppermute | solution.py:226
  3.9 2.0 %copy-start.1 = (f32[1,1024,512]{2,1,0:T(8,128)S(1)}, f32[1,1024,512]{2,1,0:T(8,128)}, u32[]{:S(2)}) copy-start(f32[1,1024,512]{2,1,0:T(8,128)} %param.8) | copy-start | bytes 6291460
  3.9 2.0 %copy-start.3 = (f32[1,512]{1,0:T(1,128)S(1)}, f32[1,512]{1,0:T(1,128)}, u32[]{:S(2)}) copy-start(f32[1,512]{1,0:T(1,128)} %gain_ref.1) | copy-start | bytes 6148
  3.9 7.0 %collective-permute-start.2 = (f32[32,1024]{1,0:T(8,128)S(1)}, f32[32,1024]{1,0:T(8,128)S(1)}, u32[]{:S(2)}, u32[]{:S(2)}) collective-permute-start(f32[32,1024]{1,0:T(8,128)S(1)} %get-tuple-element.23.refs_1_.refs_2_.refs_4_), channel_id=1, source_target_pairs={{0,16},{16,0},{32,48},{48,32},{64,80},{80,64},{96,112},{112,96},{1... | collective-permute-start | bytes 393224 | tf_op jit(solution)/shard_map/ppermute | solution.py:226
  5.9 3.1 %copy-start = (f32[1,512,1024]{2,1,0:T(8,128)S(1)}, f32[1,512,1024]{2,1,0:T(8,128)}, u32[]{:S(2)}) copy-start(f32[1,512,1024]{2,1,0:T(8,128)} %param.9) | copy-start | bytes 6291460
  6.2 6.0 %collective-permute-start = (f32[32,1024]{1,0:T(8,128)S(1)}, f32[32,1024]{1,0:T(8,128)S(1)}, u32[]{:S(2)}, u32[]{:S(2)}) collective-permute-start(f32[32,1024]{1,0:T(8,128)S(1)} %get-tuple-element.27.refs_2_.refs_0_), channel_id=1, source_target_pairs={{0,16},{16,0},{32,48},{48,32},{64,80},{80,64},{96,112},{112,96},{1... | collective-permute-start | bytes 393224 | tf_op jit(solution)/shard_map/ppermute | solution.py:262
  7.8 5.7 %collective-permute-start.5 = (f32[32,1024]{1,0:T(8,128)S(1)}, f32[32,1024]{1,0:T(8,128)S(1)}, u32[]{:S(2)}, u32[]{:S(2)}) collective-permute-start(f32[32,1024]{1,0:T(8,128)S(1)} %collective-permute-done.4), channel_id=1, source_target_pairs={{0,32},{16,112},{32,64},{48,16},{64,96},{80,48},{96,0},{112,80},{1... | collective-permute-start | bytes 393224 | tf_op jit(solution)/shard_map/ppermute | solution.py:264
  9.4 5.3 %collective-permute-start.6 = (f32[32,1024]{1,0:T(8,128)S(1)}, f32[32,1024]{1,0:T(8,128)S(1)}, u32[]{:S(2)}, u32[]{:S(2)}) collective-permute-start(f32[32,1024]{1,0:T(8,128)S(1)} %get-tuple-element.34.refs_3_.refs_1_), channel_id=1, source_target_pairs={{0,16},{16,0},{32,48},{48,32},{64,80},{80,64},{96,112},{112,96},{1... | collective-permute-start | bytes 393224 | tf_op jit(solution)/shard_map/ppermute | solution.py:262
  10.9 6.7 %collective-permute-start.3 = (f32[32,1024]{1,0:T(8,128)S(1)}, f32[32,1024]{1,0:T(8,128)S(1)}, u32[]{:S(2)}, u32[]{:S(2)}) collective-permute-start(f32[32,1024]{1,0:T(8,128)S(1)} %collective-permute-done.2.refs_4_), channel_id=1, source_target_pairs={{0,32},{16,112},{32,64},{48,16},{64,96},{80,48},{96,0},{112,80},{1... | collective-permute-start | bytes 393224 | tf_op jit(solution)/shard_map/ppermute | solution.py:264
  12.3 5.3 %collective-permute-start.1 = (f32[32,1024]{1,0:T(8,128)S(1)}, f32[32,1024]{1,0:T(8,128)S(1)}, u32[]{:S(2)}, u32[]{:S(2)}) collective-permute-start(f32[32,1024]{1,0:T(8,128)S(1)} %collective-permute-done.refs_3_), channel_id=1, source_target_pairs={{0,32},{16,112},{32,64},{48,16},{64,96},{80,48},{96,0},{112,80},{1... | collective-permute-start | bytes 393224 | tf_op jit(solution)/shard_map/ppermute | solution.py:264

commit v9 on v8

--- a/solution.py
+++ b/solution.py
@@ -63,6 +63,18 @@
     return moved
 
 
+def first_plane_kernel(x_hbm, x_ref, q_ref, sems):
+    rows = x_ref.shape[0] // PARTS
+    copies = []
+    for n in range(PARTS):
+        part = pl.ds(n * rows, rows)
+        copies.append(pltpu.make_async_copy(x_hbm.at[part], x_ref.at[part], sems.at[n]))
+        copies[-1].start()
+    for copy in copies:
+        copy.wait()
+    planes_kernel((0,), x_ref, q_ref)
+
+
 def planes_kernel(places, x_ref, *q_refs):
     last = x_ref.shape[1] - 1
     flip = turned_here()
@@ -219,10 +231,16 @@
 
     pair = [(i, i ^ 1) for i in range(count)]
     along = [(i, (i + (2 if i % 2 == 0 else count - 2)) % count) for i in range(count)]
-    own = []
-    for places in ((0,), tuple(range(1, planes))):
-        body = functools.partial(planes_kernel, places)
-        own += call(body, (plane,) * len(places), 10**9, len(places) * width * cells * 8, [VMEM])(volume)
+    here, first = call(
+        first_plane_kernel,
+        (jax.ShapeDtypeStruct(volume.shape, F32), plane),
+        10**9,
+        volume.size * 8,
+        [HBM],
+        [pltpu.SemaphoreType.DMA((PARTS,))],
+    )(pltpu.with_memory_space_constraint(volume, pltpu.HBM))
+    body = functools.partial(planes_kernel, tuple(range(1, planes)))
+    own = (first, *call(body, (plane,) * (planes - 1), 10**9, volume.size * 6, [VMEM])(here))
     there = [lax.ppermute(q, "depth", pair) for q in own[:2]]
     taps = call(
         taps_kernel,

time: 61 us -> 61 us (level)
  Pallas kernels: 12.6 us -> 13.7 us
  local copies, waits for them, and re-layouts: 1.07 us -> 0.03 us
    pallas_call x2, Pallas kernels: 0.58 us -> 1.71 us  [the longest x1 1.32 us: per_device(): call(first_plane_kernel, (jax.ShapeDtypeStruct(volume.shape, F32), plane)...]
    unnamed x10 -> x8, local copies, waits for them, and re-layouts: 1.07 us -> 0.03 us
  transfers between devices with their start and end apart: 7 -> 7, of which waited for: 2 -> 2; matrix products, arithmetic and copies ran while one was open for 0% -> 0% of each run, Pallas kernels for 12% -> 11%
where the time goes in v9:
time: 61 us; the launch traced here: 60.9 us
  blocking collectives  37.7 us (62%)
  Pallas kernels  13.7 us (22%)
  starting transfers between devices  7.76 us (13%)
  waiting for transfers between devices  1.48 us (2%)
    all_to_all x1, blocking collectives, per_device(): lax.all_to_all(mixed, 'chan', split_axis=0, concat_axis=0, tiled=True)  22.8 us
    all_to_all x1, blocking collectives, per_device(): lax.all_to_all(out.reshape(members, width, size), 'chan', split_axis=0, c...  15 us
    pallas_call x4, Pallas kernels, stage(): call(functools.partial(stage_kernel, given, work, kept, layers, len(more)...  7.11 us
    ppermute x2, starting transfers between devices, per_device(): there += [lax.ppermute(q, 'depth', pair) for q in (third, fourth)]  3.04 us
    ppermute x3, starting transfers between devices, per_device(): held[0, 2 - k] = lax.ppermute(there[k], 'depth', along)  2.41 us
    ppermute x2, starting transfers between devices, per_device(): there = [lax.ppermute(q, 'depth', pair) for q in own[:2]]  2.3 us
    pallas_call x1, Pallas kernels, per_device(): call(mlp_kernel, jax.ShapeDtypeStruct((channels, size), F32), 12 * hidden...  2.03 us
    ppermute x2, waiting for transfers between devices, per_device(): there += [lax.ppermute(q, 'depth', pair) for q in (third, fourth)]  1.36 us
  transfers between devices with their start and end apart: 7, of which 2 were waited for; matrix products, arithmetic and copies ran while one was open for 0% of the time, Pallas kernels for 11%

profile of v9, /device:TPU:1, one launch (start us, length us, event | category | flops | bytes accessed | tf_op | source)
XLA Modules:
  0.0 60.9 jit_solution(17215918971906573319)
XLA Ops:
  0.0 1.3 %shard_map.56 = (f32[32,4,1024]{2,1,0:T(4,128)S(1)}, f32[32,1024]{1,0:T(8,128)S(1)}) custom-call(f32[32,4,1024]{2,1,0:T(4,128)} %x_hbm.1), custom_call_target="tpu_custom_call" | custom-call | flops 1000000000 | bytes 1048576 | tf_op jit(solution)/shard_map/pallas_call | solution.py:234
  1.3 0.0 copy-start.2
  1.3 2.2 %collective-permute-start.4 = (f32[32,1024]{1,0:T(8,128)S(1)}, f32[32,1024]{1,0:T(8,128)S(1)}, u32[]{:S(2)}, u32[]{:S(2)}) collective-permute-start(f32[32,1024]{1,0:T(8,128)S(1)} %get-tuple-element.26.refs_0_.refs_1_.refs_3_), channel_id=1, source_target_pairs={{0,16},{16,0},{32,48},{48,32},{64,80},{80,64},{96,112},{112,96},{1... | collective-permute-start | bytes 393224 | tf_op jit(solution)/shard_map/ppermute | solution.py:244
  3.5 0.4 shard_map.57
  3.9 0.0 copy-start.1
  4.0 0.0 copy-start.3
  4.0 0.1 collective-permute-start.2
  4.1 0.0 copy-done.2
  4.1 0.9 %shard_map.55.w_ref = bf16[3,288,384]{2,1,0:T(8,128)(2,1)S(1)} custom-call(f32[3,32,864]{2,1,0:T(8,128)S(1)} %bitcast.9), custom_call_target="tpu_custom_call" | custom-call | bytes 663552 | tf_op jit(solution)/shard_map/pallas_call | solution.py:245
  5.0 0.9 %shard_map.58 = (f32[32,1024]{1,0:T(8,128)S(1)}, f32[32,1024]{1,0:T(8,128)S(1)}) custom-call(bf16[3,288,384]{2,1,0:T(8,128)(2,1)S(1)} %shard_map.55.w_ref, f32[32,1024]{1,0:T(8,128)S(1)} %get-tuple-element.26.refs_0_.refs_1_.refs_3_, f32[32,1024]{1,0:T(8,128)S(1)} %get-tuple-element.27.refs_1_.refs_2_.refs_4_, ...), custom_call_target="tpu_custom_call" | custom-call | flops 452984832 | bytes 786432 | tf_op jit(solution)/shard_map/pallas_call | solution.py:260
  5.9 0.0 copy-done.1
  6.0 0.0 copy-done.3
  6.0 0.0 copy-start
  6.0 0.3 shard_map.59.a_ref
  6.3 1.5 %collective-permute-start = (f32[32,1024]{1,0:T(8,128)S(1)}, f32[32,1024]{1,0:T(8,128)S(1)}, u32[]{:S(2)}, u32[]{:S(2)}) collective-permute-start(f32[32,1024]{1,0:T(8,128)S(1)} %get-tuple-element.31.refs_2_.refs_0_), channel_id=1, source_target_pairs={{0,16},{16,0},{32,48},{48,32},{64,80},{80,64},{96,112},{112,96},{1... | collective-permute-start | bytes 393224 | tf_op jit(solution)/shard_map/ppermute | solution.py:280
  7.9 0.0 collective-permute-done.4
  7.9 1.2 %collective-permute-start.5 = (f32[32,1024]{1,0:T(8,128)S(1)}, f32[32,1024]{1,0:T(8,128)S(1)}, u32[]{:S(2)}, u32[]{:S(2)}) collective-permute-start(f32[32,1024]{1,0:T(8,128)S(1)} %collective-permute-done.4), channel_id=1, source_target_pairs={{0,32},{16,112},{32,64},{48,16},{64,96},{80,48},{96,0},{112,80},{1... | collective-permute-start | bytes 393224 | tf_op jit(solution)/shard_map/ppermute | solution.py:282
  9.1 0.0 copy-done
  9.1 0.4 shard_map.60.b_ref
  9.5 1.5 %collective-permute-start.6 = (f32[32,1024]{1,0:T(8,128)S(1)}, f32[32,1024]{1,0:T(8,128)S(1)}, u32[]{:S(2)}, u32[]{:S(2)}) collective-permute-start(f32[32,1024]{1,0:T(8,128)S(1)} %get-tuple-element.38.refs_3_.refs_1_), channel_id=1, source_target_pairs={{0,16},{16,0},{32,48},{48,32},{64,80},{80,64},{96,112},{112,96},{1... | collective-permute-start | bytes 393224 | tf_op jit(solution)/shard_map/ppermute | solution.py:280
  11.0 0.0 collective-permute-done.2.refs_4_
  11.0 0.0 collective-permute-start.3
  11.0 1.4 %collective-permute-done.refs_3_ = f32[32,1024]{1,0:T(8,128)S(1)} collective-permute-done((f32[32,1024]{1,0:T(8,128)S(1)}, f32[32,1024]{1,0:T(8,128)S(1)}, u32[]{:S(2)}, u32[]{:S(2)}) %collective-permute-start) | collective-permute-done | bytes 131104 | tf_op jit(solution)/shard_map/ppermute | solution.py:280
  12.3 1.2 %collective-permute-start.1 = (f32[32,1024]{1,0:T(8,128)S(1)}, f32[32,1024]{1,0:T(8,128)S(1)}, u32[]{:S(2)}, u32[]{:S(2)}) collective-permute-start(f32[32,1024]{1,0:T(8,128)S(1)} %collective-permute-done.refs_3_), channel_id=1, source_target_pairs={{0,32},{16,112},{32,64},{48,16},{64,96},{80,48},{96,0},{112,80},{1... | collective-permute-start | bytes 393224 | tf_op jit(solution)/shard_map/ppermute | solution.py:282
  13.5 0.0 collective-permute-done.5.refs_0_.refs_2_
  13.5 1.2 %shard_map.61 = (f32[32,1024]{1,0:T(8,128)S(1)}, f32[32,1024]{1,0:T(8,128)S(1)}) custom-call(bf16[3,288,384]{2,1,0:T(8,128)(2,1)S(1)} %shard_map.55.w_ref, f32[32,1024]{1,0:T(8,128)S(1)} %collective-permute-done.5.refs_0_.refs_2_, f32[32,1024]{1,0:T(8,128)S(1)} %get-tuple-element.26.refs_0_.refs_1_.refs_3_, ...), custom_call_target="tpu_custom_call" | custom-call | flops 452984832 | bytes 917504 | tf_op jit(solution)/shard_map/pallas_call | solution.py:260
  14.8 0.0 collective-permute-done.6.refs_2_
  14.8 2.8 %shard_map.62 = (f32[32,1024]{1,0:T(8,128)S(1)}, f32[16,32,256]{2,1,0:T(8,128)S(1)}) custom-call(bf16[3,288,384]{2,1,0:T(8,128)(2,1)S(1)} %shard_map.55.w_ref, f32[32,1024]{1,0:T(8,128)S(1)} %get-tuple-element.31.refs_2_.refs_0_, f32[32,1024]{1,0:T(8,128)S(1)} %get-tuple-element.38.refs_3_.refs_1_, f32[32,1024]{1,0:T(8,128)S(1)} %collective-permute-done.6.refs_2_, ...), custom_call_target="tpu_custom_call" | custom-call | flops 1811939328 | bytes 1310720 | tf_op jit(solution)/shard_map/pallas_call | solution.py:260
  17.6 0.1 collective-permute-done.1.refs_0_
  17.7 0.0 collective-permute-done.3.refs_1_
  17.7 2.2 %shard_map.63 = f32[16,32,256]{2,1,0:T(8,128)S(1)} custom-call(bf16[3,288,384]{2,1,0:T(8,128)(2,1)S(1)} %shard_map.55.w_ref, f32[32,1024]{1,0:T(8,128)S(1)} %collective-permute-done.1.refs_0_, f32[32,1024]{1,0:T(8,128)S(1)} %collective-permute-done.3.refs_1_, f32[32,1024]{1,0:T(8,128)S(1)} %collective-permute-done.5.refs_0_.refs_2_, ...), custom_call_target="tpu_custom_call", output_to_operand_aliasing={{}: (10, {})} | custom-call | flops 1358954496 | bytes 1310720 | tf_op jit(solution)/shard_map/pallas_call | solution.py:260
  19.9 22.8 %all_to_all.10 = f32[16,32,256]{2,1,0:T(8,128)S(1)} all-to-all(f32[16,32,256]{2,1,0:T(8,128)S(1)} %shard_map.63), channel_id=1, replica_groups=mesh['depth'=8,'chan'=16] {'chan'}, dimensions={0} | all-to-all | bytes 1048576 | tf_op jit(solution)/shard_map/all_to_all | solution.py:296
  42.6 2.0 %shard_map.64 = f32[512,256]{1,0:T(8,128)S(1)} custom-call(f32[512,256]{1,0:T(8,128)S(1)} %bitcast.7, bf16[2048,512]{1,0:T(8,128)(2,1)S(1)} %shard_map.59.a_ref, bf16[1024,1024]{1,0:T(8,128)(2,1)S(1)} %shard_map.60.b_ref), custom_call_target="tpu_custom_call" | custom-call | flops 1610612736 | bytes 4194304 | tf_op jit(solution)/shard_map/pallas_call | solution.py:297
  44.7 15.0 %all_to_all.11.in_ref = f32[16,32,256]{2,1,0:T(8,128)S(1)} all-to-all(f32[16,32,256]{2,1,0:T(8,128)S(1)} %bitcast.8), channel_id=1, replica_groups=mesh['depth'=8,'chan'=16] {'chan'}, dimensions={0} | all-to-all | bytes 1048576 | tf_op jit(solution)/shard_map/all_to_all | solution.py:305
  59.7 1.2 %shard_map.65 = f32[32,4,1024]{2,1,0:T(4,128)} custom-call(f32[16,32,256]{2,1,0:T(8,128)S(1)} %all_to_all.11.in_ref), custom_call_target="tpu_custom_call" | custom-call | bytes 1048576 | tf_op jit(solution)/shard_map/pallas_call | solution.py:306
Async XLA Ops:
  1.3 2.7 %copy-start.2 = (f32[1,3,1,32,864]{4,3,2,1,0:T(8,128)S(1)}, f32[1,3,1,32,864]{4,3,2,1,0:T(8,128)}, u32[]{:S(2)}) copy-start(f32[1,3,1,32,864]{4,3,2,1,0:T(8,128)} %param.6) | copy-start | bytes 995332
  1.3 6.5 %collective-permute-start.4 = (f32[32,1024]{1,0:T(8,128)S(1)}, f32[32,1024]{1,0:T(8,128)S(1)}, u32[]{:S(2)}, u32[]{:S(2)}) collective-permute-start(f32[32,1024]{1,0:T(8,128)S(1)} %get-tuple-element.26.refs_0_.refs_1_.refs_3_), channel_id=1, source_target_pairs={{0,16},{16,0},{32,48},{48,32},{64,80},{80,64},{96,112},{112,96},{1... | collective-permute-start | bytes 393224 | tf_op jit(solution)/shard_map/ppermute | solution.py:244
  3.9 2.0 %copy-start.1 = (f32[1,1024,512]{2,1,0:T(8,128)S(1)}, f32[1,1024,512]{2,1,0:T(8,128)}, u32[]{:S(2)}) copy-start(f32[1,1024,512]{2,1,0:T(8,128)} %param.8) | copy-start | bytes 6291460
  4.0 2.0 %copy-start.3 = (f32[1,512]{1,0:T(1,128)S(1)}, f32[1,512]{1,0:T(1,128)}, u32[]{:S(2)}) copy-start(f32[1,512]{1,0:T(1,128)} %gain_ref.1) | copy-start | bytes 6148
  4.0 7.0 %collective-permute-start.2 = (f32[32,1024]{1,0:T(8,128)S(1)}, f32[32,1024]{1,0:T(8,128)S(1)}, u32[]{:S(2)}, u32[]{:S(2)}) collective-permute-start(f32[32,1024]{1,0:T(8,128)S(1)} %get-tuple-element.27.refs_1_.refs_2_.refs_4_), channel_id=1, source_target_pairs={{0,16},{16,0},{32,48},{48,32},{64,80},{80,64},{96,112},{112,96},{1... | collective-permute-start | bytes 393224 | tf_op jit(solution)/shard_map/ppermute | solution.py:244
  6.0 3.1 %copy-start = (f32[1,512,1024]{2,1,0:T(8,128)S(1)}, f32[1,512,1024]{2,1,0:T(8,128)}, u32[]{:S(2)}) copy-start(f32[1,512,1024]{2,1,0:T(8,128)} %param.9) | copy-start | bytes 6291460
  6.3 6.0 %collective-permute-start = (f32[32,1024]{1,0:T(8,128)S(1)}, f32[32,1024]{1,0:T(8,128)S(1)}, u32[]{:S(2)}, u32[]{:S(2)}) collective-permute-start(f32[32,1024]{1,0:T(8,128)S(1)} %get-tuple-element.31.refs_2_.refs_0_), channel_id=1, source_target_pairs={{0,16},{16,0},{32,48},{48,32},{64,80},{80,64},{96,112},{112,96},{1... | collective-permute-start | bytes 393224 | tf_op jit(solution)/shard_map/ppermute | solution.py:280
  7.9 5.7 %collective-permute-start.5 = (f32[32,1024]{1,0:T(8,128)S(1)}, f32[32,1024]{1,0:T(8,128)S(1)}, u32[]{:S(2)}, u32[]{:S(2)}) collective-permute-start(f32[32,1024]{1,0:T(8,128)S(1)} %collective-permute-done.4), channel_id=1, source_target_pairs={{0,32},{16,112},{32,64},{48,16},{64,96},{80,48},{96,0},{112,80},{1... | collective-permute-start | bytes 393224 | tf_op jit(solution)/shard_map/ppermute | solution.py:282
  9.5 5.3 %collective-permute-start.6 = (f32[32,1024]{1,0:T(8,128)S(1)}, f32[32,1024]{1,0:T(8,128)S(1)}, u32[]{:S(2)}, u32[]{:S(2)}) collective-permute-start(f32[32,1024]{1,0:T(8,128)S(1)} %get-tuple-element.38.refs_3_.refs_1_), channel_id=1, source_target_pairs={{0,16},{16,0},{32,48},{48,32},{64,80},{80,64},{96,112},{112,96},{1... | collective-permute-start | bytes 393224 | tf_op jit(solution)/shard_map/ppermute | solution.py:280
  11.0 6.7 %collective-permute-start.3 = (f32[32,1024]{1,0:T(8,128)S(1)}, f32[32,1024]{1,0:T(8,128)S(1)}, u32[]{:S(2)}, u32[]{:S(2)}) collective-permute-start(f32[32,1024]{1,0:T(8,128)S(1)} %collective-permute-done.2.refs_4_), channel_id=1, source_target_pairs={{0,32},{16,112},{32,64},{48,16},{64,96},{80,48},{96,0},{112,80},{1... | collective-permute-start | bytes 393224 | tf_op jit(solution)/shard_map/ppermute | solution.py:282
  12.3 5.3 %collective-permute-start.1 = (f32[32,1024]{1,0:T(8,128)S(1)}, f32[32,1024]{1,0:T(8,128)S(1)}, u32[]{:S(2)}, u32[]{:S(2)}) collective-permute-start(f32[32,1024]{1,0:T(8,128)S(1)} %collective-permute-done.refs_3_), channel_id=1, source_target_pairs={{0,32},{16,112},{32,64},{48,16},{64,96},{80,48},{96,0},{112,80},{1... | collective-permute-start | bytes 393224 | tf_op jit(solution)/shard_map/ppermute | solution.py:282

commit v10 on v9

--- a/solution.py
+++ b/solution.py
@@ -34,7 +34,9 @@
 
 
 def gelu(v):
-    return 0.5 * v * (1.0 + jnp.tanh(0.7978845608028654 * (v + 0.044715 * (v * v * v))))
+    half = 0.5 * v
+    slope = 0.7978845608028654
+    return half + half * jnp.tanh(v * (slope + (0.044715 * slope) * (v * v)))
 
 
 def turned_here():

time: 61 us -> 61 us (level)
  no operation moved by 1% of the time
where the time goes in v10:
time: 61 us; the launch traced here: 60.8 us
  blocking collectives  37.8 us (62%)
  Pallas kernels  13.7 us (22%)
  starting transfers between devices  7.76 us (13%)
  waiting for transfers between devices  1.49 us (2%)
    all_to_all x1, blocking collectives, per_device(): lax.all_to_all(mixed, 'chan', split_axis=0, concat_axis=0, tiled=True)  22.8 us
    all_to_all x1, blocking collectives, per_device(): lax.all_to_all(out.reshape(members, width, size), 'chan', split_axis=0, c...  15 us
    pallas_call x4, Pallas kernels, stage(): call(functools.partial(stage_kernel, given, work, kept, layers, len(more)...  7.1 us
    ppermute x2, starting transfers between devices, per_device(): there += [lax.ppermute(q, 'depth', pair) for q in (third, fourth)]  3.04 us
    ppermute x3, starting transfers between devices, per_device(): held[0, 2 - k] = lax.ppermute(there[k], 'depth', along)  2.41 us
    ppermute x2, starting transfers between devices, per_device(): there = [lax.ppermute(q, 'depth', pair) for q in own[:2]]  2.3 us
    pallas_call x1, Pallas kernels, per_device(): call(mlp_kernel, jax.ShapeDtypeStruct((channels, size), F32), 12 * hidden...  2 us
    ppermute x2, waiting for transfers between devices, per_device(): there += [lax.ppermute(q, 'depth', pair) for q in (third, fourth)]  1.37 us
  transfers between devices with their start and end apart: 7, of which 2 were waited for; matrix products, arithmetic and copies ran while one was open for 0% of the time, Pallas kernels for 11%

profile of v10, /device:TPU:1, one launch (start us, length us, event | category | flops | bytes accessed | tf_op | source)
XLA Modules:
  0.0 60.8 jit_solution(2004281166884275467)
XLA Ops:
  0.0 1.3 %shard_map.56 = (f32[32,4,1024]{2,1,0:T(4,128)S(1)}, f32[32,1024]{1,0:T(8,128)S(1)}) custom-call(f32[32,4,1024]{2,1,0:T(4,128)} %x_hbm.1), custom_call_target="tpu_custom_call" | custom-call | flops 1000000000 | bytes 1048576 | tf_op jit(solution)/shard_map/pallas_call | solution.py:236
  1.3 0.0 copy-start.2
  1.3 2.2 %collective-permute-start.4 = (f32[32,1024]{1,0:T(8,128)S(1)}, f32[32,1024]{1,0:T(8,128)S(1)}, u32[]{:S(2)}, u32[]{:S(2)}) collective-permute-start(f32[32,1024]{1,0:T(8,128)S(1)} %get-tuple-element.26.refs_0_.refs_1_.refs_3_), channel_id=1, source_target_pairs={{0,16},{16,0},{32,48},{48,32},{64,80},{80,64},{96,112},{112,96},{1... | collective-permute-start | bytes 393224 | tf_op jit(solution)/shard_map/ppermute | solution.py:246
  3.5 0.4 shard_map.57
  3.9 0.0 copy-start.1
  4.0 0.0 copy-start.3
  4.0 0.1 collective-permute-start.2
  4.1 0.0 copy-done.2
  4.1 0.9 %shard_map.55.w_ref = bf16[3,288,384]{2,1,0:T(8,128)(2,1)S(1)} custom-call(f32[3,32,864]{2,1,0:T(8,128)S(1)} %bitcast.9), custom_call_target="tpu_custom_call" | custom-call | bytes 663552 | tf_op jit(solution)/shard_map/pallas_call | solution.py:247
  5.0 0.9 %shard_map.58 = (f32[32,1024]{1,0:T(8,128)S(1)}, f32[32,1024]{1,0:T(8,128)S(1)}) custom-call(bf16[3,288,384]{2,1,0:T(8,128)(2,1)S(1)} %shard_map.55.w_ref, f32[32,1024]{1,0:T(8,128)S(1)} %get-tuple-element.26.refs_0_.refs_1_.refs_3_, f32[32,1024]{1,0:T(8,128)S(1)} %get-tuple-element.27.refs_1_.refs_2_.refs_4_, ...), custom_call_target="tpu_custom_call" | custom-call | flops 452984832 | bytes 786432 | tf_op jit(solution)/shard_map/pallas_call | solution.py:262
  5.9 0.0 copy-done.1
  6.0 0.0 copy-done.3
  6.0 0.0 copy-start
  6.0 0.3 shard_map.59.a_ref
  6.3 1.5 %collective-permute-start = (f32[32,1024]{1,0:T(8,128)S(1)}, f32[32,1024]{1,0:T(8,128)S(1)}, u32[]{:S(2)}, u32[]{:S(2)}) collective-permute-start(f32[32,1024]{1,0:T(8,128)S(1)} %get-tuple-element.31.refs_2_.refs_0_), channel_id=1, source_target_pairs={{0,16},{16,0},{32,48},{48,32},{64,80},{80,64},{96,112},{112,96},{1... | collective-permute-start | bytes 393224 | tf_op jit(solution)/shard_map/ppermute | solution.py:282
  7.8 0.0 collective-permute-done.4
  7.8 1.2 %collective-permute-start.5 = (f32[32,1024]{1,0:T(8,128)S(1)}, f32[32,1024]{1,0:T(8,128)S(1)}, u32[]{:S(2)}, u32[]{:S(2)}) collective-permute-start(f32[32,1024]{1,0:T(8,128)S(1)} %collective-permute-done.4), channel_id=1, source_target_pairs={{0,32},{16,112},{32,64},{48,16},{64,96},{80,48},{96,0},{112,80},{1... | collective-permute-start | bytes 393224 | tf_op jit(solution)/shard_map/ppermute | solution.py:284
  9.1 0.0 copy-done
  9.1 0.4 shard_map.60.b_ref
  9.5 1.5 %collective-permute-start.6 = (f32[32,1024]{1,0:T(8,128)S(1)}, f32[32,1024]{1,0:T(8,128)S(1)}, u32[]{:S(2)}, u32[]{:S(2)}) collective-permute-start(f32[32,1024]{1,0:T(8,128)S(1)} %get-tuple-element.38.refs_3_.refs_1_), channel_id=1, source_target_pairs={{0,16},{16,0},{32,48},{48,32},{64,80},{80,64},{96,112},{112,96},{1... | collective-permute-start | bytes 393224 | tf_op jit(solution)/shard_map/ppermute | solution.py:282
  11.0 0.0 collective-permute-done.2.refs_4_
  11.0 0.0 collective-permute-start.3
  11.0 1.4 %collective-permute-done.refs_3_ = f32[32,1024]{1,0:T(8,128)S(1)} collective-permute-done((f32[32,1024]{1,0:T(8,128)S(1)}, f32[32,1024]{1,0:T(8,128)S(1)}, u32[]{:S(2)}, u32[]{:S(2)}) %collective-permute-start) | collective-permute-done | bytes 131104 | tf_op jit(solution)/shard_map/ppermute | solution.py:282
  12.3 1.2 %collective-permute-start.1 = (f32[32,1024]{1,0:T(8,128)S(1)}, f32[32,1024]{1,0:T(8,128)S(1)}, u32[]{:S(2)}, u32[]{:S(2)}) collective-permute-start(f32[32,1024]{1,0:T(8,128)S(1)} %collective-permute-done.refs_3_), channel_id=1, source_target_pairs={{0,32},{16,112},{32,64},{48,16},{64,96},{80,48},{96,0},{112,80},{1... | collective-permute-start | bytes 393224 | tf_op jit(solution)/shard_map/ppermute | solution.py:284
  13.5 0.0 collective-permute-done.5.refs_0_.refs_2_
  13.5 1.2 %shard_map.61 = (f32[32,1024]{1,0:T(8,128)S(1)}, f32[32,1024]{1,0:T(8,128)S(1)}) custom-call(bf16[3,288,384]{2,1,0:T(8,128)(2,1)S(1)} %shard_map.55.w_ref, f32[32,1024]{1,0:T(8,128)S(1)} %collective-permute-done.5.refs_0_.refs_2_, f32[32,1024]{1,0:T(8,128)S(1)} %get-tuple-element.26.refs_0_.refs_1_.refs_3_, ...), custom_call_target="tpu_custom_call" | custom-call | flops 452984832 | bytes 917504 | tf_op jit(solution)/shard_map/pallas_call | solution.py:262
  14.7 0.0 collective-permute-done.6.refs_2_
  14.8 2.8 %shard_map.62 = (f32[32,1024]{1,0:T(8,128)S(1)}, f32[16,32,256]{2,1,0:T(8,128)S(1)}) custom-call(bf16[3,288,384]{2,1,0:T(8,128)(2,1)S(1)} %shard_map.55.w_ref, f32[32,1024]{1,0:T(8,128)S(1)} %get-tuple-element.31.refs_2_.refs_0_, f32[32,1024]{1,0:T(8,128)S(1)} %get-tuple-element.38.refs_3_.refs_1_, f32[32,1024]{1,0:T(8,128)S(1)} %collective-permute-done.6.refs_2_, ...), custom_call_target="tpu_custom_call" | custom-call | flops 1811939328 | bytes 1310720 | tf_op jit(solution)/shard_map/pallas_call | solution.py:262
  17.6 0.1 collective-permute-done.1.refs_0_
  17.7 0.0 collective-permute-done.3.refs_1_
  17.7 2.2 %shard_map.63 = f32[16,32,256]{2,1,0:T(8,128)S(1)} custom-call(bf16[3,288,384]{2,1,0:T(8,128)(2,1)S(1)} %shard_map.55.w_ref, f32[32,1024]{1,0:T(8,128)S(1)} %collective-permute-done.1.refs_0_, f32[32,1024]{1,0:T(8,128)S(1)} %collective-permute-done.3.refs_1_, f32[32,1024]{1,0:T(8,128)S(1)} %collective-permute-done.5.refs_0_.refs_2_, ...), custom_call_target="tpu_custom_call", output_to_operand_aliasing={{}: (10, {})} | custom-call | flops 1358954496 | bytes 1310720 | tf_op jit(solution)/shard_map/pallas_call | solution.py:262
  19.9 22.8 %all_to_all.10 = f32[16,32,256]{2,1,0:T(8,128)S(1)} all-to-all(f32[16,32,256]{2,1,0:T(8,128)S(1)} %shard_map.63), channel_id=1, replica_groups=mesh['depth'=8,'chan'=16] {'chan'}, dimensions={0} | all-to-all | bytes 1048576 | tf_op jit(solution)/shard_map/all_to_all | solution.py:298
  42.6 2.0 %shard_map.64 = f32[512,256]{1,0:T(8,128)S(1)} custom-call(f32[512,256]{1,0:T(8,128)S(1)} %bitcast.7, bf16[2048,512]{1,0:T(8,128)(2,1)S(1)} %shard_map.59.a_ref, bf16[1024,1024]{1,0:T(8,128)(2,1)S(1)} %shard_map.60.b_ref), custom_call_target="tpu_custom_call" | custom-call | flops 1610612736 | bytes 4194304 | tf_op jit(solution)/shard_map/pallas_call | solution.py:299
  44.6 15.0 %all_to_all.11.in_ref = f32[16,32,256]{2,1,0:T(8,128)S(1)} all-to-all(f32[16,32,256]{2,1,0:T(8,128)S(1)} %bitcast.8), channel_id=1, replica_groups=mesh['depth'=8,'chan'=16] {'chan'}, dimensions={0} | all-to-all | bytes 1048576 | tf_op jit(solution)/shard_map/all_to_all | solution.py:307
  59.6 1.2 %shard_map.65 = f32[32,4,1024]{2,1,0:T(4,128)} custom-call(f32[16,32,256]{2,1,0:T(8,128)S(1)} %all_to_all.11.in_ref), custom_call_target="tpu_custom_call" | custom-call | bytes 1048576 | tf_op jit(solution)/shard_map/pallas_call | solution.py:308
Async XLA Ops:
  1.3 2.7 %copy-start.2 = (f32[1,3,1,32,864]{4,3,2,1,0:T(8,128)S(1)}, f32[1,3,1,32,864]{4,3,2,1,0:T(8,128)}, u32[]{:S(2)}) copy-start(f32[1,3,1,32,864]{4,3,2,1,0:T(8,128)} %param.6) | copy-start | bytes 995332
  1.3 6.5 %collective-permute-start.4 = (f32[32,1024]{1,0:T(8,128)S(1)}, f32[32,1024]{1,0:T(8,128)S(1)}, u32[]{:S(2)}, u32[]{:S(2)}) collective-permute-start(f32[32,1024]{1,0:T(8,128)S(1)} %get-tuple-element.26.refs_0_.refs_1_.refs_3_), channel_id=1, source_target_pairs={{0,16},{16,0},{32,48},{48,32},{64,80},{80,64},{96,112},{112,96},{1... | collective-permute-start | bytes 393224 | tf_op jit(solution)/shard_map/ppermute | solution.py:246
  3.9 2.0 %copy-start.1 = (f32[1,1024,512]{2,1,0:T(8,128)S(1)}, f32[1,1024,512]{2,1,0:T(8,128)}, u32[]{:S(2)}) copy-start(f32[1,1024,512]{2,1,0:T(8,128)} %param.8) | copy-start | bytes 6291460
  4.0 2.0 %copy-start.3 = (f32[1,512]{1,0:T(1,128)S(1)}, f32[1,512]{1,0:T(1,128)}, u32[]{:S(2)}) copy-start(f32[1,512]{1,0:T(1,128)} %gain_ref.1) | copy-start | bytes 6148
  4.0 7.0 %collective-permute-start.2 = (f32[32,1024]{1,0:T(8,128)S(1)}, f32[32,1024]{1,0:T(8,128)S(1)}, u32[]{:S(2)}, u32[]{:S(2)}) collective-permute-start(f32[32,1024]{1,0:T(8,128)S(1)} %get-tuple-element.27.refs_1_.refs_2_.refs_4_), channel_id=1, source_target_pairs={{0,16},{16,0},{32,48},{48,32},{64,80},{80,64},{96,112},{112,96},{1... | collective-permute-start | bytes 393224 | tf_op jit(solution)/shard_map/ppermute | solution.py:246
  6.0 3.1 %copy-start = (f32[1,512,1024]{2,1,0:T(8,128)S(1)}, f32[1,512,1024]{2,1,0:T(8,128)}, u32[]{:S(2)}) copy-start(f32[1,512,1024]{2,1,0:T(8,128)} %param.9) | copy-start | bytes 6291460
  6.3 6.0 %collective-permute-start = (f32[32,1024]{1,0:T(8,128)S(1)}, f32[32,1024]{1,0:T(8,128)S(1)}, u32[]{:S(2)}, u32[]{:S(2)}) collective-permute-start(f32[32,1024]{1,0:T(8,128)S(1)} %get-tuple-element.31.refs_2_.refs_0_), channel_id=1, source_target_pairs={{0,16},{16,0},{32,48},{48,32},{64,80},{80,64},{96,112},{112,96},{1... | collective-permute-start | bytes 393224 | tf_op jit(solution)/shard_map/ppermute | solution.py:282
  7.8 5.7 %collective-permute-start.5 = (f32[32,1024]{1,0:T(8,128)S(1)}, f32[32,1024]{1,0:T(8,128)S(1)}, u32[]{:S(2)}, u32[]{:S(2)}) collective-permute-start(f32[32,1024]{1,0:T(8,128)S(1)} %collective-permute-done.4), channel_id=1, source_target_pairs={{0,32},{16,112},{32,64},{48,16},{64,96},{80,48},{96,0},{112,80},{1... | collective-permute-start | bytes 393224 | tf_op jit(solution)/shard_map/ppermute | solution.py:284
  9.5 5.3 %collective-permute-start.6 = (f32[32,1024]{1,0:T(8,128)S(1)}, f32[32,1024]{1,0:T(8,128)S(1)}, u32[]{:S(2)}, u32[]{:S(2)}) collective-permute-start(f32[32,1024]{1,0:T(8,128)S(1)} %get-tuple-element.38.refs_3_.refs_1_), channel_id=1, source_target_pairs={{0,16},{16,0},{32,48},{48,32},{64,80},{80,64},{96,112},{112,96},{1... | collective-permute-start | bytes 393224 | tf_op jit(solution)/shard_map/ppermute | solution.py:282
  11.0 6.7 %collective-permute-start.3 = (f32[32,1024]{1,0:T(8,128)S(1)}, f32[32,1024]{1,0:T(8,128)S(1)}, u32[]{:S(2)}, u32[]{:S(2)}) collective-permute-start(f32[32,1024]{1,0:T(8,128)S(1)} %collective-permute-done.2.refs_4_), channel_id=1, source_target_pairs={{0,32},{16,112},{32,64},{48,16},{64,96},{80,48},{96,0},{112,80},{1... | collective-permute-start | bytes 393224 | tf_op jit(solution)/shard_map/ppermute | solution.py:284
  12.3 5.3 %collective-permute-start.1 = (f32[32,1024]{1,0:T(8,128)S(1)}, f32[32,1024]{1,0:T(8,128)S(1)}, u32[]{:S(2)}, u32[]{:S(2)}) collective-permute-start(f32[32,1024]{1,0:T(8,128)S(1)} %collective-permute-done.refs_3_), channel_id=1, source_target_pairs={{0,32},{16,112},{32,64},{48,16},{64,96},{80,48},{96,0},{112,80},{1... | collective-permute-start | bytes 393224 | tf_op jit(solution)/shard_map/ppermute | solution.py:284

commit v11 on v10

--- a/solution.py
+++ b/solution.py
@@ -167,16 +167,18 @@
     refs = refs[resumes:]
     where = dict(zip(given, ins, strict=True))
     kept_at = dict(zip(kept, refs[: len(kept)], strict=True))
-    held = {key: halves(ref[...]) for key, ref in where.items()}
+    width = w_ref.shape[1] // 9
+    held = {key: (ref[:width], ref[width:]) if key[0] else halves(ref[...]) for key, ref in where.items()}
     for n, (layer, place) in enumerate(work):
         total = conv_plane(w_ref[layer - 1], [held[layer - 1, place + d] for d in (-1, 0, 1)], acc_ref.at[n % 2])
         if layer == layers:
             store_cells(refs[len(kept)], place - first, where[0, place][...] + total)
             continue
-        total = gelu(total)
-        held[layer, place] = halves(total)
+        hi, lo = halves(gelu(total))
+        held[layer, place] = hi, lo
         if (layer, place) in kept_at:
-            kept_at[layer, place][...] = total
+            kept_at[layer, place][:width] = hi
+            kept_at[layer, place][width:] = lo
 
 
 def mlp_kernel(y_ref, a_ref, b_ref, out_ref, hh_ref, hl_ref):
@@ -255,7 +257,7 @@
     held = {(0, 3 + k): v for k, v in enumerate(own)}
 
     def stage(given, work, kept, finished=None):
-        outs = (plane,) * len(kept)
+        outs = (jax.ShapeDtypeStruct((2 * width, cells), BF16),) * len(kept)
         if any(layer == layers for layer, _ in work):
             outs += (jax.ShapeDtypeStruct((members, width, size), F32),)
         more = [] if finished is None else [finished]

time: 61 us -> 61 us (level)
  no operation moved by 1% of the time
where the time goes in v11:
time: 61 us; the launch traced here: 60.8 us
  blocking collectives  37.7 us (62%)
  Pallas kernels  13.7 us (22%)
  starting transfers between devices  7.76 us (13%)
  waiting for transfers between devices  1.49 us (2%)
    all_to_all x1, blocking collectives, per_device(): lax.all_to_all(mixed, 'chan', split_axis=0, concat_axis=0, tiled=True)  22.8 us
    all_to_all x1, blocking collectives, per_device(): lax.all_to_all(out.reshape(members, width, size), 'chan', split_axis=0, c...  15 us
    pallas_call x4, Pallas kernels, stage(): call(functools.partial(stage_kernel, given, work, kept, layers, len(more)...  7.1 us
    ppermute x2, starting transfers between devices, per_device(): there += [lax.ppermute(q, 'depth', pair) for q in (third, fourth)]  3.04 us
    ppermute x3, starting transfers between devices, per_device(): held[0, 2 - k] = lax.ppermute(there[k], 'depth', along)  2.41 us
    ppermute x2, starting transfers between devices, per_device(): there = [lax.ppermute(q, 'depth', pair) for q in own[:2]]  2.3 us
    pallas_call x1, Pallas kernels, per_device(): call(mlp_kernel, jax.ShapeDtypeStruct((channels, size), F32), 12 * hidden...  2.01 us
    ppermute x2, waiting for transfers between devices, per_device(): there += [lax.ppermute(q, 'depth', pair) for q in (third, fourth)]  1.36 us
  transfers between devices with their start and end apart: 7, of which 2 were waited for; matrix products, arithmetic and copies ran while one was open for 0% of the time, Pallas kernels for 11%

profile of v11, /device:TPU:1, one launch (start us, length us, event | category | flops | bytes accessed | tf_op | source)
XLA Modules:
  0.0 60.8 jit_solution(7973872483040493007)
XLA Ops:
  0.0 1.3 %shard_map.56 = (f32[32,4,1024]{2,1,0:T(4,128)S(1)}, f32[32,1024]{1,0:T(8,128)S(1)}) custom-call(f32[32,4,1024]{2,1,0:T(4,128)} %x_hbm.1), custom_call_target="tpu_custom_call" | custom-call | flops 1000000000 | bytes 1048576 | tf_op jit(solution)/shard_map/pallas_call | solution.py:238
  1.3 0.0 copy-start.2
  1.3 2.2 %collective-permute-start.4 = (f32[32,1024]{1,0:T(8,128)S(1)}, f32[32,1024]{1,0:T(8,128)S(1)}, u32[]{:S(2)}, u32[]{:S(2)}) collective-permute-start(f32[32,1024]{1,0:T(8,128)S(1)} %get-tuple-element.26.refs_0_.refs_1_.refs_3_), channel_id=1, source_target_pairs={{0,16},{16,0},{32,48},{48,32},{64,80},{80,64},{96,112},{112,96},{1... | collective-permute-start | bytes 393224 | tf_op jit(solution)/shard_map/ppermute | solution.py:248
  3.5 0.4 shard_map.57
  3.9 0.0 copy-start.1
  4.0 0.0 copy-start.3
  4.0 0.1 collective-permute-start.2
  4.1 0.0 copy-done.2
  4.1 0.9 %shard_map.55.w_ref = bf16[3,288,384]{2,1,0:T(8,128)(2,1)S(1)} custom-call(f32[3,32,864]{2,1,0:T(8,128)S(1)} %bitcast.9), custom_call_target="tpu_custom_call" | custom-call | bytes 663552 | tf_op jit(solution)/shard_map/pallas_call | solution.py:249
  5.0 0.9 %shard_map.58 = (bf16[64,1024]{1,0:T(8,128)(2,1)S(1)}, bf16[64,1024]{1,0:T(8,128)(2,1)S(1)}) custom-call(bf16[3,288,384]{2,1,0:T(8,128)(2,1)S(1)} %shard_map.55.w_ref, f32[32,1024]{1,0:T(8,128)S(1)} %get-tuple-element.26.refs_0_.refs_1_.refs_3_, f32[32,1024]{1,0:T(8,128)S(1)} %get-tuple-element.27.refs_1_.refs_2_.refs_4_, ...), custom_call_target="tpu_custom_call" | custom-call | flops 452984832 | bytes 786432 | tf_op jit(solution)/shard_map/pallas_call | solution.py:264
  6.0 0.0 copy-done.1
  6.0 0.0 copy-done.3
  6.0 0.0 copy-start
  6.0 0.3 shard_map.59.a_ref
  6.3 1.5 %collective-permute-start = (f32[32,1024]{1,0:T(8,128)S(1)}, f32[32,1024]{1,0:T(8,128)S(1)}, u32[]{:S(2)}, u32[]{:S(2)}) collective-permute-start(f32[32,1024]{1,0:T(8,128)S(1)} %get-tuple-element.31.refs_2_.refs_0_), channel_id=1, source_target_pairs={{0,16},{16,0},{32,48},{48,32},{64,80},{80,64},{96,112},{112,96},{1... | collective-permute-start | bytes 393224 | tf_op jit(solution)/shard_map/ppermute | solution.py:284
  7.9 0.0 collective-permute-done.4
  7.9 1.2 %collective-permute-start.5 = (f32[32,1024]{1,0:T(8,128)S(1)}, f32[32,1024]{1,0:T(8,128)S(1)}, u32[]{:S(2)}, u32[]{:S(2)}) collective-permute-start(f32[32,1024]{1,0:T(8,128)S(1)} %collective-permute-done.4), channel_id=1, source_target_pairs={{0,32},{16,112},{32,64},{48,16},{64,96},{80,48},{96,0},{112,80},{1... | collective-permute-start | bytes 393224 | tf_op jit(solution)/shard_map/ppermute | solution.py:286
  9.1 0.0 copy-done
  9.1 0.4 shard_map.60.b_ref
  9.5 1.5 %collective-permute-start.6 = (f32[32,1024]{1,0:T(8,128)S(1)}, f32[32,1024]{1,0:T(8,128)S(1)}, u32[]{:S(2)}, u32[]{:S(2)}) collective-permute-start(f32[32,1024]{1,0:T(8,128)S(1)} %get-tuple-element.38.refs_3_.refs_1_), channel_id=1, source_target_pairs={{0,16},{16,0},{32,48},{48,32},{64,80},{80,64},{96,112},{112,96},{1... | collective-permute-start | bytes 393224 | tf_op jit(solution)/shard_map/ppermute | solution.py:284
  11.0 0.0 collective-permute-done.2.refs_4_
  11.0 0.0 collective-permute-start.3
  11.0 1.4 %collective-permute-done.refs_3_ = f32[32,1024]{1,0:T(8,128)S(1)} collective-permute-done((f32[32,1024]{1,0:T(8,128)S(1)}, f32[32,1024]{1,0:T(8,128)S(1)}, u32[]{:S(2)}, u32[]{:S(2)}) %collective-permute-start) | collective-permute-done | bytes 131104 | tf_op jit(solution)/shard_map/ppermute | solution.py:284
  12.3 1.2 %collective-permute-start.1 = (f32[32,1024]{1,0:T(8,128)S(1)}, f32[32,1024]{1,0:T(8,128)S(1)}, u32[]{:S(2)}, u32[]{:S(2)}) collective-permute-start(f32[32,1024]{1,0:T(8,128)S(1)} %collective-permute-done.refs_3_), channel_id=1, source_target_pairs={{0,32},{16,112},{32,64},{48,16},{64,96},{80,48},{96,0},{112,80},{1... | collective-permute-start | bytes 393224 | tf_op jit(solution)/shard_map/ppermute | solution.py:286
  13.5 0.0 collective-permute-done.5.refs_0_.refs_2_
  13.5 1.2 %shard_map.61 = (bf16[64,1024]{1,0:T(8,128)(2,1)S(1)}, bf16[64,1024]{1,0:T(8,128)(2,1)S(1)}) custom-call(bf16[3,288,384]{2,1,0:T(8,128)(2,1)S(1)} %shard_map.55.w_ref, f32[32,1024]{1,0:T(8,128)S(1)} %collective-permute-done.5.refs_0_.refs_2_, f32[32,1024]{1,0:T(8,128)S(1)} %get-tuple-element.26.refs_0_.refs_1_.refs_3_, ...), custom_call_target="tpu_custom_call" | custom-call | flops 452984832 | bytes 917504 | tf_op jit(solution)/shard_map/pallas_call | solution.py:264
  14.8 0.0 collective-permute-done.6.refs_2_
  14.8 2.8 %shard_map.62 = (bf16[64,1024]{1,0:T(8,128)(2,1)S(1)}, f32[16,32,256]{2,1,0:T(8,128)S(1)}) custom-call(bf16[3,288,384]{2,1,0:T(8,128)(2,1)S(1)} %shard_map.55.w_ref, f32[32,1024]{1,0:T(8,128)S(1)} %get-tuple-element.31.refs_2_.refs_0_, f32[32,1024]{1,0:T(8,128)S(1)} %get-tuple-element.38.refs_3_.refs_1_, f32[32,1024]{1,0:T(8,128)S(1)} %collective-permute-done.6.refs_2_, ...), custom_call_target="tpu_custom_call" | custom-call | flops 1811939328 | bytes 1310720 | tf_op jit(solution)/shard_map/pallas_call | solution.py:264
  17.6 0.1 collective-permute-done.1.refs_0_
  17.7 0.0 collective-permute-done.3.refs_1_
  17.7 2.2 %shard_map.63 = f32[16,32,256]{2,1,0:T(8,128)S(1)} custom-call(bf16[3,288,384]{2,1,0:T(8,128)(2,1)S(1)} %shard_map.55.w_ref, f32[32,1024]{1,0:T(8,128)S(1)} %collective-permute-done.1.refs_0_, f32[32,1024]{1,0:T(8,128)S(1)} %collective-permute-done.3.refs_1_, f32[32,1024]{1,0:T(8,128)S(1)} %collective-permute-done.5.refs_0_.refs_2_, ...), custom_call_target="tpu_custom_call", output_to_operand_aliasing={{}: (10, {})} | custom-call | flops 1358954496 | bytes 1310720 | tf_op jit(solution)/shard_map/pallas_call | solution.py:264
  19.9 22.8 %all_to_all.10 = f32[16,32,256]{2,1,0:T(8,128)S(1)} all-to-all(f32[16,32,256]{2,1,0:T(8,128)S(1)} %shard_map.63), channel_id=1, replica_groups=mesh['depth'=8,'chan'=16] {'chan'}, dimensions={0} | all-to-all | bytes 1048576 | tf_op jit(solution)/shard_map/all_to_all | solution.py:300
  42.6 2.0 %shard_map.64 = f32[512,256]{1,0:T(8,128)S(1)} custom-call(f32[512,256]{1,0:T(8,128)S(1)} %bitcast.7, bf16[2048,512]{1,0:T(8,128)(2,1)S(1)} %shard_map.59.a_ref, bf16[1024,1024]{1,0:T(8,128)(2,1)S(1)} %shard_map.60.b_ref), custom_call_target="tpu_custom_call" | custom-call | flops 1610612736 | bytes 4194304 | tf_op jit(solution)/shard_map/pallas_call | solution.py:301
  44.6 15.0 %all_to_all.11.in_ref = f32[16,32,256]{2,1,0:T(8,128)S(1)} all-to-all(f32[16,32,256]{2,1,0:T(8,128)S(1)} %bitcast.8), channel_id=1, replica_groups=mesh['depth'=8,'chan'=16] {'chan'}, dimensions={0} | all-to-all | bytes 1048576 | tf_op jit(solution)/shard_map/all_to_all | solution.py:309
  59.6 1.2 %shard_map.65 = f32[32,4,1024]{2,1,0:T(4,128)} custom-call(f32[16,32,256]{2,1,0:T(8,128)S(1)} %all_to_all.11.in_ref), custom_call_target="tpu_custom_call" | custom-call | bytes 1048576 | tf_op jit(solution)/shard_map/pallas_call | solution.py:310
Async XLA Ops:
  1.3 2.7 %copy-start.2 = (f32[1,3,1,32,864]{4,3,2,1,0:T(8,128)S(1)}, f32[1,3,1,32,864]{4,3,2,1,0:T(8,128)}, u32[]{:S(2)}) copy-start(f32[1,3,1,32,864]{4,3,2,1,0:T(8,128)} %param.6) | copy-start | bytes 995332
  1.3 6.5 %collective-permute-start.4 = (f32[32,1024]{1,0:T(8,128)S(1)}, f32[32,1024]{1,0:T(8,128)S(1)}, u32[]{:S(2)}, u32[]{:S(2)}) collective-permute-start(f32[32,1024]{1,0:T(8,128)S(1)} %get-tuple-element.26.refs_0_.refs_1_.refs_3_), channel_id=1, source_target_pairs={{0,16},{16,0},{32,48},{48,32},{64,80},{80,64},{96,112},{112,96},{1... | collective-permute-start | bytes 393224 | tf_op jit(solution)/shard_map/ppermute | solution.py:248
  3.9 2.0 %copy-start.1 = (f32[1,1024,512]{2,1,0:T(8,128)S(1)}, f32[1,1024,512]{2,1,0:T(8,128)}, u32[]{:S(2)}) copy-start(f32[1,1024,512]{2,1,0:T(8,128)} %param.8) | copy-start | bytes 6291460
  4.0 2.0 %copy-start.3 = (f32[1,512]{1,0:T(1,128)S(1)}, f32[1,512]{1,0:T(1,128)}, u32[]{:S(2)}) copy-start(f32[1,512]{1,0:T(1,128)} %gain_ref.1) | copy-start | bytes 6148
  4.0 7.0 %collective-permute-start.2 = (f32[32,1024]{1,0:T(8,128)S(1)}, f32[32,1024]{1,0:T(8,128)S(1)}, u32[]{:S(2)}, u32[]{:S(2)}) collective-permute-start(f32[32,1024]{1,0:T(8,128)S(1)} %get-tuple-element.27.refs_1_.refs_2_.refs_4_), channel_id=1, source_target_pairs={{0,16},{16,0},{32,48},{48,32},{64,80},{80,64},{96,112},{112,96},{1... | collective-permute-start | bytes 393224 | tf_op jit(solution)/shard_map/ppermute | solution.py:248
  6.0 3.1 %copy-start = (f32[1,512,1024]{2,1,0:T(8,128)S(1)}, f32[1,512,1024]{2,1,0:T(8,128)}, u32[]{:S(2)}) copy-start(f32[1,512,1024]{2,1,0:T(8,128)} %param.9) | copy-start | bytes 6291460
  6.3 6.0 %collective-permute-start = (f32[32,1024]{1,0:T(8,128)S(1)}, f32[32,1024]{1,0:T(8,128)S(1)}, u32[]{:S(2)}, u32[]{:S(2)}) collective-permute-start(f32[32,1024]{1,0:T(8,128)S(1)} %get-tuple-element.31.refs_2_.refs_0_), channel_id=1, source_target_pairs={{0,16},{16,0},{32,48},{48,32},{64,80},{80,64},{96,112},{112,96},{1... | collective-permute-start | bytes 393224 | tf_op jit(solution)/shard_map/ppermute | solution.py:284
  7.9 5.7 %collective-permute-start.5 = (f32[32,1024]{1,0:T(8,128)S(1)}, f32[32,1024]{1,0:T(8,128)S(1)}, u32[]{:S(2)}, u32[]{:S(2)}) collective-permute-start(f32[32,1024]{1,0:T(8,128)S(1)} %collective-permute-done.4), channel_id=1, source_target_pairs={{0,32},{16,112},{32,64},{48,16},{64,96},{80,48},{96,0},{112,80},{1... | collective-permute-start | bytes 393224 | tf_op jit(solution)/shard_map/ppermute | solution.py:286
  9.5 5.3 %collective-permute-start.6 = (f32[32,1024]{1,0:T(8,128)S(1)}, f32[32,1024]{1,0:T(8,128)S(1)}, u32[]{:S(2)}, u32[]{:S(2)}) collective-permute-start(f32[32,1024]{1,0:T(8,128)S(1)} %get-tuple-element.38.refs_3_.refs_1_), channel_id=1, source_target_pairs={{0,16},{16,0},{32,48},{48,32},{64,80},{80,64},{96,112},{112,96},{1... | collective-permute-start | bytes 393224 | tf_op jit(solution)/shard_map/ppermute | solution.py:284
  11.0 6.7 %collective-permute-start.3 = (f32[32,1024]{1,0:T(8,128)S(1)}, f32[32,1024]{1,0:T(8,128)S(1)}, u32[]{:S(2)}, u32[]{:S(2)}) collective-permute-start(f32[32,1024]{1,0:T(8,128)S(1)} %collective-permute-done.2.refs_4_), channel_id=1, source_target_pairs={{0,32},{16,112},{32,64},{48,16},{64,96},{80,48},{96,0},{112,80},{1... | collective-permute-start | bytes 393224 | tf_op jit(solution)/shard_map/ppermute | solution.py:286
  12.3 5.3 %collective-permute-start.1 = (f32[32,1024]{1,0:T(8,128)S(1)}, f32[32,1024]{1,0:T(8,128)S(1)}, u32[]{:S(2)}, u32[]{:S(2)}) collective-permute-start(f32[32,1024]{1,0:T(8,128)S(1)} %collective-permute-done.refs_3_), channel_id=1, source_target_pairs={{0,32},{16,112},{32,64},{48,16},{64,96},{80,48},{96,0},{112,80},{1... | collective-permute-start | bytes 393224 | tf_op jit(solution)/shard_map/ppermute | solution.py:286

commit v12 on v8

--- a/solution.py
+++ b/solution.py
@@ -34,7 +34,9 @@
 
 
 def gelu(v):
-    return 0.5 * v * (1.0 + jnp.tanh(0.7978845608028654 * (v + 0.044715 * (v * v * v))))
+    half = 0.5 * v
+    slope = 0.7978845608028654
+    return half + half * jnp.tanh(v * (slope + (0.044715 * slope) * (v * v)))
 
 
 def turned_here():

time: 61 us -> 61 us (level)
  transfers between devices with their start and end apart: 7 -> 7, of which waited for: 2 -> 2; matrix products, arithmetic and copies ran while one was open for 0% -> 0% of each run, Pallas kernels for 12% -> 11%
where the time goes in v12:
time: 61 us; the launch traced here: 60.7 us
  blocking collectives  37.8 us (62%)
  Pallas kernels  12.5 us (20%)
  starting transfers between devices  7.75 us (13%)
  waiting for transfers between devices  1.49 us (2%)
  local copies, waits for them, and re-layouts  1.07 us (2%)
    all_to_all x1, blocking collectives, per_device(): lax.all_to_all(mixed, 'chan', split_axis=0, concat_axis=0, tiled=True)  22.8 us
    all_to_all x1, blocking collectives, per_device(): lax.all_to_all(out.reshape(members, width, size), 'chan', split_axis=0, c...  15 us
    pallas_call x4, Pallas kernels, stage(): call(functools.partial(stage_kernel, given, work, kept, layers, len(more)...  7.1 us
    ppermute x2, starting transfers between devices, per_device(): there += [lax.ppermute(q, 'depth', pair) for q in (third, fourth)]  3.03 us
    ppermute x3, starting transfers between devices, per_device(): held[0, 2 - k] = lax.ppermute(there[k], 'depth', along)  2.41 us
    ppermute x2, starting transfers between devices, per_device(): there = [lax.ppermute(q, 'depth', pair) for q in own[:2]]  2.3 us
    pallas_call x1, Pallas kernels, per_device(): call(mlp_kernel, jax.ShapeDtypeStruct((channels, size), F32), 12 * hidden...  2.01 us
    ppermute x2, waiting for transfers between devices, per_device(): there += [lax.ppermute(q, 'depth', pair) for q in (third, fourth)]  1.37 us
  transfers between devices with their start and end apart: 7, of which 2 were waited for; matrix products, arithmetic and copies ran while one was open for 0% of the time, Pallas kernels for 11%

profile of v12, /device:TPU:1, one launch (start us, length us, event | category | flops | bytes accessed | tf_op | source)
XLA Modules:
  0.0 60.7 jit_solution(11840653090032683813)
XLA Ops:
  0.0 0.0 copy-start.4
  0.0 1.0 %copy-done.4 = f32[32,4,1024]{2,1,0:T(4,128)S(1)} copy-done((f32[32,4,1024]{2,1,0:T(4,128)S(1)}, f32[32,4,1024]{2,1,0:T(4,128)}, u32[]{:S(2)}) %copy-start.4) | copy-done | bytes 524312
  1.0 0.2 shard_map.57.refs_0_.refs_1_.refs_3_
  1.2 0.0 copy-start.2
  1.3 2.2 %collective-permute-start.4 = (f32[32,1024]{1,0:T(8,128)S(1)}, f32[32,1024]{1,0:T(8,128)S(1)}, u32[]{:S(2)}, u32[]{:S(2)}) collective-permute-start(f32[32,1024]{1,0:T(8,128)S(1)} %shard_map.57.refs_0_.refs_1_.refs_3_), channel_id=1, source_target_pairs={{0,16},{16,0},{32,48},{48,32},{64,80},{80,64},{96,112},{112,96},{1... | collective-permute-start | bytes 393224 | tf_op jit(solution)/shard_map/ppermute | solution.py:228
  3.5 0.4 shard_map.56
  3.9 0.0 copy-start.1
  3.9 0.0 copy-start.3
  3.9 0.1 collective-permute-start.2
  4.0 0.0 copy-done.2
  4.0 0.9 %shard_map.55.w_ref = bf16[3,288,384]{2,1,0:T(8,128)(2,1)S(1)} custom-call(f32[3,32,864]{2,1,0:T(8,128)S(1)} %bitcast.9), custom_call_target="tpu_custom_call" | custom-call | bytes 663552 | tf_op jit(solution)/shard_map/pallas_call | solution.py:229
  4.9 0.9 %shard_map.58 = (f32[32,1024]{1,0:T(8,128)S(1)}, f32[32,1024]{1,0:T(8,128)S(1)}) custom-call(bf16[3,288,384]{2,1,0:T(8,128)(2,1)S(1)} %shard_map.55.w_ref, f32[32,1024]{1,0:T(8,128)S(1)} %shard_map.57.refs_0_.refs_1_.refs_3_, f32[32,1024]{1,0:T(8,128)S(1)} %get-tuple-element.23.refs_1_.refs_2_.refs_4_, f32[32,1024]{1,0:T(8,128)S(1)} %get-tuple-element.27.refs_2_.refs_0_, ...), custom_call_target="tpu_custom_call" | custom-call | flops 452984832 | bytes 786432 | tf_op jit(solution)/shard_map/pallas_call | solution.py:244
  5.9 0.0 copy-done.1
  5.9 0.0 copy-done.3
  5.9 0.0 copy-start
  5.9 0.3 shard_map.59.a_ref
  6.2 1.5 %collective-permute-start = (f32[32,1024]{1,0:T(8,128)S(1)}, f32[32,1024]{1,0:T(8,128)S(1)}, u32[]{:S(2)}, u32[]{:S(2)}) collective-permute-start(f32[32,1024]{1,0:T(8,128)S(1)} %get-tuple-element.27.refs_2_.refs_0_), channel_id=1, source_target_pairs={{0,16},{16,0},{32,48},{48,32},{64,80},{80,64},{96,112},{112,96},{1... | collective-permute-start | bytes 393224 | tf_op jit(solution)/shard_map/ppermute | solution.py:264
  7.8 0.0 collective-permute-done.4
  7.8 1.2 %collective-permute-start.5 = (f32[32,1024]{1,0:T(8,128)S(1)}, f32[32,1024]{1,0:T(8,128)S(1)}, u32[]{:S(2)}, u32[]{:S(2)}) collective-permute-start(f32[32,1024]{1,0:T(8,128)S(1)} %collective-permute-done.4), channel_id=1, source_target_pairs={{0,32},{16,112},{32,64},{48,16},{64,96},{80,48},{96,0},{112,80},{1... | collective-permute-start | bytes 393224 | tf_op jit(solution)/shard_map/ppermute | solution.py:266
  9.0 0.0 copy-done
  9.0 0.4 shard_map.60.b_ref
  9.4 1.5 %collective-permute-start.6 = (f32[32,1024]{1,0:T(8,128)S(1)}, f32[32,1024]{1,0:T(8,128)S(1)}, u32[]{:S(2)}, u32[]{:S(2)}) collective-permute-start(f32[32,1024]{1,0:T(8,128)S(1)} %get-tuple-element.34.refs_3_.refs_1_), channel_id=1, source_target_pairs={{0,16},{16,0},{32,48},{48,32},{64,80},{80,64},{96,112},{112,96},{1... | collective-permute-start | bytes 393224 | tf_op jit(solution)/shard_map/ppermute | solution.py:264
  10.9 0.0 collective-permute-done.2.refs_4_
  10.9 0.0 collective-permute-start.3
  10.9 1.4 %collective-permute-done.refs_3_ = f32[32,1024]{1,0:T(8,128)S(1)} collective-permute-done((f32[32,1024]{1,0:T(8,128)S(1)}, f32[32,1024]{1,0:T(8,128)S(1)}, u32[]{:S(2)}, u32[]{:S(2)}) %collective-permute-start) | collective-permute-done | bytes 131104 | tf_op jit(solution)/shard_map/ppermute | solution.py:264
  12.3 1.2 %collective-permute-start.1 = (f32[32,1024]{1,0:T(8,128)S(1)}, f32[32,1024]{1,0:T(8,128)S(1)}, u32[]{:S(2)}, u32[]{:S(2)}) collective-permute-start(f32[32,1024]{1,0:T(8,128)S(1)} %collective-permute-done.refs_3_), channel_id=1, source_target_pairs={{0,32},{16,112},{32,64},{48,16},{64,96},{80,48},{96,0},{112,80},{1... | collective-permute-start | bytes 393224 | tf_op jit(solution)/shard_map/ppermute | solution.py:266
  13.4 0.0 collective-permute-done.5.refs_0_.refs_2_
  13.5 1.2 %shard_map.61 = (f32[32,1024]{1,0:T(8,128)S(1)}, f32[32,1024]{1,0:T(8,128)S(1)}) custom-call(bf16[3,288,384]{2,1,0:T(8,128)(2,1)S(1)} %shard_map.55.w_ref, f32[32,1024]{1,0:T(8,128)S(1)} %collective-permute-done.5.refs_0_.refs_2_, f32[32,1024]{1,0:T(8,128)S(1)} %shard_map.57.refs_0_.refs_1_.refs_3_, ...), custom_call_target="tpu_custom_call" | custom-call | flops 452984832 | bytes 917504 | tf_op jit(solution)/shard_map/pallas_call | solution.py:244
  14.7 0.0 collective-permute-done.6.refs_2_
  14.7 2.8 %shard_map.62 = (f32[32,1024]{1,0:T(8,128)S(1)}, f32[16,32,256]{2,1,0:T(8,128)S(1)}) custom-call(bf16[3,288,384]{2,1,0:T(8,128)(2,1)S(1)} %shard_map.55.w_ref, f32[32,1024]{1,0:T(8,128)S(1)} %get-tuple-element.27.refs_2_.refs_0_, f32[32,1024]{1,0:T(8,128)S(1)} %get-tuple-element.34.refs_3_.refs_1_, f32[32,1024]{1,0:T(8,128)S(1)} %collective-permute-done.6.refs_2_, ...), custom_call_target="tpu_custom_call" | custom-call | flops 1811939328 | bytes 1310720 | tf_op jit(solution)/shard_map/pallas_call | solution.py:244
  17.5 0.1 collective-permute-done.1.refs_0_
  17.6 0.0 collective-permute-done.3.refs_1_
  17.6 2.2 %shard_map.63 = f32[16,32,256]{2,1,0:T(8,128)S(1)} custom-call(bf16[3,288,384]{2,1,0:T(8,128)(2,1)S(1)} %shard_map.55.w_ref, f32[32,1024]{1,0:T(8,128)S(1)} %collective-permute-done.1.refs_0_, f32[32,1024]{1,0:T(8,128)S(1)} %collective-permute-done.3.refs_1_, f32[32,1024]{1,0:T(8,128)S(1)} %collective-permute-done.5.refs_0_.refs_2_, ...), custom_call_target="tpu_custom_call", output_to_operand_aliasing={{}: (10, {})} | custom-call | flops 1358954496 | bytes 1310720 | tf_op jit(solution)/shard_map/pallas_call | solution.py:244
  19.8 22.8 %all_to_all.10 = f32[16,32,256]{2,1,0:T(8,128)S(1)} all-to-all(f32[16,32,256]{2,1,0:T(8,128)S(1)} %shard_map.63), channel_id=1, replica_groups=mesh['depth'=8,'chan'=16] {'chan'}, dimensions={0} | all-to-all | bytes 1048576 | tf_op jit(solution)/shard_map/all_to_all | solution.py:280
  42.5 2.0 %shard_map.64 = f32[512,256]{1,0:T(8,128)S(1)} custom-call(f32[512,256]{1,0:T(8,128)S(1)} %bitcast.7, bf16[2048,512]{1,0:T(8,128)(2,1)S(1)} %shard_map.59.a_ref, bf16[1024,1024]{1,0:T(8,128)(2,1)S(1)} %shard_map.60.b_ref), custom_call_target="tpu_custom_call" | custom-call | flops 1610612736 | bytes 4194304 | tf_op jit(solution)/shard_map/pallas_call | solution.py:281
  44.6 15.0 %all_to_all.11.in_ref = f32[16,32,256]{2,1,0:T(8,128)S(1)} all-to-all(f32[16,32,256]{2,1,0:T(8,128)S(1)} %bitcast.8), channel_id=1, replica_groups=mesh['depth'=8,'chan'=16] {'chan'}, dimensions={0} | all-to-all | bytes 1048576 | tf_op jit(solution)/shard_map/all_to_all | solution.py:289
  59.5 1.2 %shard_map.65 = f32[32,4,1024]{2,1,0:T(4,128)} custom-call(f32[16,32,256]{2,1,0:T(8,128)S(1)} %all_to_all.11.in_ref), custom_call_target="tpu_custom_call" | custom-call | bytes 1048576 | tf_op jit(solution)/shard_map/pallas_call | solution.py:290
Async XLA Ops:
  0.0 1.0 %copy-start.4 = (f32[32,4,1024]{2,1,0:T(4,128)S(1)}, f32[32,4,1024]{2,1,0:T(4,128)}, u32[]{:S(2)}) copy-start(f32[32,4,1024]{2,1,0:T(4,128)} %x_ref.3) | copy-start | bytes 1572868
  1.2 2.7 %copy-start.2 = (f32[1,3,1,32,864]{4,3,2,1,0:T(8,128)S(1)}, f32[1,3,1,32,864]{4,3,2,1,0:T(8,128)}, u32[]{:S(2)}) copy-start(f32[1,3,1,32,864]{4,3,2,1,0:T(8,128)} %param.6) | copy-start | bytes 995332
  1.3 6.5 %collective-permute-start.4 = (f32[32,1024]{1,0:T(8,128)S(1)}, f32[32,1024]{1,0:T(8,128)S(1)}, u32[]{:S(2)}, u32[]{:S(2)}) collective-permute-start(f32[32,1024]{1,0:T(8,128)S(1)} %shard_map.57.refs_0_.refs_1_.refs_3_), channel_id=1, source_target_pairs={{0,16},{16,0},{32,48},{48,32},{64,80},{80,64},{96,112},{112,96},{1... | collective-permute-start | bytes 393224 | tf_op jit(solution)/shard_map/ppermute | solution.py:228
  3.9 2.0 %copy-start.1 = (f32[1,1024,512]{2,1,0:T(8,128)S(1)}, f32[1,1024,512]{2,1,0:T(8,128)}, u32[]{:S(2)}) copy-start(f32[1,1024,512]{2,1,0:T(8,128)} %param.8) | copy-start | bytes 6291460
  3.9 2.0 %copy-start.3 = (f32[1,512]{1,0:T(1,128)S(1)}, f32[1,512]{1,0:T(1,128)}, u32[]{:S(2)}) copy-start(f32[1,512]{1,0:T(1,128)} %gain_ref.1) | copy-start | bytes 6148
  3.9 7.0 %collective-permute-start.2 = (f32[32,1024]{1,0:T(8,128)S(1)}, f32[32,1024]{1,0:T(8,128)S(1)}, u32[]{:S(2)}, u32[]{:S(2)}) collective-permute-start(f32[32,1024]{1,0:T(8,128)S(1)} %get-tuple-element.23.refs_1_.refs_2_.refs_4_), channel_id=1, source_target_pairs={{0,16},{16,0},{32,48},{48,32},{64,80},{80,64},{96,112},{112,96},{1... | collective-permute-start | bytes 393224 | tf_op jit(solution)/shard_map/ppermute | solution.py:228
  5.9 3.1 %copy-start = (f32[1,512,1024]{2,1,0:T(8,128)S(1)}, f32[1,512,1024]{2,1,0:T(8,128)}, u32[]{:S(2)}) copy-start(f32[1,512,1024]{2,1,0:T(8,128)} %param.9) | copy-start | bytes 6291460
  6.2 6.0 %collective-permute-start = (f32[32,1024]{1,0:T(8,128)S(1)}, f32[32,1024]{1,0:T(8,128)S(1)}, u32[]{:S(2)}, u32[]{:S(2)}) collective-permute-start(f32[32,1024]{1,0:T(8,128)S(1)} %get-tuple-element.27.refs_2_.refs_0_), channel_id=1, source_target_pairs={{0,16},{16,0},{32,48},{48,32},{64,80},{80,64},{96,112},{112,96},{1... | collective-permute-start | bytes 393224 | tf_op jit(solution)/shard_map/ppermute | solution.py:264
  7.8 5.7 %collective-permute-start.5 = (f32[32,1024]{1,0:T(8,128)S(1)}, f32[32,1024]{1,0:T(8,128)S(1)}, u32[]{:S(2)}, u32[]{:S(2)}) collective-permute-start(f32[32,1024]{1,0:T(8,128)S(1)} %collective-permute-done.4), channel_id=1, source_target_pairs={{0,32},{16,112},{32,64},{48,16},{64,96},{80,48},{96,0},{112,80},{1... | collective-permute-start | bytes 393224 | tf_op jit(solution)/shard_map/ppermute | solution.py:266
  9.4 5.3 %collective-permute-start.6 = (f32[32,1024]{1,0:T(8,128)S(1)}, f32[32,1024]{1,0:T(8,128)S(1)}, u32[]{:S(2)}, u32[]{:S(2)}) collective-permute-start(f32[32,1024]{1,0:T(8,128)S(1)} %get-tuple-element.34.refs_3_.refs_1_), channel_id=1, source_target_pairs={{0,16},{16,0},{32,48},{48,32},{64,80},{80,64},{96,112},{112,96},{1... | collective-permute-start | bytes 393224 | tf_op jit(solution)/shard_map/ppermute | solution.py:264
  10.9 6.7 %collective-permute-start.3 = (f32[32,1024]{1,0:T(8,128)S(1)}, f32[32,1024]{1,0:T(8,128)S(1)}, u32[]{:S(2)}, u32[]{:S(2)}) collective-permute-start(f32[32,1024]{1,0:T(8,128)S(1)} %collective-permute-done.2.refs_4_), channel_id=1, source_target_pairs={{0,32},{16,112},{32,64},{48,16},{64,96},{80,48},{96,0},{112,80},{1... | collective-permute-start | bytes 393224 | tf_op jit(solution)/shard_map/ppermute | solution.py:266
  12.3 5.3 %collective-permute-start.1 = (f32[32,1024]{1,0:T(8,128)S(1)}, f32[32,1024]{1,0:T(8,128)S(1)}, u32[]{:S(2)}, u32[]{:S(2)}) collective-permute-start(f32[32,1024]{1,0:T(8,128)S(1)} %collective-permute-done.refs_3_), channel_id=1, source_target_pairs={{0,32},{16,112},{32,64},{48,16},{64,96},{80,48},{96,0},{112,80},{1... | collective-permute-start | bytes 393224 | tf_op jit(solution)/shard_map/ppermute | solution.py:266
